TPU v7x, 128 devices: a whole 4x4x4 slice. The times are simulated.
128 devices in a mesh: dp: 16 (over x_lo, z, core), shard: 8 (over y, x_hi).
Axes of the slice: x: 4 (x_hi: 2, x_lo: 2; x = x_hi * 2 + x_lo), y: 4, z: 4, core: 2. Of those that a mesh axis runs over, the one named last changes fastest.
Arguments:
- grad_qkv: bfloat16 [16, 768, 2304], P('dp', 'shard'), may hold values from -4 to 4
- grad_out: bfloat16 [16, 768, 768], P('dp', 'shard'), may hold values from -4 to 4
- grad_up: bfloat16 [16, 768, 3072], P('dp', 'shard'), may hold values from -4 to 4
- grad_down: bfloat16 [16, 3072, 768], P('dp', 'shard'), may hold values from -4 to 4
- grad_bias: bfloat16 [16, 9984], P('dp'), may hold values from -6 to 6
- grad_embed: bfloat16 [16, 32768, 768], P('dp', 'shard'), may hold values from -6 to 6
- moment_qkv: float32 [768, 2304], P('shard'), may hold values from -6 to 6
- moment_out: float32 [768, 768], P('shard'), may hold values from -6 to 6
- moment_up: float32 [768, 3072], P('shard'), may hold values from -6 to 6
- moment_down: float32 [3072, 768], P('shard'), may hold values from -6 to 6
- embed_param: float32 [8, 4096, 768], P('shard', 'dp'), may hold values from -6 to 6
- embed_first: float32 [8, 4096, 768], P('shard', 'dp'), may hold values from -6 to 6
- embed_second: float32 [8, 4096, 768], P('shard', 'dp'), may hold values from 0.01 to 1
- bias_param: float32 [9984], replicated, may hold values from -6 to 6
- bias_first: float32 [9984], replicated, may hold values from -6 to 6
- bias_second: float32 [9984], replicated, may hold values from 0.01 to 1
Outputs:
- new_moment_qkv: float32 [768, 2304], P('shard')
- update_qkv: bfloat16 [768, 2304], P('shard')
- new_moment_out: float32 [768, 768], P('shard')
- update_out: bfloat16 [768, 768], P('shard')
- new_moment_up: float32 [768, 3072], P('shard')
- update_up: bfloat16 [768, 3072], P('shard')
- new_moment_down: float32 [3072, 768], P('shard')
- update_down: bfloat16 [3072, 768], P('shard')
- new_embed_param: float32 [8, 4096, 768], P('shard', 'dp')
- new_embed_first: float32 [8, 4096, 768], P('shard', 'dp')
- new_embed_second: float32 [8, 4096, 768], P('shard', 'dp')
- new_bias_param: float32 [9984], replicated
- new_bias_first: float32 [9984], replicated
- new_bias_second: float32 [9984], replicated
All inputs are finite; a program needn't handle non-finite values.
Results may differ from a plain program's by a relative error of at most 0.029.
Values may be sent and summed in bfloat16 or wider, within the bound.
A program may use at most 192 MiB of HBM per device.

v0:
```python
import jax
import jax.numpy as jnp
from jax import lax
from jax.sharding import PartitionSpec as P

ITERS = 3
STEP = 10


coef_a = 3.4445
coef_b = -4.775
coef_c = 2.0315
keep_rate = 0.95
beta_one = 0.9
beta_two = 0.999
learn_rate = 0.001
decay_rate = 0.01
adam_eps = 1e-08


def newton_schulz(current, factor):
    wide = current.astype(jnp.float32)
    norm_value = jnp.sqrt(jnp.sum(wide * wide))
    current = (wide / (norm_value + 1e-07)).astype(jnp.bfloat16)
    result = current
    for turn in range(ITERS):
        gram = jnp.dot(current, current.T, preferred_element_type=jnp.float32).astype(jnp.bfloat16)
        square = jnp.dot(gram, gram, preferred_element_type=jnp.float32)
        poly = (coef_b * gram.astype(jnp.float32) + coef_c * square).astype(jnp.bfloat16)
        following = coef_a * current.astype(jnp.float32) + jnp.dot(
            poly, current, preferred_element_type=jnp.float32
        )
        if turn + 1 < ITERS:
            current = following.astype(jnp.bfloat16)
        else:
            result = (factor * following).astype(jnp.bfloat16)
    return result


def adamw(total, param, first, second):
    first_new = beta_one * first + (1.0 - beta_one) * total
    second_new = beta_two * second + (1.0 - beta_two) * total * total
    first_hat = first_new / (1.0 - beta_one**STEP)
    second_hat = second_new / (1.0 - beta_two**STEP)
    param_new = param - learn_rate * (
        first_hat / (jnp.sqrt(second_hat) + adam_eps) + decay_rate * param
    )
    return (param_new, first_new, second_new)


def local(
    grad_qkv,
    grad_out,
    grad_up,
    grad_down,
    grad_bias,
    grad_embed,
    moment_qkv,
    moment_out,
    moment_up,
    moment_down,
    embed_param,
    embed_first,
    embed_second,
    bias_param,
    bias_first,
    bias_second,
):
    groups = lax.axis_size("shard")
    replicas = lax.axis_size("dp")
    myself = lax.axis_index("shard")
    lanes = 128
    grads = (grad_qkv[0], grad_out[0], grad_up[0], grad_down[0], grad_bias[0])
    sizes = [g.size for g in grads]
    flat = jnp.concatenate([g.reshape(-1) for g in grads])
    block = replicas * 16 * lanes
    padded = -(-flat.shape[0] // block) * block
    flat = jnp.pad(flat, (0, padded - flat.shape[0])).reshape(padded // lanes, lanes)
    reduced = lax.psum_scatter(flat, "dp", scatter_dimension=0, tiled=True)
    gathered = lax.all_gather(reduced, "dp", axis=0, tiled=True).reshape(-1)
    sums = []
    offset = 0
    for g, n in zip(grads, sizes):
        sums.append(gathered[offset : offset + n].reshape(g.shape))
        offset += n
    moments_old = (moment_qkv, moment_out, moment_up, moment_down)
    new_moments = []
    nesterov = []
    for which in range(4):
        total = sums[which].astype(jnp.float32)
        fresh = keep_rate * moments_old[which] + total
        new_moments.append(fresh)
        nesterov.append((total + keep_rate * fresh).astype(jnp.bfloat16))

    shapes = [(p.shape[0] * groups, p.shape[1]) for p in nesterov]
    wide_rows = max(min(s) for s in shapes)
    wide_cols = max(max(s) for s in shapes)
    slot = max(p.size for p in nesterov) // lanes
    owners = [which * groups // 4 for which in range(4)]
    owned = jnp.int32(4)
    for which in range(4):
        owned = jnp.where(myself == owners[which], which, owned)

    pieces = [jnp.zeros((slot, lanes), jnp.bfloat16)] * groups
    for which in range(4):
        part = nesterov[which].reshape(-1, lanes)
        pieces[owners[which]] = jnp.pad(part, ((0, slot - part.shape[0]), (0, 0)))
    outgoing = jnp.stack(pieces)
    incoming = lax.all_to_all(outgoing, "shard", 0, 0, tiled=True)

    def assemble(which):
        rows, cols = shapes[which]

        def branch(buffer):
            used = (rows // groups) * cols // lanes
            whole = buffer[:, :used, :].reshape(rows, cols)
            if rows > cols:
                whole = whole.T
            r, c = whole.shape
            return jnp.pad(whole, ((0, wide_rows - r), (0, wide_cols - c)))

        return branch

    def nothing(buffer):
        return jnp.zeros((wide_rows, wide_cols), jnp.bfloat16)

    matrix = lax.switch(owned, [assemble(w) for w in range(4)] + [nothing], incoming)
    factors = jnp.array([0.2 * max(s) ** 0.5 for s in shapes] + [0.0], jnp.float32)
    result = newton_schulz(matrix, factors[owned])

    def disassemble(which):
        rows, cols = shapes[which]

        def branch(y):
            if rows > cols:
                part = y[:cols, :rows].T
            else:
                part = y[:rows, :cols]
            part = part.reshape(groups, -1, lanes)
            return jnp.pad(part, ((0, 0), (0, slot - part.shape[1]), (0, 0)))

        return branch

    def nothing_back(y):
        return jnp.zeros((groups, slot, lanes), jnp.bfloat16)

    answered = lax.switch(owned, [disassemble(w) for w in range(4)] + [nothing_back], result)
    returned = lax.all_to_all(answered, "shard", 0, 0, tiled=True)
    updates = [
        returned[owners[which], : nesterov[which].size // lanes, :].reshape(nesterov[which].shape)
        for which in range(4)
    ]

    _, grad_embed = lax.optimization_barrier((gathered, grad_embed))
    embed_total = lax.psum_scatter(grad_embed, "dp", scatter_dimension=1, tiled=True).astype(
        jnp.float32
    )
    embed_new = adamw(embed_total, embed_param, embed_first, embed_second)
    bias_new = adamw(sums[4].astype(jnp.float32), bias_param, bias_first, bias_second)
    return (
        new_moments[0],
        updates[0],
        new_moments[1],
        updates[1],
        new_moments[2],
        updates[2],
        new_moments[3],
        updates[3],
        embed_new[0],
        embed_new[1],
        embed_new[2],
        bias_new[0],
        bias_new[1],
        bias_new[2],
    )


def solution(mesh):
    placed = (
        P("dp", "shard", None),
        P("dp", "shard", None),
        P("dp", "shard", None),
        P("dp", "shard", None),
        P("dp", None),
        P("dp", "shard", None),
        P("shard", None),
        P("shard", None),
        P("shard", None),
        P("shard", None),
        P("shard", "dp", None),
        P("shard", "dp", None),
        P("shard", "dp", None),
        P(),
        P(),
        P(),
    )
    return jax.shard_map(
        local,
        mesh=mesh,
        in_specs=placed,
        out_specs=(
            P("shard", None),
            P("shard", None),
            P("shard", None),
            P("shard", None),
            P("shard", None),
            P("shard", None),
            P("shard", None),
            P("shard", None),
            P("shard", "dp", None),
            P("shard", "dp", None),
            P("shard", "dp", None),
            P(),
            P(),
            P(),
        ),
        check_vma=False,
    )
```

profile of v0, /device:TPU:0, one launch (start us, length us, event | category | flops | bytes accessed | tf_op | source)
XLA Modules:
  0.0 379.1 jit_solution(18322622148335464272)
XLA Ops:
  7.2 0.0 reduce-scatter.3.cloned.1.call-start
  7.2 1.5 reshape_squeeze.24
  8.8 1.1 reshape_squeeze.25
  9.9 1.2 copy.34
  11.1 1.6 reshape_squeeze.27
  12.8 0.1 reduce
  13.0 1.4 pad_bitcast_fusion
  14.4 0.0 all-gather.2.cloned.1.call-start
  14.4 66.3 %reduce-scatter.3.cloned.1.call-done = bf16[448,128]{1,0:T(8,128)(2,1)} async-done(((bf16[7168,128]{1,0:T(8,128)(2,1)}), bf16[448,128]{1,0:T(8,128)(2,1)}) %reduce-scatter.3.cloned.1.call-update) | async-done | bytes 114704 | tf_op jit(solution)/shard_map/reduce_scatter | solution.py:79
  80.7 33.7 %all-gather.2.cloned.1.call-done = bf16[7168,128]{1,0:T(8,128)(2,1)} async-done(((bf16[448,128]{1,0:T(8,128)(2,1)}), bf16[7168,128]{1,0:T(8,128)(2,1)}) %all-gather.2.cloned.1.call-update) | async-done | bytes 1835024 | tf_op jit(solution)/shard_map/all_gather | solution.py:80
  114.5 1.1 slice_convert_fusion.2
  115.6 0.1 reshape.92
  115.7 1.1 add_convert_fusion.7
  116.8 0.5 reshape.90
  117.3 0.9 bitcast_dynamic-update-slice_fusion.1
  118.2 0.9 broadcast_dynamic-update-slice_fusion.2
  119.1 0.9 slice_convert_fusion.3
  120.0 0.1 reshape.93
  120.1 0.8 add_convert_fusion.8
  120.9 0.1 reshape.91
  121.0 0.9 bitcast_dynamic-update-slice_fusion
  121.9 0.9 broadcast_dynamic-update-slice_fusion.1
  122.7 1.4 slice_convert_fusion
  124.1 0.2 reshape.94
  124.3 2.5 add_convert_fusion.6
  126.8 0.3 stack.17
  127.1 0.9 constant_dynamic-update-slice_fusion.2
  127.9 0.9 broadcast_dynamic-update-slice_fusion
  128.9 0.2 reshape.95
  129.1 1.2 add_convert_fusion.5
  130.3 0.5 stack.18
  130.8 0.9 constant_dynamic-update-slice_fusion.1
  131.8 0.9 broadcast_dynamic-update-slice_fusion.3
  132.6 6.4 %all-to-all-start = ((bf16[8,2304,128]{2,1,0:T(8,128)(2,1)}), bf16[8,2304,128]{2,1,0:T(8,128)(2,1)}, u32[]{:S(2)}, u32[]{:S(2)}) async-start(bf16[8,2304,128]{2,1,0:T(8,128)(2,1)} %broadcast_dynamic-update-slice_fusion.3), calls=%async_computation.1 | async-start | bytes 9437184 | tf_op jit(solution)/shard_map/all_to_all | solution.py:109
  139.0 0.0 reduce-scatter.5.cloned.1.call-start
  139.1 0.7 reduce-scatter.5.cloned.1.call-update
  139.8 0.6 dynamic_slice.3
  140.4 74.9 %all-to-all-done = bf16[8,2304,128]{2,1,0:T(8,128)(2,1)} async-done(((bf16[8,2304,128]{2,1,0:T(8,128)(2,1)}), bf16[8,2304,128]{2,1,0:T(8,128)(2,1)}, u32[]{:S(2)}, u32[]{:S(2)}) %all-to-all-start) | async-done | bytes 4718624 | tf_op jit(solution)/shard_map/all_to_all | solution.py:109
  215.3 12.4 %conditional.2 = (bf16[768,3072]{1,0:T(8,128)(2,1)}) conditional(s32[]{:T(128)} %clamp.4, bf16[8,2304,128]{2,1,0:T(8,128)(2,1)} %all-to-all-done, bf16[8,2304,128]{2,1,0:T(8,128)(2,1)} %all-to-all-done, bf16[8,2304,128]{2,1,0:T(8,128)(2,1)} %all-to-all-done, bf16[8,2304,128]{2,1,0:T(8,128)(2,1)} %all-to-all-done, () %tuple.39), branch_computations={%region_1.2_spmd, %region_2.3_spmd, %region_3.4_spmd, %region_4.5_... | conditional | bytes 22413322 | solution.py:127
  215.3 2.3 slice.31
  217.6 5.2 %reshape.78 = bf16[768,2304]{1,0:T(8,128)(2,1)} reshape(bf16[8,1728,128]{2,1,0:T(8,128)(2,1)S(1)} %slice.31) | data formatting | bytes 7077888 | tf_op jit(solution)/shard_map/cond/branch_0_fun/reshape | solution.py:116
  222.8 4.8 %pad.21 = bf16[768,3072]{1,0:T(8,128)(2,1)} pad(bf16[768,2304]{1,0:T(8,128)(2,1)} %reshape.78, bf16[]{:T(256)} %constant.12.clone), padding=0_0x0_768 | pad | bytes 8257538 | tf_op jit(solution)/shard_map/cond/branch_0_fun/jit(_pad)/pad | solution.py:120
  227.7 5.5 %fusion = f32[]{:T(128)} fusion(bf16[768,3072]{1,0:T(8,128)(2,1)} %get-tuple-element.52), kind=kLoop, calls=%fused_computation.2 | loop fusion | flops 7077887 | bytes 4718596 | tf_op jit(solution)/shard_map/reduce_sum | solution.py:23
  233.8 7.7 %convolution_convert_fusion.2 = bf16[768,768]{1,0:T(8,128)(2,1)S(1)} fusion(bf16[768,3072]{1,0:T(8,128)(2,1)} %get-tuple-element.52, f32[]{:T(128)S(6)} %add.102), kind=kOutput, calls=%fused_computation.13 | convolution fusion | flops 3631546368 | bytes 5898244 | tf_op jit(solution)/shard_map/dot_general | solution.py:27
  241.6 10.0 %add_convert_fusion.1 = bf16[768,3072]{1,0:T(8,128)(2,1)} fusion(bf16[768,768]{1,0:T(8,128)(2,1)S(1)} %convolution_convert_fusion.2, f32[]{:T(128)S(6)} %add.102, bf16[768,3072]{1,0:T(8,128)(2,1)} %get-tuple-element.52), kind=kOutput, calls=%fused_computation.6 | convolution fusion | flops 4556390400 | bytes 10616836 | tf_op jit(solution)/shard_map/dot_general | solution.py:30
  251.6 7.6 %convolution_convert_fusion.1 = bf16[768,768]{1,0:T(8,128)(2,1)S(1)} fusion(bf16[768,3072]{1,0:T(8,128)(2,1)} %add_convert_fusion.1), kind=kOutput, calls=%fused_computation.12 | convolution fusion | flops 3624468480 | bytes 5898240 | tf_op jit(solution)/shard_map/dot_general | solution.py:27
  259.2 10.0 %add_convert_fusion = bf16[768,3072]{1,0:T(8,128)(2,1)} fusion(bf16[768,3072]{1,0:T(8,128)(2,1)} %add_convert_fusion.1, bf16[768,768]{1,0:T(8,128)(2,1)S(1)} %convolution_convert_fusion.1), kind=kOutput, calls=%fused_computation.5 | convolution fusion | flops 4542234624 | bytes 10616832 | tf_op jit(solution)/shard_map/dot_general | solution.py:30
  269.2 7.6 %convolution_convert_fusion = bf16[768,768]{1,0:T(8,128)(2,1)S(1)} fusion(bf16[768,3072]{1,0:T(8,128)(2,1)} %add_convert_fusion), kind=kOutput, calls=%fused_computation.11 | convolution fusion | flops 3624468480 | bytes 5898240 | tf_op jit(solution)/shard_map/dot_general | solution.py:27
  276.9 11.0 %multiply_convert_fusion = bf16[768,3072]{1,0:T(8,128)(2,1)} fusion(bf16[768,3072]{1,0:T(8,128)(2,1)} %add_convert_fusion, f32[]{:T(128)} %bitcast.3, bf16[768,768]{1,0:T(8,128)(2,1)S(1)} %convolution_convert_fusion), kind=kOutput, calls=%fused_computation.4 | convolution fusion | flops 4544593920 | bytes 10616836 | tf_op jit(solution)/shard_map/dot_general | solution.py:30
  287.9 12.0 %conditional.3 = (bf16[8,2304,128]{2,1,0:T(8,128)(2,1)}) conditional(s32[]{:T(128)} %clamp.4, bf16[768,3072]{1,0:T(8,128)(2,1)} %multiply_convert_fusion, bf16[768,3072]{1,0:T(8,128)(2,1)} %multiply_convert_fusion, bf16[768,3072]{1,0:T(8,128)(2,1)} %multiply_convert_fusion, ...), branch_computations={%region_7.8_spmd, %region_8.9_spmd, %region_9.10_spmd, %region_10.... | conditional | bytes 25952290 | solution.py:147
  287.9 2.0 slice-done
  289.9 5.3 %reshape.82 = bf16[8,1728,128]{2,1,0:T(8,128)(2,1)} reshape(bf16[768,2304]{1,0:T(8,128)(2,1)S(1)} %slice-done) | data formatting | bytes 7077888 | tf_op jit(solution)/shard_map/cond/branch_0_fun/reshape | solution.py:139
  295.2 4.7 %pad.23 = bf16[8,2304,128]{2,1,0:T(8,128)(2,1)} pad(bf16[8,1728,128]{2,1,0:T(8,128)(2,1)} %reshape.82, bf16[]{:T(256)} %constant.22.clone), padding=0_0x0_576x0_0 | pad | bytes 8257538 | tf_op jit(solution)/shard_map/cond/branch_0_fun/jit(_pad)/pad | solution.py:140
  299.9 9.7 %all-to-all-start.1 = ((bf16[8,2304,128]{2,1,0:T(8,128)(2,1)}), bf16[8,2304,128]{2,1,0:T(8,128)(2,1)}, u32[]{:S(2)}, u32[]{:S(2)}) async-start(bf16[8,2304,128]{2,1,0:T(8,128)(2,1)} %get-tuple-element.53), calls=%async_computation.2 | async-start | bytes 9437184 | tf_op jit(solution)/shard_map/all_to_all | solution.py:148
  309.6 1.4 multiply_subtract_fusion.1
  311.1 2.8 multiply_subtract_fusion
  313.8 51.0 %all-to-all-done.1 = bf16[8,2304,128]{2,1,0:T(8,128)(2,1)} async-done(((bf16[8,2304,128]{2,1,0:T(8,128)(2,1)}), bf16[8,2304,128]{2,1,0:T(8,128)(2,1)}, u32[]{:S(2)}, u32[]{:S(2)}) %all-to-all-start.1) | async-done | bytes 4718624 | tf_op jit(solution)/shard_map/all_to_all | solution.py:148
  364.8 1.0 slice.57
  365.9 1.3 reshape_squeeze.28
  367.1 0.9 slice.58
  368.1 0.8 reshape_squeeze.29
  368.9 1.3 fusion.18
  370.2 1.1 reshape_squeeze.30
  371.3 1.3 reshape_squeeze.31
  (31 shorter events, 0.2 us)
Async XLA Ops:
  7.2 5.6 %copy-start.9 = (bf16[1,9984]{1,0:T(2,128)(2,1)S(1)}, bf16[1,9984]{1,0:T(2,128)(2,1)}, u32[]{:S(2)}) copy-start(bf16[1,9984]{1,0:T(2,128)(2,1)} %param.31) | copy-start | bytes 59908
  7.2 73.5 %reduce-scatter.3.cloned.1.call-start = ((), (), s32[]{:S(2)}) async-start(), calls=%async_computation.4 | async-start | bytes 1949696 | tf_op jit(solution)/shard_map/reduce_scatter | solution.py:79
  12.9 102.8 %copy-start.1 = (f32[96,2304]{1,0:T(8,128)S(1)}, f32[96,2304]{1,0:T(8,128)}, u32[]{:S(2)}) copy-start(f32[96,2304]{1,0:T(8,128)} %param.33) | copy-start | bytes 2654212
  14.4 100.1 %all-gather.2.cloned.1.call-start = ((), (), s32[]{:S(2)}) async-start(), calls=%async_computation.5 | async-start | bytes 1949696 | tf_op jit(solution)/shard_map/all_gather | solution.py:80
  115.7 4.4 %copy-start.5 = (f32[96,768]{1,0:T(8,128)S(1)}, f32[96,768]{1,0:T(8,128)}, u32[]{:S(2)}) copy-start(f32[96,768]{1,0:T(8,128)} %param.34) | copy-start | bytes 884740
  126.8 2.3 copy-start
  132.6 82.7 %all-to-all-start = ((bf16[8,2304,128]{2,1,0:T(8,128)(2,1)}), bf16[8,2304,128]{2,1,0:T(8,128)(2,1)}, u32[]{:S(2)}, u32[]{:S(2)}) async-start(bf16[8,2304,128]{2,1,0:T(8,128)(2,1)} %broadcast_dynamic-update-slice_fusion.3), calls=%async_computation.1 | async-start | bytes 9437184 | tf_op jit(solution)/shard_map/all_to_all | solution.py:109
  139.0 0.8 copy-start.10
  139.0 172.0 %reduce-scatter.5.cloned.1.call-start = ((), (), s32[]{:S(2)}) async-start(), calls=%async_computation.6 | async-start | bytes 6684672 | tf_op jit(solution)/shard_map/reduce_scatter | solution.py:155
  287.9 2.0 slice-start
  299.9 9.7 %copy-start.6 = (f32[9984]{0:T(1024)S(1)}, f32[9984]{0:T(1024)}, u32[]{:S(2)}) copy-start(f32[9984]{0:T(1024)} %param.40) | copy-start | bytes 119812
  299.9 9.7 %copy-start.7 = (f32[9984]{0:T(1024)S(1)}, f32[9984]{0:T(1024)}, u32[]{:S(2)}) copy-start(f32[9984]{0:T(1024)} %param.41) | copy-start | bytes 119812
  299.9 9.7 %copy-start.8 = (f32[9984]{0:T(1024)S(1)}, f32[9984]{0:T(1024)}, u32[]{:S(2)}) copy-start(f32[9984]{0:T(1024)} %param.42) | copy-start | bytes 119812
  299.9 11.1 %copy-start.2 = (f32[1,256,768]{2,1,0:T(8,128)S(1)}, f32[1,256,768]{2,1,0:T(8,128)}, u32[]{:S(2)}) copy-start(f32[1,256,768]{2,1,0:T(8,128)} %param.37) | copy-start | bytes 2359300
  299.9 11.1 %copy-start.3 = (f32[1,256,768]{2,1,0:T(8,128)S(1)}, f32[1,256,768]{2,1,0:T(8,128)}, u32[]{:S(2)}) copy-start(f32[1,256,768]{2,1,0:T(8,128)} %param.38) | copy-start | bytes 2359300
  299.9 11.1 %copy-start.4 = (f32[1,256,768]{2,1,0:T(8,128)S(1)}, f32[1,256,768]{2,1,0:T(8,128)}, u32[]{:S(2)}) copy-start(f32[1,256,768]{2,1,0:T(8,128)} %param.39) | copy-start | bytes 2359300
  299.9 64.9 %all-to-all-start.1 = ((bf16[8,2304,128]{2,1,0:T(8,128)(2,1)}), bf16[8,2304,128]{2,1,0:T(8,128)(2,1)}, u32[]{:S(2)}, u32[]{:S(2)}) async-start(bf16[8,2304,128]{2,1,0:T(8,128)(2,1)} %get-tuple-element.53), calls=%async_computation.2 | async-start | bytes 9437184 | tf_op jit(solution)/shard_map/all_to_all | solution.py:148
Sparse Core Ops, SparseCore 0:
  14.5 66.1 reduce-scatter.2
  82.4 32.0 all-gather.1
  142.3 93.5 reduce-scatter.4
where the time goes:
time: 380 us; the launch traced here: 379 us
  waiting for transfers between devices  227 us (60%)
  matrix products  54 us (14%)
  local copies, waits for them, and re-layouts  48.8 us (13%)
  other arithmetic  18.7 us (5%)
  starting transfers between devices  16.2 us (4%)
  between operations  14.7 us (4%)
    all_to_all x1, waiting for transfers between devices, local(): incoming = lax.all_to_all(outgoing, 'shard', 0, 0, tiled=True)  74.9 us
    reduce_scatter x1, waiting for transfers between devices, local(): reduced = lax.psum_scatter(flat, 'dp', scatter_dimension=0, tiled=True)  66.3 us
    all_to_all x1, waiting for transfers between devices, local(): returned = lax.all_to_all(answered, 'shard', 0, 0, tiled=True)  51 us
    all_gather x1, waiting for transfers between devices, local(): gathered = lax.all_gather(reduced, 'dp', axis=0, tiled=True).reshape(-1)  33.7 us
    dot_general x3, matrix products, newton_schulz(): jnp.dot(poly, current, preferred_element_type=jnp.float32)  31 us
    dot_general x3, matrix products, newton_schulz(): jnp.dot(current, current.T, preferred_element_type=jnp.float32)  23 us
    all_to_all x1, starting transfers between devices, local(): returned = lax.all_to_all(answered, 'shard', 0, 0, tiled=True)  9.68 us
  transfers between devices with their start and end apart: 5, of which 4 were waited for; matrix products, arithmetic and copies ran while one was open for 23% of the time, Pallas kernels for 0%

commit v1 on v0

--- a/solution.py
+++ b/solution.py
@@ -151,7 +151,7 @@
         for which in range(4)
     ]
 
-    _, grad_embed = lax.optimization_barrier((gathered, grad_embed))
+    _, grad_embed = lax.optimization_barrier((incoming, grad_embed))
     embed_total = lax.psum_scatter(grad_embed, "dp", scatter_dimension=1, tiled=True).astype(
         jnp.float32
     )

time: 380 us -> 370 us (0.974)
  waiting for transfers between devices: 227 us -> 211 us
    all_to_all x1, waiting for transfers between devices: 74.9 us -> 56.4 us  [local(): incoming = lax.all_to_all(outgoing, 'shard', 0, 0, tiled=True)]
    unnamed x34 -> x36, local copies, waits for them, and re-layouts: 7.51 us -> 8.36 us
  transfers between devices with their start and end apart: 5 -> 5, of which waited for: 4 -> 4; matrix products, arithmetic and copies ran while one was open for 23% -> 25% of each run, Pallas kernels for 0% -> 0%
where the time goes in v1:
time: 370 us; the launch traced here: 369 us
  waiting for transfers between devices  211 us (57%)
  matrix products  54.3 us (15%)
  local copies, waits for them, and re-layouts  51.6 us (14%)
  other arithmetic  20 us (5%)
  starting transfers between devices  16.9 us (5%)
  between operations  14.7 us (4%)
    reduce_scatter x1, waiting for transfers between devices, local(): reduced = lax.psum_scatter(flat, 'dp', scatter_dimension=0, tiled=True)  66.3 us
    all_to_all x1, waiting for transfers between devices, local(): incoming = lax.all_to_all(outgoing, 'shard', 0, 0, tiled=True)  56.4 us
    all_to_all x1, waiting for transfers between devices, local(): returned = lax.all_to_all(answered, 'shard', 0, 0, tiled=True)  54.7 us
    all_gather x1, waiting for transfers between devices, local(): gathered = lax.all_gather(reduced, 'dp', axis=0, tiled=True).reshape(-1)  33.7 us
    dot_general x3, matrix products, newton_schulz(): jnp.dot(poly, current, preferred_element_type=jnp.float32)  31.1 us
    dot_general x3, matrix products, newton_schulz(): jnp.dot(current, current.T, preferred_element_type=jnp.float32)  23.2 us
    all_to_all x1, starting transfers between devices, local(): returned = lax.all_to_all(answered, 'shard', 0, 0, tiled=True)  10.3 us
    unnamed x36, local copies, waits for them, and re-layouts  8.36 us
  transfers between devices with their start and end apart: 5, of which 4 were waited for; matrix products, arithmetic and copies ran while one was open for 25% of the time, Pallas kernels for 0%

profile of v1, /device:TPU:0, one launch (start us, length us, event | category | flops | bytes accessed | tf_op | source)
XLA Modules:
  0.0 368.8 jit_solution(86345966994657490)
XLA Ops:
  7.2 0.0 reduce-scatter.3.cloned.1.call-start
  7.2 1.7 reshape_squeeze.25
  9.0 1.5 reshape_squeeze.24
  10.5 1.2 copy.34
  11.7 1.6 reshape_squeeze.27
  13.4 0.1 reduce
  13.5 0.9 constant_dynamic-update-slice_fusion.6
  14.5 1.4 pad_bitcast_fusion
  15.9 0.0 all-gather.2.cloned.1.call-start
  16.0 66.3 %reduce-scatter.3.cloned.1.call-done = bf16[448,128]{1,0:T(8,128)(2,1)} async-done(((bf16[7168,128]{1,0:T(8,128)(2,1)}), bf16[448,128]{1,0:T(8,128)(2,1)}) %reduce-scatter.3.cloned.1.call-update) | async-done | bytes 114704 | tf_op jit(solution)/shard_map/reduce_scatter | solution.py:79
  82.3 33.7 %all-gather.2.cloned.1.call-done = bf16[7168,128]{1,0:T(8,128)(2,1)} async-done(((bf16[448,128]{1,0:T(8,128)(2,1)}), bf16[7168,128]{1,0:T(8,128)(2,1)}) %all-gather.2.cloned.1.call-update) | async-done | bytes 1835024 | tf_op jit(solution)/shard_map/all_gather | solution.py:80
  116.0 0.9 slice_convert_fusion.3
  117.0 0.1 reshape.93
  117.0 0.8 add_convert_fusion.8
  117.8 0.8 reshape.91
  118.6 1.1 slice_convert_fusion.2
  119.7 0.1 reshape.92
  119.9 1.1 add_convert_fusion.7
  120.9 1.3 reshape.90
  122.2 1.4 slice_convert_fusion
  123.6 0.2 reshape.95
  123.8 2.5 add_convert_fusion.5
  126.3 0.5 stack.18
  126.9 0.2 reshape.94
  127.1 2.5 add_convert_fusion.6
  129.6 0.3 stack.17
  129.9 0.9 bitcast_dynamic-update-slice_fusion.1
  130.7 0.9 broadcast_dynamic-update-slice_fusion.2
  131.6 0.9 bitcast_dynamic-update-slice_fusion
  132.5 0.9 broadcast_dynamic-update-slice_fusion.1
  133.3 0.8 constant_dynamic-update-slice_fusion.2
  134.2 0.9 broadcast_dynamic-update-slice_fusion
  135.1 0.9 constant_dynamic-update-slice_fusion.1
  136.0 0.9 broadcast_dynamic-update-slice_fusion.3
  136.9 6.5 %all-to-all-start = ((bf16[8,2304,128]{2,1,0:T(8,128)(2,1)}), bf16[8,2304,128]{2,1,0:T(8,128)(2,1)}, u32[]{:S(2)}, u32[]{:S(2)}) async-start(bf16[8,2304,128]{2,1,0:T(8,128)(2,1)} %broadcast_dynamic-update-slice_fusion.3), calls=%async_computation.1 | async-start | bytes 9437184 | tf_op jit(solution)/shard_map/all_to_all | solution.py:109
  143.4 0.0 reduce-scatter.5.cloned.1.call-start
  143.5 0.6 dynamic_slice.3
  144.1 56.4 %all-to-all-done = bf16[8,2304,128]{2,1,0:T(8,128)(2,1)} async-done(((bf16[8,2304,128]{2,1,0:T(8,128)(2,1)}), bf16[8,2304,128]{2,1,0:T(8,128)(2,1)}, u32[]{:S(2)}, u32[]{:S(2)}) %all-to-all-start) | async-done | bytes 4718624 | tf_op jit(solution)/shard_map/all_to_all | solution.py:109
  200.5 12.3 %conditional.2 = (bf16[768,3072]{1,0:T(8,128)(2,1)}) conditional(s32[]{:T(128)} %clamp.4, bf16[8,2304,128]{2,1,0:T(8,128)(2,1)} %all-to-all-done, bf16[8,2304,128]{2,1,0:T(8,128)(2,1)} %all-to-all-done, bf16[8,2304,128]{2,1,0:T(8,128)(2,1)} %all-to-all-done, bf16[8,2304,128]{2,1,0:T(8,128)(2,1)} %all-to-all-done, () %tuple.39), branch_computations={%region_1.2_spmd, %region_2.3_spmd, %region_3.4_spmd, %region_4.5_... | conditional | bytes 22413322 | solution.py:127
  200.5 2.3 slice.31
  202.8 5.2 %reshape.78 = bf16[768,2304]{1,0:T(8,128)(2,1)} reshape(bf16[8,1728,128]{2,1,0:T(8,128)(2,1)S(1)} %slice.31) | data formatting | bytes 7077888 | tf_op jit(solution)/shard_map/cond/branch_0_fun/reshape | solution.py:116
  208.0 4.8 %pad.21 = bf16[768,3072]{1,0:T(8,128)(2,1)} pad(bf16[768,2304]{1,0:T(8,128)(2,1)} %reshape.78, bf16[]{:T(256)} %constant.12.clone), padding=0_0x0_768 | pad | bytes 8257538 | tf_op jit(solution)/shard_map/cond/branch_0_fun/jit(_pad)/pad | solution.py:120
  212.8 5.5 %fusion = f32[]{:T(128)} fusion(bf16[768,3072]{1,0:T(8,128)(2,1)} %get-tuple-element.54), kind=kLoop, calls=%fused_computation.2 | loop fusion | flops 7077887 | bytes 4718596 | tf_op jit(solution)/shard_map/reduce_sum | solution.py:23
  219.0 7.8 %convolution_convert_fusion.2 = bf16[768,768]{1,0:T(8,128)(2,1)S(1)} fusion(bf16[768,3072]{1,0:T(8,128)(2,1)} %get-tuple-element.54, f32[]{:T(128)S(6)} %add.102), kind=kOutput, calls=%fused_computation.13 | convolution fusion | flops 3631546368 | bytes 5898244 | tf_op jit(solution)/shard_map/dot_general | solution.py:27
  226.8 10.0 %add_convert_fusion.1 = bf16[768,3072]{1,0:T(8,128)(2,1)} fusion(bf16[768,768]{1,0:T(8,128)(2,1)S(1)} %convolution_convert_fusion.2, f32[]{:T(128)S(6)} %add.102, bf16[768,3072]{1,0:T(8,128)(2,1)} %get-tuple-element.54), kind=kOutput, calls=%fused_computation.6 | convolution fusion | flops 4556390400 | bytes 10616836 | tf_op jit(solution)/shard_map/dot_general | solution.py:30
  236.8 7.7 %convolution_convert_fusion.1 = bf16[768,768]{1,0:T(8,128)(2,1)S(1)} fusion(bf16[768,3072]{1,0:T(8,128)(2,1)} %add_convert_fusion.1), kind=kOutput, calls=%fused_computation.12 | convolution fusion | flops 3624468480 | bytes 5898240 | tf_op jit(solution)/shard_map/dot_general | solution.py:27
  244.6 10.1 %add_convert_fusion = bf16[768,3072]{1,0:T(8,128)(2,1)} fusion(bf16[768,3072]{1,0:T(8,128)(2,1)} %add_convert_fusion.1, bf16[768,768]{1,0:T(8,128)(2,1)S(1)} %convolution_convert_fusion.1), kind=kOutput, calls=%fused_computation.5 | convolution fusion | flops 4542234624 | bytes 10616832 | tf_op jit(solution)/shard_map/dot_general | solution.py:30
  254.6 7.6 %convolution_convert_fusion = bf16[768,768]{1,0:T(8,128)(2,1)S(1)} fusion(bf16[768,3072]{1,0:T(8,128)(2,1)} %add_convert_fusion), kind=kOutput, calls=%fused_computation.11 | convolution fusion | flops 3624468480 | bytes 5898240 | tf_op jit(solution)/shard_map/dot_general | solution.py:27
  262.3 11.0 %multiply_convert_fusion = bf16[768,3072]{1,0:T(8,128)(2,1)} fusion(bf16[768,3072]{1,0:T(8,128)(2,1)} %add_convert_fusion, f32[]{:T(128)} %bitcast.3, bf16[768,768]{1,0:T(8,128)(2,1)S(1)} %convolution_convert_fusion), kind=kOutput, calls=%fused_computation.4 | convolution fusion | flops 4544593920 | bytes 10616836 | tf_op jit(solution)/shard_map/dot_general | solution.py:30
  273.3 12.0 %conditional.3 = (bf16[8,2304,128]{2,1,0:T(8,128)(2,1)}) conditional(s32[]{:T(128)} %clamp.4, bf16[768,3072]{1,0:T(8,128)(2,1)} %multiply_convert_fusion, bf16[768,3072]{1,0:T(8,128)(2,1)} %multiply_convert_fusion, bf16[768,3072]{1,0:T(8,128)(2,1)} %multiply_convert_fusion, ...), branch_computations={%region_7.8_spmd, %region_8.9_spmd, %region_9.10_spmd, %region_10.... | conditional | bytes 25952290 | solution.py:147
  273.3 2.0 slice-done
  275.3 5.3 %reshape.82 = bf16[8,1728,128]{2,1,0:T(8,128)(2,1)} reshape(bf16[768,2304]{1,0:T(8,128)(2,1)S(1)} %slice-done) | data formatting | bytes 7077888 | tf_op jit(solution)/shard_map/cond/branch_0_fun/reshape | solution.py:139
  280.6 4.7 %pad.23 = bf16[8,2304,128]{2,1,0:T(8,128)(2,1)} pad(bf16[8,1728,128]{2,1,0:T(8,128)(2,1)} %reshape.82, bf16[]{:T(256)} %constant.22.clone), padding=0_0x0_576x0_0 | pad | bytes 8257538 | tf_op jit(solution)/shard_map/cond/branch_0_fun/jit(_pad)/pad | solution.py:140
  285.3 10.3 %all-to-all-start.1 = ((bf16[8,2304,128]{2,1,0:T(8,128)(2,1)}), bf16[8,2304,128]{2,1,0:T(8,128)(2,1)}, u32[]{:S(2)}, u32[]{:S(2)}) async-start(bf16[8,2304,128]{2,1,0:T(8,128)(2,1)} %get-tuple-element.55), calls=%async_computation.2 | async-start | bytes 9437184 | tf_op jit(solution)/shard_map/all_to_all | solution.py:148
  295.6 1.4 multiply_subtract_fusion.1
  297.0 54.7 %all-to-all-done.1 = bf16[8,2304,128]{2,1,0:T(8,128)(2,1)} async-done(((bf16[8,2304,128]{2,1,0:T(8,128)(2,1)}), bf16[8,2304,128]{2,1,0:T(8,128)(2,1)}, u32[]{:S(2)}, u32[]{:S(2)}) %all-to-all-start.1) | async-done | bytes 4718624 | tf_op jit(solution)/shard_map/all_to_all | solution.py:148
  351.7 0.9 slice.58
  352.6 0.8 reshape_squeeze.29
  353.4 1.3 fusion.18
  354.7 1.3 reshape_squeeze.31
  356.1 1.0 slice.57
  357.1 1.3 reshape_squeeze.28
  358.4 1.1 reshape_squeeze.30
  359.5 2.8 multiply_subtract_fusion
  (33 shorter events, 0.2 us)
Async XLA Ops:
  7.2 6.2 %copy-start.10 = (bf16[1,9984]{1,0:T(2,128)(2,1)S(1)}, bf16[1,9984]{1,0:T(2,128)(2,1)}, u32[]{:S(2)}) copy-start(bf16[1,9984]{1,0:T(2,128)(2,1)} %param.31) | copy-start | bytes 59908
  7.2 75.1 %reduce-scatter.3.cloned.1.call-start = ((), (), s32[]{:S(2)}) async-start(), calls=%async_computation.4 | async-start | bytes 1949696 | tf_op jit(solution)/shard_map/reduce_scatter | solution.py:79
  14.5 102.5 %copy-start.6 = (f32[96,768]{1,0:T(8,128)S(1)}, f32[96,768]{1,0:T(8,128)}, u32[]{:S(2)}) copy-start(f32[96,768]{1,0:T(8,128)} %param.34) | copy-start | bytes 884740
  15.9 104.0 %copy-start.1 = (f32[96,2304]{1,0:T(8,128)S(1)}, f32[96,2304]{1,0:T(8,128)}, u32[]{:S(2)}) copy-start(f32[96,2304]{1,0:T(8,128)} %param.33) | copy-start | bytes 2654212
  15.9 100.1 %all-gather.2.cloned.1.call-start = ((), (), s32[]{:S(2)}) async-start(), calls=%async_computation.5 | async-start | bytes 1949696 | tf_op jit(solution)/shard_map/all_gather | solution.py:80
  126.8 3.0 copy-start
  127.0 4.6 %copy-start.5 = (bf16[576,128]{1,0:T(8,128)(2,1)S(1)}, bf16[576,128]{1,0:T(8,128)(2,1)}, u32[]{:S(2)}) copy-start(bf16[576,128]{1,0:T(8,128)(2,1)} %reshape.91) | copy-start | bytes 442372
  136.9 6.6 %copy-start.11 = (f32[5]{0:T(128)S(1)}, f32[5]{0:T(128)}, u32[]{:S(2)}) copy-start(f32[5]{0:T(128)} %constant.29.clone) | copy-start | bytes 64
  136.9 63.6 %all-to-all-start = ((bf16[8,2304,128]{2,1,0:T(8,128)(2,1)}), bf16[8,2304,128]{2,1,0:T(8,128)(2,1)}, u32[]{:S(2)}, u32[]{:S(2)}) async-start(bf16[8,2304,128]{2,1,0:T(8,128)(2,1)} %broadcast_dynamic-update-slice_fusion.3), calls=%async_computation.1 | async-start | bytes 9437184 | tf_op jit(solution)/shard_map/all_to_all | solution.py:109
  143.4 216.1 %reduce-scatter.5.cloned.1.call-start = ((), (), s32[]{:S(2)}) async-start(), calls=%async_computation.6 | async-start | bytes 6684672 | tf_op jit(solution)/shard_map/reduce_scatter | solution.py:155
  273.3 2.0 slice-start
  285.3 10.3 %copy-start.7 = (f32[9984]{0:T(1024)S(1)}, f32[9984]{0:T(1024)}, u32[]{:S(2)}) copy-start(f32[9984]{0:T(1024)} %param.40) | copy-start | bytes 119812
  285.3 10.3 %copy-start.8 = (f32[9984]{0:T(1024)S(1)}, f32[9984]{0:T(1024)}, u32[]{:S(2)}) copy-start(f32[9984]{0:T(1024)} %param.41) | copy-start | bytes 119812
  285.3 10.3 %copy-start.9 = (f32[9984]{0:T(1024)S(1)}, f32[9984]{0:T(1024)}, u32[]{:S(2)}) copy-start(f32[9984]{0:T(1024)} %param.42) | copy-start | bytes 119812
  285.3 66.4 %all-to-all-start.1 = ((bf16[8,2304,128]{2,1,0:T(8,128)(2,1)}), bf16[8,2304,128]{2,1,0:T(8,128)(2,1)}, u32[]{:S(2)}, u32[]{:S(2)}) async-start(bf16[8,2304,128]{2,1,0:T(8,128)(2,1)} %get-tuple-element.55), calls=%async_computation.2 | async-start | bytes 9437184 | tf_op jit(solution)/shard_map/all_to_all | solution.py:148
  297.0 62.4 %copy-start.2 = (f32[1,256,768]{2,1,0:T(8,128)S(1)}, f32[1,256,768]{2,1,0:T(8,128)}, u32[]{:S(2)}) copy-start(f32[1,256,768]{2,1,0:T(8,128)} %param.37) | copy-start | bytes 2359300
  297.0 62.4 %copy-start.3 = (f32[1,256,768]{2,1,0:T(8,128)S(1)}, f32[1,256,768]{2,1,0:T(8,128)}, u32[]{:S(2)}) copy-start(f32[1,256,768]{2,1,0:T(8,128)} %param.38) | copy-start | bytes 2359300
  297.0 62.4 %copy-start.4 = (f32[1,256,768]{2,1,0:T(8,128)S(1)}, f32[1,256,768]{2,1,0:T(8,128)}, u32[]{:S(2)}) copy-start(f32[1,256,768]{2,1,0:T(8,128)} %param.39) | copy-start | bytes 2359300
Sparse Core Ops, SparseCore 0:
  16.0 66.1 reduce-scatter.2
  84.0 32.0 all-gather.1
  200.6 67.5 reduce-scatter.4

commit v2 on v1

--- a/solution.py
+++ b/solution.py
@@ -18,13 +18,15 @@
 adam_eps = 1e-08
 
 
-def newton_schulz(current, factor):
+def newton_schulz(current, factor, exchange):
     wide = current.astype(jnp.float32)
-    norm_value = jnp.sqrt(jnp.sum(wide * wide))
+    squares = jnp.sum(wide * wide)
+    norm_value = jnp.sqrt(squares + exchange(squares))
     current = (wide / (norm_value + 1e-07)).astype(jnp.bfloat16)
     result = current
     for turn in range(ITERS):
-        gram = jnp.dot(current, current.T, preferred_element_type=jnp.float32).astype(jnp.bfloat16)
+        part = jnp.dot(current, current.T, preferred_element_type=jnp.float32)
+        gram = (part + exchange(part)).astype(jnp.bfloat16)
         square = jnp.dot(gram, gram, preferred_element_type=jnp.float32)
         poly = (coef_b * gram.astype(jnp.float32) + coef_c * square).astype(jnp.bfloat16)
         following = coef_a * current.astype(jnp.float32) + jnp.dot(
@@ -92,10 +94,23 @@
         new_moments.append(fresh)
         nesterov.append((total + keep_rate * fresh).astype(jnp.bfloat16))
 
+    core = lax.axis_index("dp") % 2
+    partner = [(d, d ^ 1) for d in range(replicas)]
+
+    def exchange(value):
+        return lax.ppermute(value, "dp", partner)
+
     shapes = [(p.shape[0] * groups, p.shape[1]) for p in nesterov]
+    flipped = [rows > cols for rows, cols in shapes]
     wide_rows = max(min(s) for s in shapes)
-    wide_cols = max(max(s) for s in shapes)
-    slot = max(p.size for p in nesterov) // lanes
+    half_cols = max(max(s) for s in shapes) // 2
+    halves = []
+    for which in range(4):
+        part = nesterov[which]
+        axis = 0 if flipped[which] else 1
+        size = part.shape[axis] // 2
+        halves.append(lax.dynamic_slice_in_dim(part, core * size, size, axis))
+    slot = max(h.size for h in halves) // lanes
     owners = [which * groups // 4 for which in range(4)]
     owned = jnp.int32(4)
     for which in range(4):
@@ -103,39 +118,39 @@
 
     pieces = [jnp.zeros((slot, lanes), jnp.bfloat16)] * groups
     for which in range(4):
-        part = nesterov[which].reshape(-1, lanes)
+        part = halves[which].reshape(-1, lanes)
         pieces[owners[which]] = jnp.pad(part, ((0, slot - part.shape[0]), (0, 0)))
     outgoing = jnp.stack(pieces)
     incoming = lax.all_to_all(outgoing, "shard", 0, 0, tiled=True)
 
     def assemble(which):
-        rows, cols = shapes[which]
+        hr, hc = halves[which].shape
 
         def branch(buffer):
-            used = (rows // groups) * cols // lanes
-            whole = buffer[:, :used, :].reshape(rows, cols)
-            if rows > cols:
+            used = hr * hc // lanes
+            whole = buffer[:, :used, :].reshape(groups * hr, hc)
+            if flipped[which]:
                 whole = whole.T
             r, c = whole.shape
-            return jnp.pad(whole, ((0, wide_rows - r), (0, wide_cols - c)))
+            return jnp.pad(whole, ((0, wide_rows - r), (0, half_cols - c)))
 
         return branch
 
     def nothing(buffer):
-        return jnp.zeros((wide_rows, wide_cols), jnp.bfloat16)
+        return jnp.zeros((wide_rows, half_cols), jnp.bfloat16)
 
     matrix = lax.switch(owned, [assemble(w) for w in range(4)] + [nothing], incoming)
     factors = jnp.array([0.2 * max(s) ** 0.5 for s in shapes] + [0.0], jnp.float32)
-    result = newton_schulz(matrix, factors[owned])
+    result = newton_schulz(matrix, factors[owned], exchange)
 
     def disassemble(which):
-        rows, cols = shapes[which]
+        hr, hc = halves[which].shape
 
         def branch(y):
-            if rows > cols:
-                part = y[:cols, :rows].T
+            if flipped[which]:
+                part = y[:hc, : groups * hr].T
             else:
-                part = y[:rows, :cols]
+                part = y[: groups * hr, :hc]
             part = part.reshape(groups, -1, lanes)
             return jnp.pad(part, ((0, 0), (0, slot - part.shape[1]), (0, 0)))
 
@@ -146,10 +161,18 @@
 
     answered = lax.switch(owned, [disassemble(w) for w in range(4)] + [nothing_back], result)
     returned = lax.all_to_all(answered, "shard", 0, 0, tiled=True)
-    updates = [
-        returned[owners[which], : nesterov[which].size // lanes, :].reshape(nesterov[which].shape)
-        for which in range(4)
-    ]
+    mine = jnp.stack([returned[owners[which]] for which in range(4)])
+    theirs = exchange(mine)
+    first = core == 0
+    updates = []
+    for which in range(4):
+        hr, hc = halves[which].shape
+        used = hr * hc // lanes
+        own = mine[which, :used].reshape(hr, hc)
+        other = theirs[which, :used].reshape(hr, hc)
+        low = jnp.where(first, own, other)
+        high = jnp.where(first, other, own)
+        updates.append(jnp.concatenate([low, high], axis=0 if flipped[which] else 1))
 
     _, grad_embed = lax.optimization_barrier((incoming, grad_embed))
     embed_total = lax.psum_scatter(grad_embed, "dp", scatter_dimension=1, tiled=True).astype(

time: 370 us -> 332 us (0.90)
  waiting for transfers between devices: 211 us -> 147 us
  blocking collectives: 0 us -> 50.3 us
  local copies, waits for them, and re-layouts: 51.6 us -> 39.8 us
  matrix products: 54.3 us -> 44.7 us
  starting transfers between devices: 16.9 us -> 7.49 us
  other arithmetic: 20 us -> 25.3 us
    all_to_all x1 -> x0, waiting for transfers between devices: 54.7 us -> none  [local(): returned = lax.all_to_all(answered, 'shard', 0, 0, tiled=True)]
    all_to_all x0 -> x1, blocking collectives: none -> 50.3 us  [local(): returned = lax.all_to_all(answered, 'shard', 0, 0, tiled=True)]
    all_to_all x1, waiting for transfers between devices: 56.4 us -> 31.6 us  [local(): incoming = lax.all_to_all(outgoing, 'shard', 0, 0, tiled=True)]
    ppermute x0 -> x5, waiting for transfers between devices: none -> 15.4 us  [exchange(): return lax.ppermute(value, 'dp', partner)]
    all_to_all x1 -> x0, starting transfers between devices: 10.3 us -> none  [local(): returned = lax.all_to_all(answered, 'shard', 0, 0, tiled=True)]
    dot_general x3, matrix products: 23.2 us -> 14.6 us  [newton_schulz(): part = jnp.dot(current, current.T, preferred_element_type=jnp.float32)]
    convert_element_type x4, other arithmetic: 6.85 us -> 0.24 us  [local(): nesterov.append((total + keep_rate * fresh).astype(jnp.bfloat16))]
    select_n x0 -> x8, local copies, waits for them, and re-layouts: none -> 5.73 us  [the longest x4 3.22 us: local(): low = jnp.where(first, own, other)]
  transfers between devices with their start and end apart: 5 -> 9, of which waited for: 4 -> 8; matrix products, arithmetic and copies ran while one was open for 25% -> 14% of each run, Pallas kernels for 0% -> 0%
where the time goes in v2:
time: 332 us; the launch traced here: 330 us
  waiting for transfers between devices  147 us (44%)
  blocking collectives  50.3 us (15%)
  matrix products  44.7 us (13%)
  local copies, waits for them, and re-layouts  39.8 us (12%)
  other arithmetic  25.3 us (8%)
  between operations  15.5 us (5%)
  starting transfers between devices  7.49 us (2%)
    reduce_scatter x1, waiting for transfers between devices, local(): reduced = lax.psum_scatter(flat, 'dp', scatter_dimension=0, tiled=True)  66.3 us
    all_to_all x1, blocking collectives, local(): returned = lax.all_to_all(answered, 'shard', 0, 0, tiled=True)  50.3 us
    all_gather x1, waiting for transfers between devices, local(): gathered = lax.all_gather(reduced, 'dp', axis=0, tiled=True).reshape(-1)  33.7 us
    all_to_all x1, waiting for transfers between devices, local(): incoming = lax.all_to_all(outgoing, 'shard', 0, 0, tiled=True)  31.6 us
    dot_general x3, matrix products, newton_schulz(): jnp.dot(poly, current, preferred_element_type=jnp.float32)  30.1 us
    ppermute x5, waiting for transfers between devices, exchange(): return lax.ppermute(value, 'dp', partner)  15.4 us
    dot_general x3, matrix products, newton_schulz(): part = jnp.dot(current, current.T, preferred_element_type=jnp.float32)  14.6 us
    unnamed x42, local copies, waits for them, and re-layouts  11.5 us
  transfers between devices with their start and end apart: 9, of which 8 were waited for; matrix products, arithmetic and copies ran while one was open for 14% of the time, Pallas kernels for 0%

profile of v2, /device:TPU:0, one launch (start us, length us, event | category | flops | bytes accessed | tf_op | source)
XLA Modules:
  0.0 330.2 jit_solution(798006505795598476)
XLA Ops:
  7.2 1.8 reshape_squeeze.9
  9.0 1.5 reshape_squeeze.8
  10.6 1.2 copy.34
  12.4 0.9 constant_dynamic-update-slice_fusion.6
  13.5 1.4 pad_bitcast_fusion
  14.9 66.3 %reduce-scatter.3.cloned.1.call-done = bf16[448,128]{1,0:T(8,128)(2,1)} async-done(((bf16[7168,128]{1,0:T(8,128)(2,1)}), bf16[448,128]{1,0:T(8,128)(2,1)}) %reduce-scatter.3.cloned.1.call-update) | async-done | bytes 114704 | tf_op jit(solution)/shard_map/reduce_scatter | solution.py:81
  81.3 33.7 %all-gather.2.cloned.1.call-done = bf16[7168,128]{1,0:T(8,128)(2,1)} async-done(((bf16[448,128]{1,0:T(8,128)(2,1)}), bf16[7168,128]{1,0:T(8,128)(2,1)}) %all-gather.2.cloned.1.call-update) | async-done | bytes 1835024 | tf_op jit(solution)/shard_map/all_gather | solution.py:82
  115.0 0.9 slice_convert_fusion.3
  116.1 0.7 copy-done.7
  116.8 0.7 reshape.107
  117.5 1.1 slice_convert_fusion.2
  118.7 2.4 slice_convert_fusion
  121.1 1.5 reshape.112
  122.6 1.3 multiply_add_fusion.2
  123.9 0.9 copy-done.2
  124.8 0.9 reshape.106
  125.8 1.4 multiply_add_fusion
  127.2 1.0 copy-done
  128.8 1.4 multiply_add_fusion.1
  130.7 0.7 bitcast_dynamic-update-slice_fusion.1
  131.5 0.7 broadcast_dynamic-update-slice_fusion.2
  132.2 0.7 bitcast_dynamic-update-slice_fusion
  132.9 0.7 broadcast_dynamic-update-slice_fusion.1
  133.7 0.7 constant_dynamic-update-slice_fusion.2
  134.4 0.7 broadcast_dynamic-update-slice_fusion
  135.1 0.8 constant_dynamic-update-slice_fusion.1
  135.9 0.7 broadcast_dynamic-update-slice_fusion.3
  136.6 6.4 %all-to-all-start = ((bf16[8,1152,128]{2,1,0:T(8,128)(2,1)}), bf16[8,1152,128]{2,1,0:T(8,128)(2,1)S(1)}, u32[]{:S(2)}, u32[]{:S(2)}) async-start(bf16[8,1152,128]{2,1,0:T(8,128)(2,1)} %broadcast_dynamic-update-slice_fusion.3), calls=%async_computation.1 | async-start | bytes 4718592 | tf_op jit(solution)/shard_map/all_to_all | solution.py:124
  143.1 31.6 %all-to-all-done = bf16[8,1152,128]{2,1,0:T(8,128)(2,1)S(1)} async-done(((bf16[8,1152,128]{2,1,0:T(8,128)(2,1)}), bf16[8,1152,128]{2,1,0:T(8,128)(2,1)S(1)}, u32[]{:S(2)}, u32[]{:S(2)}) %all-to-all-start) | async-done | bytes 2359328 | tf_op jit(solution)/shard_map/all_to_all | solution.py:124
  174.7 8.8 %conditional.2 = (f32[768,1536]{1,0:T(8,128)}, f32[]{:T(128)}) conditional(s32[]{:T(128)} %clamp.4, bf16[8,1152,128]{2,1,0:T(8,128)(2,1)S(1)} %all-to-all-done, bf16[8,1152,128]{2,1,0:T(8,128)(2,1)S(1)} %all-to-all-done, bf16[8,1152,128]{2,1,0:T(8,128)(2,1)S(1)} %all-to-all-done, ...), branch_computations={%region_1.3_spmd, %region_3.5_spmd, %region_5.7_spmd, %region_7.9_... | conditional | flops 3538943 | bytes 21233684 | solution.py:142
  174.7 1.4 slice.45
  176.1 3.6 %reshape.96 = bf16[768,1152]{1,0:T(8,128)(2,1)S(1)} reshape(bf16[8,864,128]{2,1,0:T(8,128)(2,1)} %slice.45) | data formatting | bytes 3538944 | tf_op jit(solution)/shard_map/cond/branch_0_fun/reshape | solution.py:131
  179.7 3.8 %multiply_reduce_fusion = (f32[]{:T(128)}, f32[768,1536]{1,0:T(8,128)}) fusion(bf16[768,1152]{1,0:T(8,128)(2,1)S(1)} %reshape.96), kind=kLoop, calls=%fused_computation | loop fusion | flops 3538943 | bytes 6488068 | tf_op jit(solution)/shard_map/reduce_sum | solution.py:23
  183.5 1.4 collective-permute-done
  186.2 5.8 %fusion.14 = f32[768,768]{1,0:T(8,128)S(1)} fusion(f32[768,1536]{1,0:T(8,128)} %get-tuple-element.34, f32[]{:T(128)S(6)} %add.137), kind=kOutput, calls=%fused_computation.81 | convolution fusion | flops 1814298624 | bytes 7077892 | tf_op jit(solution)/shard_map/dot_general | solution.py:28
  192.3 4.5 %collective-permute-done.1 = f32[768,768]{1,0:T(8,128)} collective-permute-done((f32[768,768]{1,0:T(8,128)S(1)}, f32[768,768]{1,0:T(8,128)}, u32[]{:S(2)}, u32[]{:S(2)}) %collective-permute-start.1) | collective-permute-done | bytes 2359328 | tf_op jit(solution)/shard_map/ppermute | solution.py:101
  196.8 10.7 %add_convert_fusion.1 = bf16[768,1536]{1,0:T(8,128)(2,1)} fusion(f32[768,768]{1,0:T(8,128)S(1)} %fusion.14, f32[768,768]{1,0:T(8,128)} %collective-permute-done.1, f32[768,1536]{1,0:T(8,128)} %get-tuple-element.34, f32[]{:T(128)S(6)} %add.137), kind=kOutput, calls=%fused_computation.8 | convolution fusion | flops 2732654592 | bytes 11796484 | tf_op jit(solution)/shard_map/dot_general | solution.py:32
  207.5 4.4 %fusion.20 = f32[768,768]{1,0:T(8,128)S(1)} fusion(bf16[768,1536]{1,0:T(8,128)(2,1)} %add_convert_fusion.1), kind=kOutput, calls=%fused_computation.83 | convolution fusion | flops 1811939328 | bytes 4718592 | tf_op jit(solution)/shard_map/dot_general | solution.py:28
  212.2 4.5 %collective-permute-done.2 = f32[768,768]{1,0:T(8,128)} collective-permute-done((f32[768,768]{1,0:T(8,128)S(1)}, f32[768,768]{1,0:T(8,128)}, u32[]{:S(2)}, u32[]{:S(2)}) %collective-permute-start.2) | collective-permute-done | bytes 2359328 | tf_op jit(solution)/shard_map/ppermute | solution.py:101
  216.6 9.0 %add_convert_fusion = bf16[768,1536]{1,0:T(8,128)(2,1)} fusion(bf16[768,1536]{1,0:T(8,128)(2,1)} %add_convert_fusion.1, f32[768,768]{1,0:T(8,128)S(1)} %fusion.20, f32[768,768]{1,0:T(8,128)} %collective-permute-done.2), kind=kOutput, calls=%fused_computation.7 | convolution fusion | flops 2727936000 | bytes 9437184 | tf_op jit(solution)/shard_map/dot_general | solution.py:32
  225.6 4.4 %fusion.21 = f32[768,768]{1,0:T(8,128)S(1)} fusion(bf16[768,1536]{1,0:T(8,128)(2,1)} %add_convert_fusion), kind=kOutput, calls=%fused_computation.84 | convolution fusion | flops 1811939328 | bytes 4718592 | tf_op jit(solution)/shard_map/dot_general | solution.py:28
  230.4 0.9 dynamic_slice.15
  231.3 3.6 %collective-permute-done.3 = f32[768,768]{1,0:T(8,128)S(1)} collective-permute-done((f32[768,768]{1,0:T(8,128)S(1)}, f32[768,768]{1,0:T(8,128)S(1)}, u32[]{:S(2)}, u32[]{:S(2)}) %collective-permute-start.3) | collective-permute-done | bytes 2359328 | tf_op jit(solution)/shard_map/ppermute | solution.py:101
  235.0 1.4 copy-done.13
  236.4 10.4 %multiply_convert_fusion = bf16[768,1536]{1,0:T(8,128)(2,1)S(1)} fusion(bf16[768,1536]{1,0:T(8,128)(2,1)} %add_convert_fusion, f32[]{:T(128)} %bitcast.3, f32[768,768]{1,0:T(8,128)} %copy-done.12, f32[768,768]{1,0:T(8,128)} %copy-done.13), kind=kOutput, calls=%fused_computation.6 | convolution fusion | flops 2729115648 | bytes 9437188 | tf_op jit(solution)/shard_map/dot_general | solution.py:32
  246.8 6.5 %conditional.3 = (bf16[8,1152,128]{2,1,0:T(8,128)(2,1)}) conditional(s32[]{:T(128)} %clamp.4, bf16[768,1536]{1,0:T(8,128)(2,1)S(1)} %multiply_convert_fusion, bf16[768,1536]{1,0:T(8,128)(2,1)S(1)} %multiply_convert_fusion, bf16[768,1536]{1,0:T(8,128)(2,1)S(1)} %multiply_convert_fusion, ...), branch_computations={%region_10.11_spmd, %region_11.12_spmd, %region_12.13_spmd, %regio... | conditional | bytes 11206666 | solution.py:162
  246.8 1.4 slice.47
  248.2 3.5 %reshape.98 = bf16[8,864,128]{2,1,0:T(8,128)(2,1)S(1)} reshape(bf16[768,1152]{1,0:T(8,128)(2,1)} %slice.47) | data formatting | bytes 3538944 | tf_op jit(solution)/shard_map/cond/branch_0_fun/reshape | solution.py:154
  251.7 1.6 pad.23
  253.3 50.3 %all_to_all.22 = bf16[8,1152,128]{2,1,0:T(8,128)(2,1)S(1)} all-to-all(bf16[8,1152,128]{2,1,0:T(8,128)(2,1)} %get-tuple-element.73), channel_id=1, replica_groups=mesh['dp'=16,'shard'=8] {'shard'}, dimensions={0} | all-to-all | bytes 4718592 | tf_op jit(solution)/shard_map/all_to_all | solution.py:163
  303.9 1.5 multiply_subtract_fusion.1
  305.4 1.5 collective-permute-done.4
  306.9 0.9 broadcast_select_fusion.7
  307.8 0.7 select_n.119
  309.1 1.1 broadcast_select_fusion.1
  310.3 1.0 select_n.128
  311.3 1.8 broadcast_select_fusion.5
  313.0 1.2 select_n.114
  314.2 1.2 select_n.116
  316.5 1.6 pad_maximum_fusion.4
  318.1 0.9 pad_maximum_fusion.2
  318.9 0.8 pad_maximum_fusion.3
  319.7 0.9 pad_maximum_fusion.1
  320.6 3.0 multiply_subtract_fusion
  (60 shorter events, 5.1 us)
Async XLA Ops:
  7.2 4.6 %copy-start.8 = (bf16[1,384,768]{2,1,0:T(8,128)(2,1)S(1)}, bf16[1,384,768]{2,1,0:T(8,128)(2,1)}, u32[]{:S(2)}) copy-start(bf16[1,384,768]{2,1,0:T(8,128)(2,1)} %param.30) | copy-start | bytes 1769476
  7.2 5.1 %copy-start.11 = (bf16[1,9984]{1,0:T(2,128)(2,1)S(1)}, bf16[1,9984]{1,0:T(2,128)(2,1)}, u32[]{:S(2)}) copy-start(bf16[1,9984]{1,0:T(2,128)(2,1)} %param.31) | copy-start | bytes 59908
  7.2 74.0 %reduce-scatter.3.cloned.1.call-start = ((), (), s32[]{:S(2)}) async-start(), calls=%async_computation.4 | async-start | bytes 1949696 | tf_op jit(solution)/shard_map/reduce_scatter | solution.py:81
  14.8 101.1 %copy-start.9 = (f32[96,768]{1,0:T(8,128)S(1)}, f32[96,768]{1,0:T(8,128)}, u32[]{:S(2)}) copy-start(f32[96,768]{1,0:T(8,128)} %param.34) | copy-start | bytes 884740
  14.9 100.1 %all-gather.2.cloned.1.call-start = ((), (), s32[]{:S(2)}) async-start(), calls=%async_computation.5 | async-start | bytes 1949696 | tf_op jit(solution)/shard_map/all_gather | solution.py:82
  116.0 0.7 copy-start.7
  123.9 0.9 copy-start.2
  127.2 1.0 copy-start
  128.8 1.9 copy-start.4
  128.8 3.4 %copy-start.10 = (bf16[288,128]{1,0:T(8,128)(2,1)S(1)}, bf16[288,128]{1,0:T(8,128)(2,1)}, u32[]{:S(2)}) copy-start(bf16[288,128]{1,0:T(8,128)(2,1)} %reshape.107) | copy-start | bytes 221188
  130.3 5.7 %copy-start.1 = (f32[96,3072]{1,0:T(8,128)}, f32[96,3072]{1,0:T(8,128)S(1)}, u32[]{:S(2)}) copy-start(f32[96,3072]{1,0:T(8,128)S(1)} %multiply_add_fusion.1) | copy-start | bytes 3538948
  136.6 38.1 %all-to-all-start = ((bf16[8,1152,128]{2,1,0:T(8,128)(2,1)}), bf16[8,1152,128]{2,1,0:T(8,128)(2,1)S(1)}, u32[]{:S(2)}, u32[]{:S(2)}) async-start(bf16[8,1152,128]{2,1,0:T(8,128)(2,1)} %broadcast_dynamic-update-slice_fusion.3), calls=%async_computation.1 | async-start | bytes 4718592 | tf_op jit(solution)/shard_map/all_to_all | solution.py:124
  143.0 177.6 %reduce-scatter.5.cloned.1.call-start = ((), (), s32[]{:S(2)}) async-start(), calls=%async_computation.6 | async-start | bytes 6684672 | tf_op jit(solution)/shard_map/reduce_scatter | solution.py:178
  183.5 1.4 collective-permute-start
  192.1 4.7 %collective-permute-start.1 = (f32[768,768]{1,0:T(8,128)S(1)}, f32[768,768]{1,0:T(8,128)}, u32[]{:S(2)}, u32[]{:S(2)}) collective-permute-start(f32[768,768]{1,0:T(8,128)S(1)} %fusion.14), channel_id=1, source_target_pairs={{0,8},{8,0},{16,24},{24,16},{32,40},{40,32},{48,56},{56,48},{64,72... | collective-permute-start | bytes 7077896 | tf_op jit(solution)/shard_map/ppermute | solution.py:101
  211.9 4.7 %collective-permute-start.2 = (f32[768,768]{1,0:T(8,128)S(1)}, f32[768,768]{1,0:T(8,128)}, u32[]{:S(2)}, u32[]{:S(2)}) collective-permute-start(f32[768,768]{1,0:T(8,128)S(1)} %fusion.20), channel_id=1, source_target_pairs={{0,8},{8,0},{16,24},{24,16},{32,40},{40,32},{48,56},{56,48},{64,72... | collective-permute-start | bytes 7077896 | tf_op jit(solution)/shard_map/ppermute | solution.py:101
  225.6 4.8 %copy-start.14 = (f32[5]{0:T(128)S(1)}, f32[5]{0:T(128)}, u32[]{:S(2)}) copy-start(f32[5]{0:T(128)} %constant.121.clone) | copy-start | bytes 64
  230.0 4.9 %copy-start.12 = (f32[768,768]{1,0:T(8,128)}, f32[768,768]{1,0:T(8,128)S(1)}, u32[]{:S(2)}) copy-start(f32[768,768]{1,0:T(8,128)S(1)} %fusion.21) | copy-start | bytes 7077892
  230.1 4.9 %collective-permute-start.3 = (f32[768,768]{1,0:T(8,128)S(1)}, f32[768,768]{1,0:T(8,128)S(1)}, u32[]{:S(2)}, u32[]{:S(2)}) collective-permute-start(f32[768,768]{1,0:T(8,128)S(1)} %fusion.21), channel_id=1, source_target_pairs={{0,8},{8,0},{16,24},{24,16},{32,40},{40,32},{48,56},{56,48},{64,72... | collective-permute-start | bytes 7077896 | tf_op jit(solution)/shard_map/ppermute | solution.py:101
  235.0 1.4 copy-start.13
  303.8 3.1 collective-permute-start.4
  311.3 6.8 %copy-start.3 = (bf16[192,768]{1,0:T(8,128)(2,1)S(1)}, bf16[192,768]{1,0:T(8,128)(2,1)}, u32[]{:S(2)}) copy-start(bf16[192,768]{1,0:T(8,128)(2,1)} %select_n.128) | copy-start | bytes 884740
  315.8 4.8 %copy-start.5 = (f32[1,256,768]{2,1,0:T(8,128)S(1)}, f32[1,256,768]{2,1,0:T(8,128)}, u32[]{:S(2)}) copy-start(f32[1,256,768]{2,1,0:T(8,128)} %param.37) | copy-start | bytes 2359300
  315.8 4.8 %copy-start.6 = (f32[1,256,768]{2,1,0:T(8,128)S(1)}, f32[1,256,768]{2,1,0:T(8,128)}, u32[]{:S(2)}) copy-start(f32[1,256,768]{2,1,0:T(8,128)} %param.38) | copy-start | bytes 2359300
Sparse Core Ops, SparseCore 0:
  15.0 66.1 reduce-scatter.2
  82.9 32.0 all-gather.1
  212.3 86.3 reduce-scatter.4

commit v3 on v2

--- a/solution.py
+++ b/solution.py
@@ -78,7 +78,8 @@
     block = replicas * 16 * lanes
     padded = -(-flat.shape[0] // block) * block
     flat = jnp.pad(flat, (0, padded - flat.shape[0])).reshape(padded // lanes, lanes)
-    reduced = lax.psum_scatter(flat, "dp", scatter_dimension=0, tiled=True)
+    parts = lax.all_to_all(flat.reshape(replicas, -1, lanes), "dp", 0, 0, tiled=True)
+    reduced = jnp.sum(parts.astype(jnp.float32), axis=0).astype(jnp.bfloat16)
     gathered = lax.all_gather(reduced, "dp", axis=0, tiled=True).reshape(-1)
     sums = []
     offset = 0

time: 332 us -> 296 us (0.89)
  waiting for transfers between devices: 147 us -> 79.7 us
  blocking collectives: 50.3 us -> 81.6 us
    reduce_scatter x1 -> x0, waiting for transfers between devices: 66.3 us -> none  [local(): reduced = lax.psum_scatter(flat, 'dp', scatter_dimension=0, tiled=True)]
    all_to_all x0 -> x1, blocking collectives: none -> 31.1 us  [local(): lax.all_to_all(flat.reshape(replicas, -1, lanes), 'dp', 0, 0, tiled=True)]
  transfers between devices with their start and end apart: 9 -> 8, of which waited for: 8 -> 7; matrix products, arithmetic and copies ran while one was open for 14% -> 16% of each run, Pallas kernels for 0% -> 0%
where the time goes in v3:
time: 296 us; the launch traced here: 294 us
  blocking collectives  81.6 us (28%)
  waiting for transfers between devices  79.7 us (27%)
  matrix products  44.6 us (15%)
  local copies, waits for them, and re-layouts  38.5 us (13%)
  other arithmetic  26.2 us (9%)
  between operations  15.9 us (5%)
  starting transfers between devices  7.43 us (3%)
    all_to_all x1, blocking collectives, local(): returned = lax.all_to_all(answered, 'shard', 0, 0, tiled=True)  50.4 us
    all_gather x1, waiting for transfers between devices, local(): gathered = lax.all_gather(reduced, 'dp', axis=0, tiled=True).reshape(-1)  32.7 us
    all_to_all x1, waiting for transfers between devices, local(): incoming = lax.all_to_all(outgoing, 'shard', 0, 0, tiled=True)  31.6 us
    all_to_all x1, blocking collectives, local(): lax.all_to_all(flat.reshape(replicas, -1, lanes), 'dp', 0, 0, tiled=True)  31.1 us
    dot_general x3, matrix products, newton_schulz(): jnp.dot(poly, current, preferred_element_type=jnp.float32)  30 us
    ppermute x5, waiting for transfers between devices, exchange(): return lax.ppermute(value, 'dp', partner)  15.4 us
    dot_general x3, matrix products, newton_schulz(): part = jnp.dot(current, current.T, preferred_element_type=jnp.float32)  14.6 us
    unnamed x42, local copies, waits for them, and re-layouts  11.5 us
  transfers between devices with their start and end apart: 8, of which 7 were waited for; matrix products, arithmetic and copies ran while one was open for 16% of the time, Pallas kernels for 0%

profile of v3, /device:TPU:0, one launch (start us, length us, event | category | flops | bytes accessed | tf_op | source)
XLA Modules:
  0.0 293.9 jit_solution(3575817451260243383)
XLA Ops:
  7.2 1.8 reshape_squeeze.9
  9.0 1.5 reshape_squeeze.8
  10.6 1.2 copy.36
  12.4 0.9 constant_dynamic-update-slice_fusion.6
  13.6 31.1 %all_to_all.27 = bf16[16,448,128]{2,1,0:T(8,128)(2,1)S(1)} all-to-all(bf16[16,448,128]{2,1,0:T(8,128)(2,1)S(1)} %bitcast.28), channel_id=1, replica_groups=mesh['dp'=16,'shard'=8] {'dp'}, dimensions={0} | all-to-all | bytes 3670016 | tf_op jit(solution)/shard_map/all_to_all | solution.py:81
  44.7 0.9 reduce_sum.41
  45.7 32.7 %all-gather.2.cloned.1.call-done = bf16[7168,128]{1,0:T(8,128)(2,1)} async-done(((bf16[448,128]{1,0:T(8,128)(2,1)}), bf16[7168,128]{1,0:T(8,128)(2,1)}) %all-gather.2.cloned.1.call-update) | async-done | bytes 1835024 | tf_op jit(solution)/shard_map/all_gather | solution.py:83
  78.4 0.9 slice_convert_fusion.3
  79.5 0.7 copy-done.7
  80.2 0.7 reshape.103
  80.9 1.1 slice_convert_fusion.2
  82.1 2.4 slice_convert_fusion
  84.5 1.5 reshape.108
  86.0 1.3 multiply_add_fusion.2
  87.3 0.9 copy-done.2
  88.3 0.9 reshape.102
  89.2 1.4 multiply_add_fusion
  90.6 1.0 copy-done
  92.2 1.4 multiply_add_fusion.1
  94.1 0.7 bitcast_dynamic-update-slice_fusion.1
  94.9 0.7 broadcast_dynamic-update-slice_fusion.2
  95.6 0.7 bitcast_dynamic-update-slice_fusion
  96.4 0.7 broadcast_dynamic-update-slice_fusion.1
  97.1 0.7 constant_dynamic-update-slice_fusion.2
  97.8 0.8 broadcast_dynamic-update-slice_fusion
  98.6 0.8 constant_dynamic-update-slice_fusion.1
  99.4 0.7 broadcast_dynamic-update-slice_fusion.3
  100.1 6.4 %all-to-all-start.1 = ((bf16[8,1152,128]{2,1,0:T(8,128)(2,1)}), bf16[8,1152,128]{2,1,0:T(8,128)(2,1)S(1)}, u32[]{:S(2)}, u32[]{:S(2)}) async-start(bf16[8,1152,128]{2,1,0:T(8,128)(2,1)} %broadcast_dynamic-update-slice_fusion.3), calls=%async_computation.1 | async-start | bytes 4718592 | tf_op jit(solution)/shard_map/all_to_all | solution.py:125
  106.6 31.6 %all-to-all-done.1 = bf16[8,1152,128]{2,1,0:T(8,128)(2,1)S(1)} async-done(((bf16[8,1152,128]{2,1,0:T(8,128)(2,1)}), bf16[8,1152,128]{2,1,0:T(8,128)(2,1)S(1)}, u32[]{:S(2)}, u32[]{:S(2)}) %all-to-all-start.1) | async-done | bytes 2359328 | tf_op jit(solution)/shard_map/all_to_all | solution.py:125
  138.2 8.8 %conditional.2 = (f32[768,1536]{1,0:T(8,128)}, f32[]{:T(128)}) conditional(s32[]{:T(128)} %clamp.4, bf16[8,1152,128]{2,1,0:T(8,128)(2,1)S(1)} %all-to-all-done.1, bf16[8,1152,128]{2,1,0:T(8,128)(2,1)S(1)} %all-to-all-done.1, bf16[8,1152,128]{2,1,0:T(8,128)(2,1)S(1)} %all-to-all-done.1, ...), branch_computations={%region_1.3_spmd, %region_3.5_spmd, %region_5.7_spmd, %region_7.9_... | conditional | flops 3538943 | bytes 21233684 | solution.py:143
  138.2 1.4 slice.45
  139.6 3.6 %reshape.94 = bf16[768,1152]{1,0:T(8,128)(2,1)S(1)} reshape(bf16[8,864,128]{2,1,0:T(8,128)(2,1)} %slice.45) | data formatting | bytes 3538944 | tf_op jit(solution)/shard_map/cond/branch_0_fun/reshape | solution.py:132
  143.2 3.8 %multiply_reduce_fusion = (f32[]{:T(128)}, f32[768,1536]{1,0:T(8,128)}) fusion(bf16[768,1152]{1,0:T(8,128)(2,1)S(1)} %reshape.94), kind=kLoop, calls=%fused_computation | loop fusion | flops 3538943 | bytes 6488068 | tf_op jit(solution)/shard_map/reduce_sum | solution.py:23
  147.0 1.3 collective-permute-done
  149.6 5.8 %fusion.14 = f32[768,768]{1,0:T(8,128)S(1)} fusion(f32[768,1536]{1,0:T(8,128)} %get-tuple-element.34, f32[]{:T(128)S(6)} %add.135), kind=kOutput, calls=%fused_computation.80 | convolution fusion | flops 1814298624 | bytes 7077892 | tf_op jit(solution)/shard_map/dot_general | solution.py:28
  155.7 4.5 %collective-permute-done.1 = f32[768,768]{1,0:T(8,128)} collective-permute-done((f32[768,768]{1,0:T(8,128)S(1)}, f32[768,768]{1,0:T(8,128)}, u32[]{:S(2)}, u32[]{:S(2)}) %collective-permute-start.1) | collective-permute-done | bytes 2359328 | tf_op jit(solution)/shard_map/ppermute | solution.py:102
  160.2 10.6 %add_convert_fusion.1 = bf16[768,1536]{1,0:T(8,128)(2,1)} fusion(f32[768,768]{1,0:T(8,128)S(1)} %fusion.14, f32[768,768]{1,0:T(8,128)} %collective-permute-done.1, f32[768,1536]{1,0:T(8,128)} %get-tuple-element.34, f32[]{:T(128)S(6)} %add.135), kind=kOutput, calls=%fused_computation.8 | convolution fusion | flops 2732654592 | bytes 11796484 | tf_op jit(solution)/shard_map/dot_general | solution.py:32
  170.8 4.4 %fusion.20 = f32[768,768]{1,0:T(8,128)S(1)} fusion(bf16[768,1536]{1,0:T(8,128)(2,1)} %add_convert_fusion.1), kind=kOutput, calls=%fused_computation.82 | convolution fusion | flops 1811939328 | bytes 4718592 | tf_op jit(solution)/shard_map/dot_general | solution.py:28
  175.5 4.5 %collective-permute-done.2 = f32[768,768]{1,0:T(8,128)} collective-permute-done((f32[768,768]{1,0:T(8,128)S(1)}, f32[768,768]{1,0:T(8,128)}, u32[]{:S(2)}, u32[]{:S(2)}) %collective-permute-start.2) | collective-permute-done | bytes 2359328 | tf_op jit(solution)/shard_map/ppermute | solution.py:102
  180.0 9.0 %add_convert_fusion = bf16[768,1536]{1,0:T(8,128)(2,1)} fusion(bf16[768,1536]{1,0:T(8,128)(2,1)} %add_convert_fusion.1, f32[768,768]{1,0:T(8,128)S(1)} %fusion.20, f32[768,768]{1,0:T(8,128)} %collective-permute-done.2), kind=kOutput, calls=%fused_computation.7 | convolution fusion | flops 2727936000 | bytes 9437184 | tf_op jit(solution)/shard_map/dot_general | solution.py:32
  188.9 4.4 %fusion.21 = f32[768,768]{1,0:T(8,128)S(1)} fusion(bf16[768,1536]{1,0:T(8,128)(2,1)} %add_convert_fusion), kind=kOutput, calls=%fused_computation.83 | convolution fusion | flops 1811939328 | bytes 4718592 | tf_op jit(solution)/shard_map/dot_general | solution.py:28
  193.7 0.9 dynamic_slice.15
  194.6 3.7 %collective-permute-done.3 = f32[768,768]{1,0:T(8,128)S(1)} collective-permute-done((f32[768,768]{1,0:T(8,128)S(1)}, f32[768,768]{1,0:T(8,128)S(1)}, u32[]{:S(2)}, u32[]{:S(2)}) %collective-permute-start.3) | collective-permute-done | bytes 2359328 | tf_op jit(solution)/shard_map/ppermute | solution.py:102
  198.2 1.4 copy-done.13
  199.7 10.4 %multiply_convert_fusion = bf16[768,1536]{1,0:T(8,128)(2,1)S(1)} fusion(bf16[768,1536]{1,0:T(8,128)(2,1)} %add_convert_fusion, f32[]{:T(128)} %bitcast.3, f32[768,768]{1,0:T(8,128)} %copy-done.12, f32[768,768]{1,0:T(8,128)} %copy-done.13), kind=kOutput, calls=%fused_computation.6 | convolution fusion | flops 2729115648 | bytes 9437188 | tf_op jit(solution)/shard_map/dot_general | solution.py:32
  210.1 6.5 %conditional.3 = (bf16[8,1152,128]{2,1,0:T(8,128)(2,1)}) conditional(s32[]{:T(128)} %clamp.4, bf16[768,1536]{1,0:T(8,128)(2,1)S(1)} %multiply_convert_fusion, bf16[768,1536]{1,0:T(8,128)(2,1)S(1)} %multiply_convert_fusion, bf16[768,1536]{1,0:T(8,128)(2,1)S(1)} %multiply_convert_fusion, ...), branch_computations={%region_10.11_spmd, %region_11.12_spmd, %region_12.13_spmd, %regio... | conditional | bytes 11206666 | solution.py:163
  210.1 1.4 slice.47
  211.5 3.5 %reshape.96 = bf16[8,864,128]{2,1,0:T(8,128)(2,1)S(1)} reshape(bf16[768,1152]{1,0:T(8,128)(2,1)} %slice.47) | data formatting | bytes 3538944 | tf_op jit(solution)/shard_map/cond/branch_0_fun/reshape | solution.py:155
  215.0 1.6 pad.23
  216.6 50.4 %all_to_all.28 = bf16[8,1152,128]{2,1,0:T(8,128)(2,1)S(1)} all-to-all(bf16[8,1152,128]{2,1,0:T(8,128)(2,1)} %get-tuple-element.75), channel_id=1, replica_groups=mesh['dp'=16,'shard'=8] {'shard'}, dimensions={0} | all-to-all | bytes 4718592 | tf_op jit(solution)/shard_map/all_to_all | solution.py:164
  267.4 1.5 multiply_subtract_fusion.1
  268.9 1.5 collective-permute-done.4
  270.3 0.9 broadcast_select_fusion.7
  271.2 0.7 select_n.119
  272.6 1.1 broadcast_select_fusion.1
  273.7 1.0 select_n.128
  274.7 1.8 broadcast_select_fusion.5
  276.5 1.2 select_n.114
  277.7 1.2 select_n.116
  279.9 1.6 pad_maximum_fusion.4
  281.5 0.9 pad_maximum_fusion.2
  282.4 0.8 pad_maximum_fusion.3
  283.2 0.9 pad_maximum_fusion.1
  284.0 3.0 %multiply_subtract_fusion = (f32[1,256,768]{2,1,0:T(8,128)}, f32[1,256,768]{2,1,0:T(8,128)}, f32[1,256,768]{2,1,0:T(8,128)}) fusion(f32[1,256,768]{2,1,0:T(8,128)S(1)} %copy-done.5, bf16[1,256,768]{2,1,0:T(8,128)(2,1)} %reduce-scatter.2.cloned.1.call-done, f32[1,256,768]{2,1,0:T(8,128)S(1)} %copy-done.6, f32[1,256,768]{2,1,0:T(8,128)} %param.39), kind=kLoop, calls=%fused_computation.24 | loop fusion | flops 3145728 | bytes 5111808 | tf_op jit(solution)/shard_map/sub | solution.py:47
  (59 shorter events, 5.2 us)
Async XLA Ops:
  7.2 4.6 %copy-start.8 = (bf16[1,384,768]{2,1,0:T(8,128)(2,1)S(1)}, bf16[1,384,768]{2,1,0:T(8,128)(2,1)}, u32[]{:S(2)}) copy-start(bf16[1,384,768]{2,1,0:T(8,128)(2,1)} %param.30) | copy-start | bytes 1769476
  7.2 5.1 %copy-start.11 = (bf16[1,9984]{1,0:T(2,128)(2,1)S(1)}, bf16[1,9984]{1,0:T(2,128)(2,1)}, u32[]{:S(2)}) copy-start(bf16[1,9984]{1,0:T(2,128)(2,1)} %param.31) | copy-start | bytes 59908
  7.2 71.2 %all-gather.2.cloned.1.call-start = ((), (), s32[]{:S(2)}) async-start(), calls=%async_computation.4 | async-start | bytes 1949696 | tf_op jit(solution)/shard_map/all_gather | solution.py:83
  44.7 34.7 %copy-start.9 = (f32[96,768]{1,0:T(8,128)S(1)}, f32[96,768]{1,0:T(8,128)}, u32[]{:S(2)}) copy-start(f32[96,768]{1,0:T(8,128)} %param.34) | copy-start | bytes 884740
  79.5 0.7 copy-start.7
  87.3 0.9 copy-start.2
  90.6 1.0 copy-start
  92.2 1.9 copy-start.4
  92.2 3.4 %copy-start.10 = (bf16[288,128]{1,0:T(8,128)(2,1)S(1)}, bf16[288,128]{1,0:T(8,128)(2,1)}, u32[]{:S(2)}) copy-start(bf16[288,128]{1,0:T(8,128)(2,1)} %reshape.103) | copy-start | bytes 221188
  93.7 5.7 %copy-start.1 = (f32[96,3072]{1,0:T(8,128)}, f32[96,3072]{1,0:T(8,128)S(1)}, u32[]{:S(2)}) copy-start(f32[96,3072]{1,0:T(8,128)S(1)} %multiply_add_fusion.1) | copy-start | bytes 3538948
  100.1 38.1 %all-to-all-start.1 = ((bf16[8,1152,128]{2,1,0:T(8,128)(2,1)}), bf16[8,1152,128]{2,1,0:T(8,128)(2,1)S(1)}, u32[]{:S(2)}, u32[]{:S(2)}) async-start(bf16[8,1152,128]{2,1,0:T(8,128)(2,1)} %broadcast_dynamic-update-slice_fusion.3), calls=%async_computation.1 | async-start | bytes 4718592 | tf_op jit(solution)/shard_map/all_to_all | solution.py:125
  106.5 177.5 %reduce-scatter.2.cloned.1.call-start = ((), (), s32[]{:S(2)}) async-start(), calls=%async_computation.5 | async-start | bytes 6684672 | tf_op jit(solution)/shard_map/reduce_scatter | solution.py:179
  147.0 1.3 collective-permute-start
  155.4 4.7 %collective-permute-start.1 = (f32[768,768]{1,0:T(8,128)S(1)}, f32[768,768]{1,0:T(8,128)}, u32[]{:S(2)}, u32[]{:S(2)}) collective-permute-start(f32[768,768]{1,0:T(8,128)S(1)} %fusion.14), channel_id=1, source_target_pairs={{0,8},{8,0},{16,24},{24,16},{32,40},{40,32},{48,56},{56,48},{64,72... | collective-permute-start | bytes 7077896 | tf_op jit(solution)/shard_map/ppermute | solution.py:102
  175.2 4.7 %collective-permute-start.2 = (f32[768,768]{1,0:T(8,128)S(1)}, f32[768,768]{1,0:T(8,128)}, u32[]{:S(2)}, u32[]{:S(2)}) collective-permute-start(f32[768,768]{1,0:T(8,128)S(1)} %fusion.20), channel_id=1, source_target_pairs={{0,8},{8,0},{16,24},{24,16},{32,40},{40,32},{48,56},{56,48},{64,72... | collective-permute-start | bytes 7077896 | tf_op jit(solution)/shard_map/ppermute | solution.py:102
  188.9 4.8 %copy-start.14 = (f32[5]{0:T(128)S(1)}, f32[5]{0:T(128)}, u32[]{:S(2)}) copy-start(f32[5]{0:T(128)} %constant.122.clone) | copy-start | bytes 64
  193.3 4.9 %copy-start.12 = (f32[768,768]{1,0:T(8,128)}, f32[768,768]{1,0:T(8,128)S(1)}, u32[]{:S(2)}) copy-start(f32[768,768]{1,0:T(8,128)S(1)} %fusion.21) | copy-start | bytes 7077892
  193.3 4.9 %collective-permute-start.3 = (f32[768,768]{1,0:T(8,128)S(1)}, f32[768,768]{1,0:T(8,128)S(1)}, u32[]{:S(2)}, u32[]{:S(2)}) collective-permute-start(f32[768,768]{1,0:T(8,128)S(1)} %fusion.21), channel_id=1, source_target_pairs={{0,8},{8,0},{16,24},{24,16},{32,40},{40,32},{48,56},{56,48},{64,72... | collective-permute-start | bytes 7077896 | tf_op jit(solution)/shard_map/ppermute | solution.py:102
  198.2 1.4 copy-start.13
  267.3 3.1 %collective-permute-start.4 = (bf16[4,1152,128]{2,1,0:T(8,128)(2,1)S(1)}, bf16[4,1152,128]{2,1,0:T(8,128)(2,1)}, u32[]{:S(2)}, u32[]{:S(2)}) collective-permute-start(bf16[4,1152,128]{2,1,0:T(8,128)(2,1)S(1)} %pad_maximum_fusion), channel_id=1, source_target_pairs={{0,8},{8,0},{16,24},{24,16},{32,40},{40,32},{48,56},{56,48},{64,72... | collective-permute-start | bytes 3538952 | tf_op jit(solution)/shard_map/ppermute | solution.py:102
  274.7 6.8 %copy-start.3 = (bf16[192,768]{1,0:T(8,128)(2,1)S(1)}, bf16[192,768]{1,0:T(8,128)(2,1)}, u32[]{:S(2)}) copy-start(bf16[192,768]{1,0:T(8,128)(2,1)} %select_n.128) | copy-start | bytes 884740
  279.2 4.8 %copy-start.5 = (f32[1,256,768]{2,1,0:T(8,128)S(1)}, f32[1,256,768]{2,1,0:T(8,128)}, u32[]{:S(2)}) copy-start(f32[1,256,768]{2,1,0:T(8,128)} %param.37) | copy-start | bytes 2359300
  279.3 4.8 %copy-start.6 = (f32[1,256,768]{2,1,0:T(8,128)S(1)}, f32[1,256,768]{2,1,0:T(8,128)}, u32[]{:S(2)}) copy-start(f32[1,256,768]{2,1,0:T(8,128)} %param.38) | copy-start | bytes 2359300
Sparse Core Ops, SparseCore 0:
  45.8 32.5 all-gather.1
  175.6 86.4 reduce-scatter.1

commit v4 on v3

--- a/solution.py
+++ b/solution.py
@@ -25,8 +25,8 @@
     current = (wide / (norm_value + 1e-07)).astype(jnp.bfloat16)
     result = current
     for turn in range(ITERS):
-        part = jnp.dot(current, current.T, preferred_element_type=jnp.float32)
-        gram = (part + exchange(part)).astype(jnp.bfloat16)
+        part = jnp.dot(current, current.T, preferred_element_type=jnp.bfloat16)
+        gram = (part.astype(jnp.float32) + exchange(part).astype(jnp.float32)).astype(jnp.bfloat16)
         square = jnp.dot(gram, gram, preferred_element_type=jnp.float32)
         poly = (coef_b * gram.astype(jnp.float32) + coef_c * square).astype(jnp.bfloat16)
         following = coef_a * current.astype(jnp.float32) + jnp.dot(

time: 296 us -> 279 us (0.943)
  matrix products: 44.6 us -> 32 us
  waiting for transfers between devices: 79.7 us -> 74.9 us
    dot_general x3, matrix products: 30 us -> 20.9 us  [newton_schulz(): jnp.dot(poly, current, preferred_element_type=jnp.float32)]
    ppermute x5, waiting for transfers between devices: 15.4 us -> 10.5 us  [exchange(): return lax.ppermute(value, 'dp', partner)]
    dot_general x3, matrix products: 14.6 us -> 11.1 us  [newton_schulz(): part = jnp.dot(current, current.T, preferred_element_type=jnp.bfloat16)]
    unnamed x42 -> x40, local copies, waits for them, and re-layouts: 11.5 us -> 10.1 us
  transfers between devices with their start and end apart: 8 -> 8, of which waited for: 7 -> 7; matrix products, arithmetic and copies ran while one was open for 16% -> 21% of each run, Pallas kernels for 0% -> 0%
where the time goes in v4:
time: 279 us; the launch traced here: 277 us
  blocking collectives  79.6 us (29%)
  waiting for transfers between devices  74.9 us (27%)
  local copies, waits for them, and re-layouts  38.6 us (14%)
  matrix products  32 us (11%)
  other arithmetic  28.7 us (10%)
  between operations  15.7 us (6%)
  starting transfers between devices  7.28 us (3%)
    all_to_all x1, blocking collectives, local(): returned = lax.all_to_all(answered, 'shard', 0, 0, tiled=True)  48.5 us
    all_gather x1, waiting for transfers between devices, local(): gathered = lax.all_gather(reduced, 'dp', axis=0, tiled=True).reshape(-1)  32.7 us
    all_to_all x1, waiting for transfers between devices, local(): incoming = lax.all_to_all(outgoing, 'shard', 0, 0, tiled=True)  31.6 us
    all_to_all x1, blocking collectives, local(): lax.all_to_all(flat.reshape(replicas, -1, lanes), 'dp', 0, 0, tiled=True)  31.1 us
    dot_general x3, matrix products, newton_schulz(): jnp.dot(poly, current, preferred_element_type=jnp.float32)  20.9 us
    dot_general x3, matrix products, newton_schulz(): part = jnp.dot(current, current.T, preferred_element_type=jnp.bfloat16)  11.1 us
    ppermute x5, waiting for transfers between devices, exchange(): return lax.ppermute(value, 'dp', partner)  10.5 us
    unnamed x40, local copies, waits for them, and re-layouts  10.1 us
  transfers between devices with their start and end apart: 8, of which 7 were waited for; matrix products, arithmetic and copies ran while one was open for 21% of the time, Pallas kernels for 0%

profile of v4, /device:TPU:0, one launch (start us, length us, event | category | flops | bytes accessed | tf_op | source)
XLA Modules:
  0.0 276.8 jit_solution(14258023288067580738)
XLA Ops:
  7.2 1.5 reshape_squeeze.8
  8.8 1.1 reshape_squeeze.9
  9.9 1.2 copy.36
  11.1 1.6 reshape_squeeze.21
  13.1 31.1 %all_to_all.27 = bf16[16,448,128]{2,1,0:T(8,128)(2,1)S(1)} all-to-all(bf16[16,448,128]{2,1,0:T(8,128)(2,1)S(1)} %bitcast.31), channel_id=1, replica_groups=mesh['dp'=16,'shard'=8] {'dp'}, dimensions={0} | all-to-all | bytes 3670016 | tf_op jit(solution)/shard_map/all_to_all | solution.py:81
  44.2 0.9 reduce_sum.41
  45.2 32.7 %all-gather.2.cloned.1.call-done = bf16[7168,128]{1,0:T(8,128)(2,1)} async-done(((bf16[448,128]{1,0:T(8,128)(2,1)}), bf16[7168,128]{1,0:T(8,128)(2,1)}) %all-gather.2.cloned.1.call-update) | async-done | bytes 1835024 | tf_op jit(solution)/shard_map/all_gather | solution.py:83
  77.9 1.4 slice_convert_fusion
  79.5 1.4 multiply_add_fusion.1
  80.9 1.0 copy-done
  82.4 0.9 slice_convert_fusion.3
  84.1 1.1 slice_convert_fusion.2
  85.4 1.3 multiply_add_fusion.2
  86.7 0.9 copy-done.2
  87.9 0.7 bitcast_dynamic-update-slice_fusion.1
  88.6 0.7 broadcast_dynamic-update-slice_fusion.2
  89.3 0.7 bitcast_dynamic-update-slice_fusion
  90.0 0.7 broadcast_dynamic-update-slice_fusion.1
  90.8 0.7 constant_dynamic-update-slice_fusion.2
  91.5 0.7 broadcast_dynamic-update-slice_fusion
  92.5 1.4 multiply_add_fusion
  94.3 0.8 constant_dynamic-update-slice_fusion.1
  95.1 0.7 broadcast_dynamic-update-slice_fusion.3
  95.8 6.4 %all-to-all-start.1 = ((bf16[8,1152,128]{2,1,0:T(8,128)(2,1)}), bf16[8,1152,128]{2,1,0:T(8,128)(2,1)S(1)}, u32[]{:S(2)}, u32[]{:S(2)}) async-start(bf16[8,1152,128]{2,1,0:T(8,128)(2,1)} %broadcast_dynamic-update-slice_fusion.3), calls=%async_computation.1 | async-start | bytes 4718592 | tf_op jit(solution)/shard_map/all_to_all | solution.py:125
  102.3 31.6 %all-to-all-done.1 = bf16[8,1152,128]{2,1,0:T(8,128)(2,1)S(1)} async-done(((bf16[8,1152,128]{2,1,0:T(8,128)(2,1)}), bf16[8,1152,128]{2,1,0:T(8,128)(2,1)S(1)}, u32[]{:S(2)}, u32[]{:S(2)}) %all-to-all-start.1) | async-done | bytes 2359328 | tf_op jit(solution)/shard_map/all_to_all | solution.py:125
  133.9 8.8 %conditional.2 = (f32[768,1536]{1,0:T(8,128)}, f32[]{:T(128)}) conditional(s32[]{:T(128)} %clamp.4, bf16[8,1152,128]{2,1,0:T(8,128)(2,1)S(1)} %all-to-all-done.1, bf16[8,1152,128]{2,1,0:T(8,128)(2,1)S(1)} %all-to-all-done.1, bf16[8,1152,128]{2,1,0:T(8,128)(2,1)S(1)} %all-to-all-done.1, ...), branch_computations={%region_1.3_spmd, %region_3.5_spmd, %region_5.7_spmd, %region_7.9_... | conditional | flops 3538943 | bytes 21233684 | solution.py:143
  133.9 1.4 slice.45
  135.3 3.6 %reshape.94 = bf16[768,1152]{1,0:T(8,128)(2,1)S(1)} reshape(bf16[8,864,128]{2,1,0:T(8,128)(2,1)} %slice.45) | data formatting | bytes 3538944 | tf_op jit(solution)/shard_map/cond/branch_0_fun/reshape | solution.py:132
  138.9 3.8 %multiply_reduce_fusion = (f32[]{:T(128)}, f32[768,1536]{1,0:T(8,128)}) fusion(bf16[768,1152]{1,0:T(8,128)(2,1)S(1)} %reshape.94), kind=kLoop, calls=%fused_computation | loop fusion | flops 3538943 | bytes 6488068 | tf_op jit(solution)/shard_map/reduce_sum | solution.py:23
  142.7 1.4 collective-permute-done
  145.3 2.9 %divide_convert_fusion = bf16[768,1536]{1,0:T(8,128)(2,1)S(1)} fusion(f32[768,1536]{1,0:T(8,128)} %get-tuple-element.34, f32[]{:T(128)S(6)} %add.135), kind=kLoop, calls=%fused_computation.9 | loop fusion | flops 2359296 | bytes 7077892 | tf_op jit(solution)/shard_map/convert_element_type | solution.py:25
  148.2 2.0 fusion.19
  150.5 2.8 %collective-permute-done.1 = bf16[768,768]{1,0:T(8,128)(2,1)} collective-permute-done((bf16[768,768]{1,0:T(8,128)(2,1)S(1)}, bf16[768,768]{1,0:T(8,128)(2,1)}, u32[]{:S(2)}, u32[]{:S(2)}) %collective-permute-start.1) | collective-permute-done | bytes 1179680 | tf_op jit(solution)/shard_map/ppermute | solution.py:102
  153.3 6.7 %add_convert_fusion.1 = bf16[768,1536]{1,0:T(8,128)(2,1)} fusion(bf16[768,1536]{1,0:T(8,128)(2,1)S(1)} %divide_convert_fusion, bf16[768,768]{1,0:T(8,128)(2,1)} %collective-permute-done.1, bf16[768,768]{1,0:T(8,128)(2,1)S(1)} %fusion.19), kind=kOutput, calls=%fused_computation.8 | convolution fusion | flops 2730295296 | bytes 7077888 | tf_op jit(solution)/shard_map/dot_general | solution.py:32
  160.0 4.6 %fusion.20 = bf16[768,768]{1,0:T(8,128)(2,1)S(1)} fusion(bf16[768,1536]{1,0:T(8,128)(2,1)} %add_convert_fusion.1), kind=kOutput, calls=%fused_computation.82 | convolution fusion | flops 1811939328 | bytes 3538944 | tf_op jit(solution)/shard_map/dot_general | solution.py:28
  164.8 2.8 %collective-permute-done.2 = bf16[768,768]{1,0:T(8,128)(2,1)S(1)} collective-permute-done((bf16[768,768]{1,0:T(8,128)(2,1)S(1)}, bf16[768,768]{1,0:T(8,128)(2,1)S(1)}, u32[]{:S(2)}, u32[]{:S(2)}) %collective-permute-start.2) | collective-permute-done | bytes 1179680 | tf_op jit(solution)/shard_map/ppermute | solution.py:102
  167.5 6.8 %add_convert_fusion = bf16[768,1536]{1,0:T(8,128)(2,1)} fusion(bf16[768,1536]{1,0:T(8,128)(2,1)} %add_convert_fusion.1, bf16[768,768]{1,0:T(8,128)(2,1)S(1)} %collective-permute-done.2, bf16[768,768]{1,0:T(8,128)(2,1)S(1)} %fusion.20), kind=kOutput, calls=%fused_computation.7 | convolution fusion | flops 2730295296 | bytes 7077888 | tf_op jit(solution)/shard_map/dot_general | solution.py:32
  174.4 4.5 %fusion.21 = bf16[768,768]{1,0:T(8,128)(2,1)S(1)} fusion(bf16[768,1536]{1,0:T(8,128)(2,1)} %add_convert_fusion), kind=kOutput, calls=%fused_computation.83 | convolution fusion | flops 1811939328 | bytes 3538944 | tf_op jit(solution)/shard_map/dot_general | solution.py:28
  179.7 2.1 collective-permute-done.3
  181.8 1.0 copy-done.12
  182.9 7.4 %multiply_convert_fusion = bf16[768,1536]{1,0:T(8,128)(2,1)S(1)} fusion(bf16[768,1536]{1,0:T(8,128)(2,1)} %add_convert_fusion, f32[]{:T(128)} %bitcast.3, bf16[768,768]{1,0:T(8,128)(2,1)} %copy-done.12, bf16[768,768]{1,0:T(8,128)(2,1)S(1)} %fusion.21), kind=kOutput, calls=%fused_computation.6 | convolution fusion | flops 2731474944 | bytes 7077892 | tf_op jit(solution)/shard_map/dot_general | solution.py:32
  190.3 6.5 %conditional.3 = (bf16[8,1152,128]{2,1,0:T(8,128)(2,1)}) conditional(s32[]{:T(128)} %clamp.4, bf16[768,1536]{1,0:T(8,128)(2,1)S(1)} %multiply_convert_fusion, bf16[768,1536]{1,0:T(8,128)(2,1)S(1)} %multiply_convert_fusion, bf16[768,1536]{1,0:T(8,128)(2,1)S(1)} %multiply_convert_fusion, ...), branch_computations={%region_10.11_spmd, %region_11.12_spmd, %region_12.13_spmd, %regio... | conditional | bytes 11206666 | solution.py:163
  190.3 1.4 slice.47
  191.7 3.5 %reshape.96 = bf16[8,864,128]{2,1,0:T(8,128)(2,1)S(1)} reshape(bf16[768,1152]{1,0:T(8,128)(2,1)} %slice.47) | data formatting | bytes 3538944 | tf_op jit(solution)/shard_map/cond/branch_0_fun/reshape | solution.py:155
  195.2 1.6 pad.23
  196.8 48.5 %all_to_all.28 = bf16[8,1152,128]{2,1,0:T(8,128)(2,1)S(1)} all-to-all(bf16[8,1152,128]{2,1,0:T(8,128)(2,1)} %get-tuple-element.75), channel_id=1, replica_groups=mesh['dp'=16,'shard'=8] {'shard'}, dimensions={0} | all-to-all | bytes 4718592 | tf_op jit(solution)/shard_map/all_to_all | solution.py:164
  245.6 1.5 multiply_subtract_fusion.1
  247.1 1.5 collective-permute-done.4
  248.6 1.1 broadcast_select_fusion.1
  249.7 1.0 select_n.128
  250.7 1.0 select_n.130
  251.7 1.1 select_n.124
  252.7 1.1 select_n.126
  253.8 1.6 broadcast_select_fusion.7
  255.4 1.5 select_n.119
  256.9 1.6 select_n.121
  258.5 1.7 broadcast_select_fusion.5
  260.2 1.3 select_n.114
  261.6 1.2 select_n.116
  262.8 1.6 pad_maximum_fusion.4
  264.4 0.9 pad_maximum_fusion.2
  265.2 0.9 pad_maximum_fusion.1
  266.1 0.8 pad_maximum_fusion.3
  266.9 3.0 %multiply_subtract_fusion = (f32[1,256,768]{2,1,0:T(8,128)}, f32[1,256,768]{2,1,0:T(8,128)}, f32[1,256,768]{2,1,0:T(8,128)}) fusion(f32[1,256,768]{2,1,0:T(8,128)S(1)} %copy-done.7, bf16[1,256,768]{2,1,0:T(8,128)(2,1)} %reduce-scatter.2.cloned.1.call-done, f32[1,256,768]{2,1,0:T(8,128)S(1)} %copy-done.8, f32[1,256,768]{2,1,0:T(8,128)} %param.39), kind=kLoop, calls=%fused_computation.24 | loop fusion | flops 3145728 | bytes 5111808 | tf_op jit(solution)/shard_map/sub | solution.py:47
  (58 shorter events, 4.6 us)
Async XLA Ops:
  7.2 70.7 %all-gather.2.cloned.1.call-start = ((), (), s32[]{:S(2)}) async-start(), calls=%async_computation.4 | async-start | bytes 1949696 | tf_op jit(solution)/shard_map/all_gather | solution.py:83
  9.9 2.9 %copy-start.11 = (bf16[1,9984]{1,0:T(2,128)(2,1)S(1)}, bf16[1,9984]{1,0:T(2,128)(2,1)}, u32[]{:S(2)}) copy-start(bf16[1,9984]{1,0:T(2,128)(2,1)} %param.31) | copy-start | bytes 59908
  80.9 1.0 copy-start
  81.9 1.5 copy-start.10
  83.4 0.7 copy-start.9
  86.6 0.9 copy-start.2
  93.9 1.9 copy-start.1
  95.8 38.1 %all-to-all-start.1 = ((bf16[8,1152,128]{2,1,0:T(8,128)(2,1)}), bf16[8,1152,128]{2,1,0:T(8,128)(2,1)S(1)}, u32[]{:S(2)}, u32[]{:S(2)}) async-start(bf16[8,1152,128]{2,1,0:T(8,128)(2,1)} %broadcast_dynamic-update-slice_fusion.3), calls=%async_computation.1 | async-start | bytes 4718592 | tf_op jit(solution)/shard_map/all_to_all | solution.py:125
  102.2 164.7 %reduce-scatter.2.cloned.1.call-start = ((), (), s32[]{:S(2)}) async-start(), calls=%async_computation.5 | async-start | bytes 6684672 | tf_op jit(solution)/shard_map/reduce_scatter | solution.py:179
  142.7 1.4 collective-permute-start
  150.2 3.1 %collective-permute-start.1 = (bf16[768,768]{1,0:T(8,128)(2,1)S(1)}, bf16[768,768]{1,0:T(8,128)(2,1)}, u32[]{:S(2)}, u32[]{:S(2)}) collective-permute-start(bf16[768,768]{1,0:T(8,128)(2,1)S(1)} %fusion.19), channel_id=1, source_target_pairs={{0,8},{8,0},{16,24},{24,16},{32,40},{40,32},{48,56},{56,48},{64,72... | collective-permute-start | bytes 3538952 | tf_op jit(solution)/shard_map/ppermute | solution.py:102
  164.5 3.0 %collective-permute-start.2 = (bf16[768,768]{1,0:T(8,128)(2,1)S(1)}, bf16[768,768]{1,0:T(8,128)(2,1)S(1)}, u32[]{:S(2)}, u32[]{:S(2)}) collective-permute-start(bf16[768,768]{1,0:T(8,128)(2,1)S(1)} %fusion.20), channel_id=1, source_target_pairs={{0,8},{8,0},{16,24},{24,16},{32,40},{40,32},{48,56},{56,48},{64,72... | collective-permute-start | bytes 3538952 | tf_op jit(solution)/shard_map/ppermute | solution.py:102
  174.4 4.8 %copy-start.13 = (f32[5]{0:T(128)S(1)}, f32[5]{0:T(128)}, u32[]{:S(2)}) copy-start(f32[5]{0:T(128)} %constant.122.clone) | copy-start | bytes 64
  178.9 2.9 %collective-permute-start.3 = (bf16[768,768]{1,0:T(8,128)(2,1)S(1)}, bf16[768,768]{1,0:T(8,128)(2,1)S(1)}, u32[]{:S(2)}, u32[]{:S(2)}) collective-permute-start(bf16[768,768]{1,0:T(8,128)(2,1)S(1)} %fusion.21), channel_id=1, source_target_pairs={{0,8},{8,0},{16,24},{24,16},{32,40},{40,32},{48,56},{56,48},{64,72... | collective-permute-start | bytes 3538952 | tf_op jit(solution)/shard_map/ppermute | solution.py:102
  181.8 1.0 copy-start.12
  245.5 3.1 %collective-permute-start.4 = (bf16[4,1152,128]{2,1,0:T(8,128)(2,1)S(1)}, bf16[4,1152,128]{2,1,0:T(8,128)(2,1)}, u32[]{:S(2)}, u32[]{:S(2)}) collective-permute-start(bf16[4,1152,128]{2,1,0:T(8,128)(2,1)S(1)} %pad_maximum_fusion), channel_id=1, source_target_pairs={{0,8},{8,0},{16,24},{24,16},{32,40},{40,32},{48,56},{56,48},{64,72... | collective-permute-start | bytes 3538952 | tf_op jit(solution)/shard_map/ppermute | solution.py:102
  250.7 13.7 %copy-start.3 = (bf16[192,768]{1,0:T(8,128)(2,1)S(1)}, bf16[192,768]{1,0:T(8,128)(2,1)}, u32[]{:S(2)}) copy-start(bf16[192,768]{1,0:T(8,128)(2,1)} %select_n.128) | copy-start | bytes 884740
  251.7 12.7 %copy-start.4 = (bf16[192,768]{1,0:T(8,128)(2,1)S(1)}, bf16[192,768]{1,0:T(8,128)(2,1)}, u32[]{:S(2)}) copy-start(bf16[192,768]{1,0:T(8,128)(2,1)} %select_n.130) | copy-start | bytes 884740
  252.7 12.5 %copy-start.5 = (bf16[96,1536]{1,0:T(8,128)(2,1)S(1)}, bf16[96,1536]{1,0:T(8,128)(2,1)}, u32[]{:S(2)}) copy-start(bf16[96,1536]{1,0:T(8,128)(2,1)} %select_n.124) | copy-start | bytes 884740
  253.8 11.5 %copy-start.6 = (bf16[96,1536]{1,0:T(8,128)(2,1)S(1)}, bf16[96,1536]{1,0:T(8,128)(2,1)}, u32[]{:S(2)}) copy-start(bf16[96,1536]{1,0:T(8,128)(2,1)} %select_n.126) | copy-start | bytes 884740
  260.2 6.7 %copy-start.7 = (f32[1,256,768]{2,1,0:T(8,128)S(1)}, f32[1,256,768]{2,1,0:T(8,128)}, u32[]{:S(2)}) copy-start(f32[1,256,768]{2,1,0:T(8,128)} %param.37) | copy-start | bytes 2359300
  260.2 6.7 %copy-start.8 = (f32[1,256,768]{2,1,0:T(8,128)S(1)}, f32[1,256,768]{2,1,0:T(8,128)}, u32[]{:S(2)}) copy-start(f32[1,256,768]{2,1,0:T(8,128)} %param.38) | copy-start | bytes 2359300
Sparse Core Ops, SparseCore 0:
  45.3 32.5 all-gather.1
  150.6 81.9 reduce-scatter.1

commit v5 on v4

--- a/solution.py
+++ b/solution.py
@@ -164,16 +164,18 @@
     returned = lax.all_to_all(answered, "shard", 0, 0, tiled=True)
     mine = jnp.stack([returned[owners[which]] for which in range(4)])
     theirs = exchange(mine)
-    first = core == 0
     updates = []
     for which in range(4):
         hr, hc = halves[which].shape
         used = hr * hc // lanes
+        axis = 0 if flipped[which] else 1
+        size = (hr, hc)[axis]
         own = mine[which, :used].reshape(hr, hc)
         other = theirs[which, :used].reshape(hr, hc)
-        low = jnp.where(first, own, other)
-        high = jnp.where(first, other, own)
-        updates.append(jnp.concatenate([low, high], axis=0 if flipped[which] else 1))
+        whole = jnp.zeros(nesterov[which].shape, jnp.bfloat16)
+        whole = lax.dynamic_update_slice_in_dim(whole, own, core * size, axis)
+        whole = lax.dynamic_update_slice_in_dim(whole, other, (1 - core) * size, axis)
+        updates.append(whole)
 
     _, grad_embed = lax.optimization_barrier((incoming, grad_embed))
     embed_total = lax.psum_scatter(grad_embed, "dp", scatter_dimension=1, tiled=True).astype(

time: 279 us -> 267 us (0.957)
  other arithmetic: 28.7 us -> 19.6 us
  blocking collectives: 79.6 us -> 75.4 us
    select_n x8 -> x0, local copies, waits for them, and re-layouts: 9.73 us -> none  [the longest x4 4.92 us: local(): low = jnp.where(first, own, other)]
    select_n x3 -> x0, other arithmetic: 4.46 us -> none  [local(): low = jnp.where(first, own, other)]
    all_to_all x1, blocking collectives: 48.5 us -> 44.3 us  [local(): returned = lax.all_to_all(answered, 'shard', 0, 0, tiled=True)]
    concatenate x4 -> x0, other arithmetic: 4.11 us -> none  [local(): jnp.concatenate([low, high], axis=0 if flipped[which] else 1)]
    dynamic_update_slice x0 -> x8, local copies, waits for them, and re-layouts: none -> 3.54 us  [the longest x4 2.81 us: local(): lax.dynamic_update_slice_in_dim(whole, other, (1 - core) * size, axis)]
    slice x0 -> x5, local copies, waits for them, and re-layouts: none -> 3.16 us  [the longest x3 3.13 us: local(): other = theirs[which, :used].reshape(hr, hc)]
    unnamed x40 -> x48, local copies, waits for them, and re-layouts: 10.1 us -> 12.2 us
  transfers between devices with their start and end apart: 8 -> 8, of which waited for: 7 -> 6; matrix products, arithmetic and copies ran while one was open for 21% -> 20% of each run, Pallas kernels for 0% -> 0%
where the time goes in v5:
time: 267 us; the launch traced here: 265 us
  blocking collectives  75.4 us (28%)
  waiting for transfers between devices  73.4 us (27%)
  local copies, waits for them, and re-layouts  41 us (15%)
  matrix products  32 us (12%)
  other arithmetic  19.6 us (7%)
  between operations  16 us (6%)
  starting transfers between devices  7.27 us (3%)
    all_to_all x1, blocking collectives, local(): returned = lax.all_to_all(answered, 'shard', 0, 0, tiled=True)  44.3 us
    all_gather x1, waiting for transfers between devices, local(): gathered = lax.all_gather(reduced, 'dp', axis=0, tiled=True).reshape(-1)  32.7 us
    all_to_all x1, waiting for transfers between devices, local(): incoming = lax.all_to_all(outgoing, 'shard', 0, 0, tiled=True)  31.6 us
    all_to_all x1, blocking collectives, local(): lax.all_to_all(flat.reshape(replicas, -1, lanes), 'dp', 0, 0, tiled=True)  31.1 us
    dot_general x3, matrix products, newton_schulz(): jnp.dot(poly, current, preferred_element_type=jnp.float32)  21 us
    unnamed x48, local copies, waits for them, and re-layouts  12.2 us
    dot_general x3, matrix products, newton_schulz(): part = jnp.dot(current, current.T, preferred_element_type=jnp.bfloat16)  11 us
    ppermute x5, waiting for transfers between devices, exchange(): return lax.ppermute(value, 'dp', partner)  9.06 us
  transfers between devices with their start and end apart: 8, of which 6 were waited for; matrix products, arithmetic and copies ran while one was open for 20% of the time, Pallas kernels for 0%

profile of v5, /device:TPU:0, one launch (start us, length us, event | category | flops | bytes accessed | tf_op | source)
XLA Modules:
  0.0 264.6 jit_solution(6817454168784420177)
XLA Ops:
  7.2 1.5 reshape_squeeze.30
  8.8 1.1 reshape_squeeze.31
  9.9 1.2 copy.36
  11.1 1.6 reshape_squeeze.33
  13.1 31.1 %all_to_all.27 = bf16[16,448,128]{2,1,0:T(8,128)(2,1)S(1)} all-to-all(bf16[16,448,128]{2,1,0:T(8,128)(2,1)S(1)} %bitcast.31), channel_id=1, replica_groups=mesh['dp'=16,'shard'=8] {'dp'}, dimensions={0} | all-to-all | bytes 3670016 | tf_op jit(solution)/shard_map/all_to_all | solution.py:81
  44.2 0.9 reduce_sum.41
  45.2 32.7 %all-gather.2.cloned.1.call-done = bf16[7168,128]{1,0:T(8,128)(2,1)} async-done(((bf16[448,128]{1,0:T(8,128)(2,1)}), bf16[7168,128]{1,0:T(8,128)(2,1)}) %all-gather.2.cloned.1.call-update) | async-done | bytes 1835024 | tf_op jit(solution)/shard_map/all_gather | solution.py:83
  77.9 1.4 slice_convert_fusion
  79.5 1.4 multiply_add_fusion.1
  80.9 1.0 copy-done
  82.0 0.4 stack.20
  82.4 0.9 slice_convert_fusion.3
  83.5 0.7 reshape.87
  84.2 1.1 slice_convert_fusion.2
  85.4 1.3 multiply_add_fusion.2
  86.7 0.9 copy-done.2
  87.9 0.7 bitcast_dynamic-update-slice_fusion.1
  88.6 0.7 broadcast_dynamic-update-slice_fusion.2
  89.4 1.6 bitcast_dynamic-update-slice_fusion
  91.0 0.7 broadcast_dynamic-update-slice_fusion.1
  91.7 0.7 constant_dynamic-update-slice_fusion.2
  92.4 0.7 broadcast_dynamic-update-slice_fusion
  93.6 1.0 copy-done.1
  95.0 0.8 constant_dynamic-update-slice_fusion.1
  95.7 0.7 broadcast_dynamic-update-slice_fusion.3
  96.5 6.4 %all-to-all-start.1 = ((bf16[8,1152,128]{2,1,0:T(8,128)(2,1)}), bf16[8,1152,128]{2,1,0:T(8,128)(2,1)S(1)}, u32[]{:S(2)}, u32[]{:S(2)}) async-start(bf16[8,1152,128]{2,1,0:T(8,128)(2,1)} %broadcast_dynamic-update-slice_fusion.3), calls=%async_computation.1 | async-start | bytes 4718592 | tf_op jit(solution)/shard_map/all_to_all | solution.py:125
  102.9 31.6 %all-to-all-done.1 = bf16[8,1152,128]{2,1,0:T(8,128)(2,1)S(1)} async-done(((bf16[8,1152,128]{2,1,0:T(8,128)(2,1)}), bf16[8,1152,128]{2,1,0:T(8,128)(2,1)S(1)}, u32[]{:S(2)}, u32[]{:S(2)}) %all-to-all-start.1) | async-done | bytes 2359328 | tf_op jit(solution)/shard_map/all_to_all | solution.py:125
  134.5 8.8 %conditional.2 = (f32[768,1536]{1,0:T(8,128)}, f32[]{:T(128)}) conditional(s32[]{:T(128)} %clamp.4, bf16[8,1152,128]{2,1,0:T(8,128)(2,1)S(1)} %all-to-all-done.1, bf16[8,1152,128]{2,1,0:T(8,128)(2,1)S(1)} %all-to-all-done.1, bf16[8,1152,128]{2,1,0:T(8,128)(2,1)S(1)} %all-to-all-done.1, ...), branch_computations={%region_1.3_spmd, %region_3.5_spmd, %region_5.7_spmd, %region_7.9_... | conditional | flops 3538943 | bytes 21233684 | solution.py:143
  134.5 1.4 slice.45
  135.9 3.6 %reshape.78 = bf16[768,1152]{1,0:T(8,128)(2,1)S(1)} reshape(bf16[8,864,128]{2,1,0:T(8,128)(2,1)} %slice.45) | data formatting | bytes 3538944 | tf_op jit(solution)/shard_map/cond/branch_0_fun/reshape | solution.py:132
  139.5 3.8 %multiply_reduce_fusion = (f32[]{:T(128)}, f32[768,1536]{1,0:T(8,128)}) fusion(bf16[768,1152]{1,0:T(8,128)(2,1)S(1)} %reshape.78), kind=kLoop, calls=%fused_computation | loop fusion | flops 3538943 | bytes 6488068 | tf_op jit(solution)/shard_map/reduce_sum | solution.py:23
  143.3 1.2 collective-permute-done
  146.0 2.9 %divide_convert_fusion = bf16[768,1536]{1,0:T(8,128)(2,1)S(1)} fusion(f32[768,1536]{1,0:T(8,128)} %get-tuple-element.34, f32[]{:T(128)S(6)} %add.151), kind=kLoop, calls=%fused_computation.9 | loop fusion | flops 2359296 | bytes 7077892 | tf_op jit(solution)/shard_map/convert_element_type | solution.py:25
  148.9 2.0 fusion.20
  151.1 3.1 %collective-permute-done.1 = bf16[768,768]{1,0:T(8,128)(2,1)} collective-permute-done((bf16[768,768]{1,0:T(8,128)(2,1)S(1)}, bf16[768,768]{1,0:T(8,128)(2,1)}, u32[]{:S(2)}, u32[]{:S(2)}) %collective-permute-start.1) | collective-permute-done | bytes 1179680 | tf_op jit(solution)/shard_map/ppermute | solution.py:102
  154.2 6.7 %add_convert_fusion.1 = bf16[768,1536]{1,0:T(8,128)(2,1)} fusion(bf16[768,1536]{1,0:T(8,128)(2,1)S(1)} %divide_convert_fusion, bf16[768,768]{1,0:T(8,128)(2,1)} %collective-permute-done.1, bf16[768,768]{1,0:T(8,128)(2,1)S(1)} %fusion.20), kind=kOutput, calls=%fused_computation.8 | convolution fusion | flops 2730295296 | bytes 7077888 | tf_op jit(solution)/shard_map/dot_general | solution.py:32
  160.9 4.5 %fusion.21 = bf16[768,768]{1,0:T(8,128)(2,1)S(1)} fusion(bf16[768,1536]{1,0:T(8,128)(2,1)} %add_convert_fusion.1), kind=kOutput, calls=%fused_computation.79 | convolution fusion | flops 1811939328 | bytes 3538944 | tf_op jit(solution)/shard_map/dot_general | solution.py:28
  165.6 2.7 %collective-permute-done.2 = bf16[768,768]{1,0:T(8,128)(2,1)S(1)} collective-permute-done((bf16[768,768]{1,0:T(8,128)(2,1)S(1)}, bf16[768,768]{1,0:T(8,128)(2,1)S(1)}, u32[]{:S(2)}, u32[]{:S(2)}) %collective-permute-start.2) | collective-permute-done | bytes 1179680 | tf_op jit(solution)/shard_map/ppermute | solution.py:102
  168.4 6.9 %add_convert_fusion = bf16[768,1536]{1,0:T(8,128)(2,1)} fusion(bf16[768,1536]{1,0:T(8,128)(2,1)} %add_convert_fusion.1, bf16[768,768]{1,0:T(8,128)(2,1)S(1)} %collective-permute-done.2, bf16[768,768]{1,0:T(8,128)(2,1)S(1)} %fusion.21), kind=kOutput, calls=%fused_computation.7 | convolution fusion | flops 2730295296 | bytes 7077888 | tf_op jit(solution)/shard_map/dot_general | solution.py:32
  175.2 4.5 %fusion.22 = bf16[768,768]{1,0:T(8,128)(2,1)S(1)} fusion(bf16[768,1536]{1,0:T(8,128)(2,1)} %add_convert_fusion), kind=kOutput, calls=%fused_computation.80 | convolution fusion | flops 1811939328 | bytes 3538944 | tf_op jit(solution)/shard_map/dot_general | solution.py:28
  180.1 0.6 dynamic_slice.15
  180.6 2.0 collective-permute-done.3
  182.7 1.0 copy-done.16
  183.7 7.4 %multiply_convert_fusion = bf16[768,1536]{1,0:T(8,128)(2,1)S(1)} fusion(bf16[768,1536]{1,0:T(8,128)(2,1)} %add_convert_fusion, f32[]{:T(128)} %bitcast.3, bf16[768,768]{1,0:T(8,128)(2,1)} %copy-done.16, bf16[768,768]{1,0:T(8,128)(2,1)S(1)} %fusion.22), kind=kOutput, calls=%fused_computation.6 | convolution fusion | flops 2731474944 | bytes 7077892 | tf_op jit(solution)/shard_map/dot_general | solution.py:32
  191.1 6.5 %conditional.3 = (bf16[8,1152,128]{2,1,0:T(8,128)(2,1)}) conditional(s32[]{:T(128)} %clamp.4, bf16[768,1536]{1,0:T(8,128)(2,1)S(1)} %multiply_convert_fusion, bf16[768,1536]{1,0:T(8,128)(2,1)S(1)} %multiply_convert_fusion, bf16[768,1536]{1,0:T(8,128)(2,1)S(1)} %multiply_convert_fusion, ...), branch_computations={%region_10.11_spmd, %region_11.12_spmd, %region_12.13_spmd, %regio... | conditional | bytes 11206666 | solution.py:163
  191.1 1.4 slice.47
  192.5 3.5 %reshape.80 = bf16[8,864,128]{2,1,0:T(8,128)(2,1)S(1)} reshape(bf16[768,1152]{1,0:T(8,128)(2,1)} %slice.47) | data formatting | bytes 3538944 | tf_op jit(solution)/shard_map/cond/branch_0_fun/reshape | solution.py:155
  196.0 1.6 pad.23
  197.7 44.3 %all_to_all.28 = bf16[8,1152,128]{2,1,0:T(8,128)(2,1)S(1)} all-to-all(bf16[8,1152,128]{2,1,0:T(8,128)(2,1)} %get-tuple-element.69), channel_id=1, replica_groups=mesh['dp'=16,'shard'=8] {'shard'}, dimensions={0} | all-to-all | bytes 4718592 | tf_op jit(solution)/shard_map/all_to_all | solution.py:164
  242.0 1.2 pad_maximum_fusion
  243.2 1.4 multiply_subtract_fusion.1
  244.9 0.3 reshape_squeeze_stack_squeeze.6
  245.6 0.7 broadcast_in_dim.13
  246.3 0.6 constant_dynamic-update-slice_fusion.12
  247.2 0.6 copy-done.8
  248.0 1.3 fusion.19
  249.6 0.3 reshape_squeeze.38
  250.0 0.9 slice.90
  250.9 1.0 slice.88
  252.2 0.6 constant_dynamic-update-slice_fusion.11
  252.8 0.7 constant_dynamic-update-slice_fusion.7
  253.6 0.7 constant_dynamic-update-slice_fusion.9
  254.3 0.7 constant_dynamic-update-slice_fusion.13
  255.0 2.8 %multiply_subtract_fusion = (f32[1,256,768]{2,1,0:T(8,128)}, f32[1,256,768]{2,1,0:T(8,128)}, f32[1,256,768]{2,1,0:T(8,128)}) fusion(f32[1,256,768]{2,1,0:T(8,128)S(1)} %copy-done.4, bf16[1,256,768]{2,1,0:T(8,128)(2,1)} %reduce-scatter.2.cloned.1.call-done, f32[1,256,768]{2,1,0:T(8,128)S(1)} %copy-done.5, f32[1,256,768]{2,1,0:T(8,128)S(1)} %copy-done.6), kind=kLoop, calls=%fused_computation.24 | loop fusion | flops 3145728 | bytes 5111808 | tf_op jit(solution)/shard_map/sub | solution.py:47
  (76 shorter events, 4.6 us)
Async XLA Ops:
  7.2 70.7 %all-gather.2.cloned.1.call-start = ((), (), s32[]{:S(2)}) async-start(), calls=%async_computation.4 | async-start | bytes 1949696 | tf_op jit(solution)/shard_map/all_gather | solution.py:83
  9.9 2.9 %copy-start.15 = (bf16[1,9984]{1,0:T(2,128)(2,1)S(1)}, bf16[1,9984]{1,0:T(2,128)(2,1)}, u32[]{:S(2)}) copy-start(bf16[1,9984]{1,0:T(2,128)(2,1)} %param.31) | copy-start | bytes 59908
  80.9 1.0 copy-start
  81.9 1.5 copy-start.11
  83.4 0.7 copy-start.7
  86.7 0.9 copy-start.2
  87.9 5.5 %copy-start.3 = (f32[384,768]{1,0:T(8,128)S(1)}, f32[384,768]{1,0:T(8,128)}, u32[]{:S(2)}) copy-start(f32[384,768]{1,0:T(8,128)} %param.36) | copy-start | bytes 3538948
  93.6 1.0 copy-start.1
  96.5 38.1 %all-to-all-start.1 = ((bf16[8,1152,128]{2,1,0:T(8,128)(2,1)}), bf16[8,1152,128]{2,1,0:T(8,128)(2,1)S(1)}, u32[]{:S(2)}, u32[]{:S(2)}) async-start(bf16[8,1152,128]{2,1,0:T(8,128)(2,1)} %broadcast_dynamic-update-slice_fusion.3), calls=%async_computation.1 | async-start | bytes 4718592 | tf_op jit(solution)/shard_map/all_to_all | solution.py:125
  102.9 152.1 %reduce-scatter.2.cloned.1.call-start = ((), (), s32[]{:S(2)}) async-start(), calls=%async_computation.5 | async-start | bytes 6684672 | tf_op jit(solution)/shard_map/reduce_scatter | solution.py:181
  143.3 1.3 collective-permute-start
  150.9 3.3 %collective-permute-start.1 = (bf16[768,768]{1,0:T(8,128)(2,1)S(1)}, bf16[768,768]{1,0:T(8,128)(2,1)}, u32[]{:S(2)}, u32[]{:S(2)}) collective-permute-start(bf16[768,768]{1,0:T(8,128)(2,1)S(1)} %fusion.20), channel_id=1, source_target_pairs={{0,8},{8,0},{16,24},{24,16},{32,40},{40,32},{48,56},{56,48},{64,72... | collective-permute-start | bytes 3538952 | tf_op jit(solution)/shard_map/ppermute | solution.py:102
  165.4 2.9 %collective-permute-start.2 = (bf16[768,768]{1,0:T(8,128)(2,1)S(1)}, bf16[768,768]{1,0:T(8,128)(2,1)S(1)}, u32[]{:S(2)}, u32[]{:S(2)}) collective-permute-start(bf16[768,768]{1,0:T(8,128)(2,1)S(1)} %fusion.21), channel_id=1, source_target_pairs={{0,8},{8,0},{16,24},{24,16},{32,40},{40,32},{48,56},{56,48},{64,72... | collective-permute-start | bytes 3538952 | tf_op jit(solution)/shard_map/ppermute | solution.py:102
  175.2 4.8 %copy-start.17 = (f32[5]{0:T(128)S(1)}, f32[5]{0:T(128)}, u32[]{:S(2)}) copy-start(f32[5]{0:T(128)} %constant.126.clone) | copy-start | bytes 64
  179.7 2.9 %collective-permute-start.3 = (bf16[768,768]{1,0:T(8,128)(2,1)S(1)}, bf16[768,768]{1,0:T(8,128)(2,1)S(1)}, u32[]{:S(2)}, u32[]{:S(2)}) collective-permute-start(bf16[768,768]{1,0:T(8,128)(2,1)S(1)} %fusion.22), channel_id=1, source_target_pairs={{0,8},{8,0},{16,24},{24,16},{32,40},{40,32},{48,56},{56,48},{64,72... | collective-permute-start | bytes 3538952 | tf_op jit(solution)/shard_map/ppermute | solution.py:102
  182.7 1.1 copy-start.16
  241.9 1.3 copy-start.12
  241.9 1.3 copy-start.13
  241.9 1.3 copy-start.14
  243.2 4.8 %collective-permute-start.4 = (bf16[4,1152,128]{2,1,0:T(8,128)(2,1)}, bf16[4,1152,128]{2,1,0:T(8,128)(2,1)}, u32[]{:S(2)}, u32[]{:S(2)}) collective-permute-start(bf16[4,1152,128]{2,1,0:T(8,128)(2,1)} %pad_maximum_fusion), channel_id=1, source_target_pairs={{0,8},{8,0},{16,24},{24,16},{32,40},{40,32},{48,56},{56,48},{64,72... | collective-permute-start | bytes 3538952 | tf_op jit(solution)/shard_map/ppermute | solution.py:102
  247.0 0.8 copy-start.8
  247.1 0.9 copy-start.9
  248.0 1.3 copy-start.10
  249.3 5.7 %copy-start.4 = (f32[1,256,768]{2,1,0:T(8,128)S(1)}, f32[1,256,768]{2,1,0:T(8,128)}, u32[]{:S(2)}) copy-start(f32[1,256,768]{2,1,0:T(8,128)} %param.37) | copy-start | bytes 2359300
  249.3 5.7 %copy-start.5 = (f32[1,256,768]{2,1,0:T(8,128)S(1)}, f32[1,256,768]{2,1,0:T(8,128)}, u32[]{:S(2)}) copy-start(f32[1,256,768]{2,1,0:T(8,128)} %param.38) | copy-start | bytes 2359300
  249.3 5.7 %copy-start.6 = (f32[1,256,768]{2,1,0:T(8,128)S(1)}, f32[1,256,768]{2,1,0:T(8,128)}, u32[]{:S(2)}) copy-start(f32[1,256,768]{2,1,0:T(8,128)} %param.39) | copy-start | bytes 2359300
Sparse Core Ops, SparseCore 0:
  45.3 32.5 all-gather.1
  143.5 77.6 reduce-scatter.1

commit v6 on v5

--- a/solution.py
+++ b/solution.py
@@ -117,11 +117,10 @@
     for which in range(4):
         owned = jnp.where(myself == owners[which], which, owned)
 
-    pieces = [jnp.zeros((slot, lanes), jnp.bfloat16)] * groups
-    for which in range(4):
-        part = halves[which].reshape(-1, lanes)
-        pieces[owners[which]] = jnp.pad(part, ((0, slot - part.shape[0]), (0, 0)))
-    outgoing = jnp.stack(pieces)
+    outgoing = jnp.zeros((groups, slot, lanes), jnp.bfloat16)
+    for which in range(4):
+        part = halves[which].reshape(1, -1, lanes)
+        outgoing = lax.dynamic_update_slice(outgoing, part, (owners[which], 0, 0))
     incoming = lax.all_to_all(outgoing, "shard", 0, 0, tiled=True)
 
     def assemble(which):
@@ -153,7 +152,8 @@
             else:
                 part = y[: groups * hr, :hc]
             part = part.reshape(groups, -1, lanes)
-            return jnp.pad(part, ((0, 0), (0, slot - part.shape[1]), (0, 0)))
+            empty = jnp.zeros((groups, slot, lanes), jnp.bfloat16)
+            return lax.dynamic_update_slice(empty, part, (0, 0, 0))
 
         return branch
 

time: 267 us -> 265 us (level)
    dynamic_update_slice x0 -> x5, local copies, waits for them, and re-layouts: none -> 5.49 us  [the longest x4 3.87 us: local(): outgoing = lax.dynamic_update_slice(outgoing, part, (owners[which], 0, 0))]
    unnamed x48 -> x45, local copies, waits for them, and re-layouts: 12.2 us -> 6.77 us
  transfers between devices with their start and end apart: 8 -> 8, of which waited for: 6 -> 6; matrix products, arithmetic and copies ran while one was open for 20% -> 21% of each run, Pallas kernels for 0% -> 0%
where the time goes in v6:
time: 265 us; the launch traced here: 263 us
  blocking collectives  75.3 us (28%)
  waiting for transfers between devices  73.5 us (28%)
  local copies, waits for them, and re-layouts  39.7 us (15%)
  matrix products  32 us (12%)
  other arithmetic  19.1 us (7%)
  between operations  15.9 us (6%)
  starting transfers between devices  7.34 us (3%)
    all_to_all x1, blocking collectives, local(): returned = lax.all_to_all(answered, 'shard', 0, 0, tiled=True)  44.2 us
    all_gather x1, waiting for transfers between devices, local(): gathered = lax.all_gather(reduced, 'dp', axis=0, tiled=True).reshape(-1)  32.7 us
    all_to_all x1, waiting for transfers between devices, local(): incoming = lax.all_to_all(outgoing, 'shard', 0, 0, tiled=True)  31.6 us
    all_to_all x1, blocking collectives, local(): lax.all_to_all(flat.reshape(replicas, -1, lanes), 'dp', 0, 0, tiled=True)  31.1 us
    dot_general x3, matrix products, newton_schulz(): jnp.dot(poly, current, preferred_element_type=jnp.float32)  21 us
    dot_general x3, matrix products, newton_schulz(): part = jnp.dot(current, current.T, preferred_element_type=jnp.bfloat16)  11 us
    ppermute x5, waiting for transfers between devices, exchange(): return lax.ppermute(value, 'dp', partner)  9.14 us
    unnamed x45, local copies, waits for them, and re-layouts  6.77 us
  transfers between devices with their start and end apart: 8, of which 6 were waited for; matrix products, arithmetic and copies ran while one was open for 21% of the time, Pallas kernels for 0%

profile of v6, /device:TPU:0, one launch (start us, length us, event | category | flops | bytes accessed | tf_op | source)
XLA Modules:
  0.0 263.0 jit_solution(9426736222365060728)
XLA Ops:
  7.2 1.5 reshape_squeeze.30
  8.8 1.1 reshape_squeeze.31
  9.9 1.2 copy.36
  11.1 1.6 reshape_squeeze.33
  13.1 31.1 %all_to_all.27 = bf16[16,448,128]{2,1,0:T(8,128)(2,1)S(1)} all-to-all(bf16[16,448,128]{2,1,0:T(8,128)(2,1)S(1)} %bitcast.27), channel_id=1, replica_groups=mesh['dp'=16,'shard'=8] {'dp'}, dimensions={0} | all-to-all | bytes 3670016 | tf_op jit(solution)/shard_map/all_to_all | solution.py:81
  44.2 0.9 reduce_sum.41
  45.2 32.7 %all-gather.2.cloned.1.call-done = bf16[7168,128]{1,0:T(8,128)(2,1)} async-done(((bf16[448,128]{1,0:T(8,128)(2,1)}), bf16[7168,128]{1,0:T(8,128)(2,1)}) %all-gather.2.cloned.1.call-update) | async-done | bytes 1835024 | tf_op jit(solution)/shard_map/all_gather | solution.py:83
  77.9 1.4 slice_convert_fusion
  79.5 1.4 multiply_add_fusion
  81.0 1.0 copy-done
  82.0 0.8 fusion.2
  82.8 1.9 reshape.91
  85.1 1.0 copy-done.1
  86.2 0.4 reshape.90
  86.5 0.9 slice_convert_fusion.3
  87.7 0.6 copy-done.9
  88.3 1.1 slice_convert_fusion.2
  89.7 0.9 copy-done.2
  90.9 1.7 dynamic_update_slice.42
  92.6 0.6 constant_dynamic-update-slice_fusion.10
  93.3 0.7 constant_dynamic-update-slice_fusion.9
  94.0 0.8 constant_dynamic-update-slice_fusion.8
  94.8 6.4 %all-to-all-start.1 = ((bf16[8,1152,128]{2,1,0:T(8,128)(2,1)}), bf16[8,1152,128]{2,1,0:T(8,128)(2,1)S(1)}, u32[]{:S(2)}, u32[]{:S(2)}) async-start(bf16[8,1152,128]{2,1,0:T(8,128)(2,1)} %constant_dynamic-update-slice_fusion.8), calls=%async_computation.1 | async-start | bytes 4718592 | tf_op jit(solution)/shard_map/all_to_all | solution.py:124
  101.2 31.6 %all-to-all-done.1 = bf16[8,1152,128]{2,1,0:T(8,128)(2,1)S(1)} async-done(((bf16[8,1152,128]{2,1,0:T(8,128)(2,1)}), bf16[8,1152,128]{2,1,0:T(8,128)(2,1)S(1)}, u32[]{:S(2)}, u32[]{:S(2)}) %all-to-all-start.1) | async-done | bytes 2359328 | tf_op jit(solution)/shard_map/all_to_all | solution.py:124
  132.8 8.8 %conditional.2 = (f32[768,1536]{1,0:T(8,128)}, f32[]{:T(128)}) conditional(s32[]{:T(128)} %clamp.4, bf16[8,1152,128]{2,1,0:T(8,128)(2,1)S(1)} %all-to-all-done.1, bf16[8,1152,128]{2,1,0:T(8,128)(2,1)S(1)} %all-to-all-done.1, bf16[8,1152,128]{2,1,0:T(8,128)(2,1)S(1)} %all-to-all-done.1, ...), branch_computations={%region_1.3_spmd, %region_3.5_spmd, %region_5.7_spmd, %region_7.9_... | conditional | flops 3538943 | bytes 21233684 | solution.py:142
  132.8 1.4 slice.45
  134.2 3.6 %reshape.78 = bf16[768,1152]{1,0:T(8,128)(2,1)S(1)} reshape(bf16[8,864,128]{2,1,0:T(8,128)(2,1)} %slice.45) | data formatting | bytes 3538944 | tf_op jit(solution)/shard_map/cond/branch_0_fun/reshape | solution.py:131
  137.8 3.8 %multiply_reduce_fusion = (f32[]{:T(128)}, f32[768,1536]{1,0:T(8,128)}) fusion(bf16[768,1152]{1,0:T(8,128)(2,1)S(1)} %reshape.78), kind=kLoop, calls=%fused_computation | loop fusion | flops 3538943 | bytes 6488068 | tf_op jit(solution)/shard_map/reduce_sum | solution.py:23
  141.6 1.4 collective-permute-done
  144.4 2.9 %divide_convert_fusion = bf16[768,1536]{1,0:T(8,128)(2,1)S(1)} fusion(f32[768,1536]{1,0:T(8,128)} %get-tuple-element.34, f32[]{:T(128)S(6)} %add.149), kind=kLoop, calls=%fused_computation.9 | loop fusion | flops 2359296 | bytes 7077892 | tf_op jit(solution)/shard_map/convert_element_type | solution.py:25
  147.2 2.0 fusion.20
  149.5 3.1 %collective-permute-done.1 = bf16[768,768]{1,0:T(8,128)(2,1)} collective-permute-done((bf16[768,768]{1,0:T(8,128)(2,1)S(1)}, bf16[768,768]{1,0:T(8,128)(2,1)}, u32[]{:S(2)}, u32[]{:S(2)}) %collective-permute-start.1) | collective-permute-done | bytes 1179680 | tf_op jit(solution)/shard_map/ppermute | solution.py:102
  152.6 6.8 %add_convert_fusion.1 = bf16[768,1536]{1,0:T(8,128)(2,1)} fusion(bf16[768,1536]{1,0:T(8,128)(2,1)S(1)} %divide_convert_fusion, bf16[768,768]{1,0:T(8,128)(2,1)} %collective-permute-done.1, bf16[768,768]{1,0:T(8,128)(2,1)S(1)} %fusion.20), kind=kOutput, calls=%fused_computation.8 | convolution fusion | flops 2730295296 | bytes 7077888 | tf_op jit(solution)/shard_map/dot_general | solution.py:32
  159.4 4.5 %fusion.21 = bf16[768,768]{1,0:T(8,128)(2,1)S(1)} fusion(bf16[768,1536]{1,0:T(8,128)(2,1)} %add_convert_fusion.1), kind=kOutput, calls=%fused_computation.74 | convolution fusion | flops 1811939328 | bytes 3538944 | tf_op jit(solution)/shard_map/dot_general | solution.py:28
  164.1 2.7 %collective-permute-done.2 = bf16[768,768]{1,0:T(8,128)(2,1)S(1)} collective-permute-done((bf16[768,768]{1,0:T(8,128)(2,1)S(1)}, bf16[768,768]{1,0:T(8,128)(2,1)S(1)}, u32[]{:S(2)}, u32[]{:S(2)}) %collective-permute-start.2) | collective-permute-done | bytes 1179680 | tf_op jit(solution)/shard_map/ppermute | solution.py:102
  166.8 6.9 %add_convert_fusion = bf16[768,1536]{1,0:T(8,128)(2,1)} fusion(bf16[768,1536]{1,0:T(8,128)(2,1)} %add_convert_fusion.1, bf16[768,768]{1,0:T(8,128)(2,1)S(1)} %collective-permute-done.2, bf16[768,768]{1,0:T(8,128)(2,1)S(1)} %fusion.21), kind=kOutput, calls=%fused_computation.7 | convolution fusion | flops 2730295296 | bytes 7077888 | tf_op jit(solution)/shard_map/dot_general | solution.py:32
  173.7 4.5 %fusion.22 = bf16[768,768]{1,0:T(8,128)(2,1)S(1)} fusion(bf16[768,1536]{1,0:T(8,128)(2,1)} %add_convert_fusion), kind=kOutput, calls=%fused_computation.75 | convolution fusion | flops 1811939328 | bytes 3538944 | tf_op jit(solution)/shard_map/dot_general | solution.py:28
  178.2 0.4 collective-permute-start.3
  178.6 0.6 dynamic_slice.15
  179.2 1.9 collective-permute-done.3
  181.1 1.0 copy-done.18
  182.2 7.4 %multiply_convert_fusion = bf16[768,1536]{1,0:T(8,128)(2,1)S(1)} fusion(bf16[768,1536]{1,0:T(8,128)(2,1)} %add_convert_fusion, f32[]{:T(128)} %bitcast.3, bf16[768,768]{1,0:T(8,128)(2,1)} %copy-done.18, bf16[768,768]{1,0:T(8,128)(2,1)S(1)} %fusion.22), kind=kOutput, calls=%fused_computation.6 | convolution fusion | flops 2731474944 | bytes 7077892 | tf_op jit(solution)/shard_map/dot_general | solution.py:32
  189.6 6.5 %conditional.3 = (bf16[8,1152,128]{2,1,0:T(8,128)(2,1)}) conditional(s32[]{:T(128)} %clamp.4, bf16[768,1536]{1,0:T(8,128)(2,1)S(1)} %multiply_convert_fusion, bf16[768,1536]{1,0:T(8,128)(2,1)S(1)} %multiply_convert_fusion, bf16[768,1536]{1,0:T(8,128)(2,1)S(1)} %multiply_convert_fusion, ...), branch_computations={%region_10.11_spmd, %region_11.12_spmd, %region_12.13_spmd, %regio... | conditional | bytes 11206666 | solution.py:163
  189.6 1.4 slice.47
  191.0 3.5 %reshape.80 = bf16[8,864,128]{2,1,0:T(8,128)(2,1)S(1)} reshape(bf16[768,1152]{1,0:T(8,128)(2,1)} %slice.47) | data formatting | bytes 3538944 | tf_op jit(solution)/shard_map/cond/branch_0_fun/reshape | solution.py:154
  194.5 1.6 dynamic_update_slice.28
  196.1 44.2 %all_to_all.28 = bf16[8,1152,128]{2,1,0:T(8,128)(2,1)S(1)} all-to-all(bf16[8,1152,128]{2,1,0:T(8,128)(2,1)} %get-tuple-element.69), channel_id=1, replica_groups=mesh['dp'=16,'shard'=8] {'shard'}, dimensions={0} | all-to-all | bytes 4718592 | tf_op jit(solution)/shard_map/all_to_all | solution.py:164
  240.4 1.2 pad_maximum_fusion
  241.6 1.4 multiply_subtract_fusion.1
  243.2 0.3 reshape_squeeze_stack_squeeze.6
  243.7 0.3 reshape_squeeze.34
  244.0 0.7 broadcast_in_dim.13
  244.6 0.6 constant_dynamic-update-slice_fusion.5
  245.6 0.6 copy-done.10
  246.4 1.3 fusion.19
  248.0 0.3 reshape_squeeze.38
  248.3 0.9 slice.90
  249.3 1.0 slice.88
  250.2 0.3 reshape_squeeze.35
  250.5 0.6 constant_dynamic-update-slice_fusion.4
  251.2 0.7 constant_dynamic-update-slice_fusion
  251.9 0.7 constant_dynamic-update-slice_fusion.2
  252.6 0.7 constant_dynamic-update-slice_fusion.6
  253.4 2.8 %multiply_subtract_fusion = (f32[1,256,768]{2,1,0:T(8,128)}, f32[1,256,768]{2,1,0:T(8,128)}, f32[1,256,768]{2,1,0:T(8,128)}) fusion(f32[1,256,768]{2,1,0:T(8,128)S(1)} %copy-done.6, bf16[1,256,768]{2,1,0:T(8,128)(2,1)} %reduce-scatter.2.cloned.1.call-done, f32[1,256,768]{2,1,0:T(8,128)S(1)} %copy-done.7, f32[1,256,768]{2,1,0:T(8,128)S(1)} %copy-done.8), kind=kLoop, calls=%fused_computation.24 | loop fusion | flops 3145728 | bytes 5111808 | tf_op jit(solution)/shard_map/sub | solution.py:47
  (76 shorter events, 3.5 us)
Async XLA Ops:
  7.2 70.7 %all-gather.2.cloned.1.call-start = ((), (), s32[]{:S(2)}) async-start(), calls=%async_computation.4 | async-start | bytes 1949696 | tf_op jit(solution)/shard_map/all_gather | solution.py:83
  9.9 2.9 %copy-start.17 = (bf16[1,9984]{1,0:T(2,128)(2,1)S(1)}, bf16[1,9984]{1,0:T(2,128)(2,1)}, u32[]{:S(2)}) copy-start(bf16[1,9984]{1,0:T(2,128)(2,1)} %param.31) | copy-start | bytes 59908
  81.0 1.0 copy-start
  82.0 2.9 %copy-start.3 = (f32[96,3072]{1,0:T(8,128)S(1)}, f32[96,3072]{1,0:T(8,128)}, u32[]{:S(2)}) copy-start(f32[96,3072]{1,0:T(8,128)} %param.35) | copy-start | bytes 3538948
  85.0 1.0 copy-start.1
  86.1 1.5 copy-start.13
  87.5 2.0 copy-start.5
  87.6 0.7 copy-start.9
  89.7 0.9 copy-start.2
  90.6 3.4 %copy-start.4 = (bf16[1,1152,128]{2,1,0:T(8,128)(2,1)S(1)}, bf16[1,1152,128]{2,1,0:T(8,128)(2,1)}, u32[]{:S(2)}) copy-start(bf16[1,1152,128]{2,1,0:T(8,128)(2,1)} %reshape.91) | copy-start | bytes 884740
  94.8 38.1 %all-to-all-start.1 = ((bf16[8,1152,128]{2,1,0:T(8,128)(2,1)}), bf16[8,1152,128]{2,1,0:T(8,128)(2,1)S(1)}, u32[]{:S(2)}, u32[]{:S(2)}) async-start(bf16[8,1152,128]{2,1,0:T(8,128)(2,1)} %constant_dynamic-update-slice_fusion.8), calls=%async_computation.1 | async-start | bytes 4718592 | tf_op jit(solution)/shard_map/all_to_all | solution.py:124
  101.2 152.2 %reduce-scatter.2.cloned.1.call-start = ((), (), s32[]{:S(2)}) async-start(), calls=%async_computation.5 | async-start | bytes 6684672 | tf_op jit(solution)/shard_map/reduce_scatter | solution.py:181
  141.6 1.4 collective-permute-start
  149.3 3.3 %collective-permute-start.1 = (bf16[768,768]{1,0:T(8,128)(2,1)S(1)}, bf16[768,768]{1,0:T(8,128)(2,1)}, u32[]{:S(2)}, u32[]{:S(2)}) collective-permute-start(bf16[768,768]{1,0:T(8,128)(2,1)S(1)} %fusion.20), channel_id=1, source_target_pairs={{0,8},{8,0},{16,24},{24,16},{32,40},{40,32},{48,56},{56,48},{64,72... | collective-permute-start | bytes 3538952 | tf_op jit(solution)/shard_map/ppermute | solution.py:102
  163.9 2.9 %collective-permute-start.2 = (bf16[768,768]{1,0:T(8,128)(2,1)S(1)}, bf16[768,768]{1,0:T(8,128)(2,1)S(1)}, u32[]{:S(2)}, u32[]{:S(2)}) collective-permute-start(bf16[768,768]{1,0:T(8,128)(2,1)S(1)} %fusion.21), channel_id=1, source_target_pairs={{0,8},{8,0},{16,24},{24,16},{32,40},{40,32},{48,56},{56,48},{64,72... | collective-permute-start | bytes 3538952 | tf_op jit(solution)/shard_map/ppermute | solution.py:102
  173.7 4.9 %copy-start.19 = (f32[5]{0:T(128)S(1)}, f32[5]{0:T(128)}, u32[]{:S(2)}) copy-start(f32[5]{0:T(128)} %constant.124.clone) | copy-start | bytes 64
  178.2 2.9 %collective-permute-start.3 = (bf16[768,768]{1,0:T(8,128)(2,1)S(1)}, bf16[768,768]{1,0:T(8,128)(2,1)S(1)}, u32[]{:S(2)}, u32[]{:S(2)}) collective-permute-start(bf16[768,768]{1,0:T(8,128)(2,1)S(1)} %fusion.22), channel_id=1, source_target_pairs={{0,8},{8,0},{16,24},{24,16},{32,40},{40,32},{48,56},{56,48},{64,72... | collective-permute-start | bytes 3538952 | tf_op jit(solution)/shard_map/ppermute | solution.py:102
  181.1 1.0 copy-start.18
  240.3 1.3 copy-start.14
  240.3 1.3 copy-start.15
  240.3 1.3 copy-start.16
  241.6 4.8 %collective-permute-start.4 = (bf16[4,1152,128]{2,1,0:T(8,128)(2,1)}, bf16[4,1152,128]{2,1,0:T(8,128)(2,1)}, u32[]{:S(2)}, u32[]{:S(2)}) collective-permute-start(bf16[4,1152,128]{2,1,0:T(8,128)(2,1)} %pad_maximum_fusion), channel_id=1, source_target_pairs={{0,8},{8,0},{16,24},{24,16},{32,40},{40,32},{48,56},{56,48},{64,72... | collective-permute-start | bytes 3538952 | tf_op jit(solution)/shard_map/ppermute | solution.py:102
  245.4 0.8 copy-start.10
  245.5 0.9 copy-start.11
  246.4 1.3 copy-start.12
  247.6 5.7 %copy-start.6 = (f32[1,256,768]{2,1,0:T(8,128)S(1)}, f32[1,256,768]{2,1,0:T(8,128)}, u32[]{:S(2)}) copy-start(f32[1,256,768]{2,1,0:T(8,128)} %param.37) | copy-start | bytes 2359300
  247.7 5.7 %copy-start.7 = (f32[1,256,768]{2,1,0:T(8,128)S(1)}, f32[1,256,768]{2,1,0:T(8,128)}, u32[]{:S(2)}) copy-start(f32[1,256,768]{2,1,0:T(8,128)} %param.38) | copy-start | bytes 2359300
  247.7 5.7 %copy-start.8 = (f32[1,256,768]{2,1,0:T(8,128)S(1)}, f32[1,256,768]{2,1,0:T(8,128)}, u32[]{:S(2)}) copy-start(f32[1,256,768]{2,1,0:T(8,128)} %param.39) | copy-start | bytes 2359300
Sparse Core Ops, SparseCore 0:
  45.3 32.5 all-gather.1
  141.8 77.3 reduce-scatter.1

commit v7 on v6

--- a/solution.py
+++ b/solution.py
@@ -78,9 +78,14 @@
     block = replicas * 16 * lanes
     padded = -(-flat.shape[0] // block) * block
     flat = jnp.pad(flat, (0, padded - flat.shape[0])).reshape(padded // lanes, lanes)
-    parts = lax.all_to_all(flat.reshape(replicas, -1, lanes), "dp", 0, 0, tiled=True)
-    reduced = jnp.sum(parts.astype(jnp.float32), axis=0).astype(jnp.bfloat16)
-    gathered = lax.all_gather(reduced, "dp", axis=0, tiled=True).reshape(-1)
+    blocks = flat.reshape(replicas, -1, lanes)
+    split = blocks.shape[1] // 2
+    collected = []
+    for rows in (slice(0, split), slice(split, None)):
+        parts = lax.all_to_all(blocks[:, rows, :], "dp", 0, 0, tiled=True)
+        reduced = jnp.sum(parts.astype(jnp.float32), axis=0).astype(jnp.bfloat16)
+        collected.append(lax.all_gather(reduced, "dp", axis=0, tiled=False))
+    gathered = jnp.concatenate(collected, axis=1).reshape(-1)
     sums = []
     offset = 0
     for g, n in zip(grads, sizes):

time: 265 us -> 276 us (1.042)
  blocking collectives: 75.3 us -> 113 us
  waiting for transfers between devices: 73.5 us -> 41 us
  starting transfers between devices: 7.34 us -> 11.1 us
    all_gather x0 -> x2, blocking collectives: none -> 48.1 us  [local(): collected.append(lax.all_gather(reduced, 'dp', axis=0, tiled=False))]
    all_gather x1 -> x0, waiting for transfers between devices: 32.7 us -> none  [local(): gathered = lax.all_gather(reduced, 'dp', axis=0, tiled=True).reshape(-1)]
    all_to_all x1, blocking collectives: 31.1 us -> 21.3 us  [local(): parts = lax.all_to_all(blocks[:, rows, :], 'dp', 0, 0, tiled=True)]
    all_to_all x0 -> x1, starting transfers between devices: none -> 3.64 us  [local(): parts = lax.all_to_all(blocks[:, rows, :], 'dp', 0, 0, tiled=True)]
    unnamed x45 -> x49, local copies, waits for them, and re-layouts: 6.77 us -> 6.17 us
  transfers between devices with their start and end apart: 8 -> 8, of which waited for: 6 -> 5; matrix products, arithmetic and copies ran while one was open for 21% -> 20% of each run, Pallas kernels for 0% -> 0%
where the time goes in v7:
time: 276 us; the launch traced here: 273 us
  blocking collectives  113 us (41%)
  local copies, waits for them, and re-layouts  41.8 us (15%)
  waiting for transfers between devices  41 us (15%)
  matrix products  32 us (12%)
  other arithmetic  18.3 us (7%)
  between operations  15.8 us (6%)
  starting transfers between devices  11.1 us (4%)
    all_gather x2, blocking collectives, local(): collected.append(lax.all_gather(reduced, 'dp', axis=0, tiled=False))  48.1 us
    all_to_all x1, blocking collectives, local(): returned = lax.all_to_all(answered, 'shard', 0, 0, tiled=True)  43.9 us
    all_to_all x1, waiting for transfers between devices, local(): incoming = lax.all_to_all(outgoing, 'shard', 0, 0, tiled=True)  31.7 us
    all_to_all x1, blocking collectives, local(): parts = lax.all_to_all(blocks[:, rows, :], 'dp', 0, 0, tiled=True)  21.3 us
    dot_general x3, matrix products, newton_schulz(): jnp.dot(poly, current, preferred_element_type=jnp.float32)  21 us
    dot_general x3, matrix products, newton_schulz(): part = jnp.dot(current, current.T, preferred_element_type=jnp.bfloat16)  11 us
    ppermute x5, waiting for transfers between devices, exchange(): return lax.ppermute(value, 'dp', partner)  9.22 us
    all_to_all x1, starting transfers between devices, local(): incoming = lax.all_to_all(outgoing, 'shard', 0, 0, tiled=True)  6.64 us
  transfers between devices with their start and end apart: 8, of which 5 were waited for; matrix products, arithmetic and copies ran while one was open for 20% of the time, Pallas kernels for 0%

profile of v7, /device:TPU:0, one launch (start us, length us, event | category | flops | bytes accessed | tf_op | source)
XLA Modules:
  0.0 273.4 jit_solution(5953355723076001211)
XLA Ops:
  7.2 1.5 reshape_squeeze.30
  8.8 1.1 reshape_squeeze.31
  9.8 1.2 copy.36
  11.0 1.6 reshape_squeeze.33
  13.0 1.0 fusion.19
  14.1 21.3 %all_to_all.32 = bf16[16,224,128]{2,1,0:T(8,128)(2,1)S(1)} all-to-all(bf16[16,224,128]{2,1,0:T(8,128)(2,1)S(1)} %get-tuple-element.57), channel_id=1, replica_groups=mesh['dp'=16,'shard'=8] {'dp'}, dimensions={0} | all-to-all | bytes 1835008 | tf_op jit(solution)/shard_map/all_to_all | solution.py:85
  35.4 3.6 %all-to-all-start.1 = ((bf16[16,224,128]{2,1,0:T(8,128)(2,1)}), bf16[16,224,128]{2,1,0:T(8,128)(2,1)S(1)}, u32[]{:S(2)}, u32[]{:S(2)}) async-start(bf16[16,224,128]{2,1,0:T(8,128)(2,1)} %get-tuple-element.58), calls=%async_computation.1 | async-start | bytes 1835008 | tf_op jit(solution)/shard_map/all_to_all | solution.py:85
  39.2 29.2 %all-gather = bf16[3584,128]{1,0:T(8,128)(2,1)S(1)} all-gather(bf16[224,128]{1,0:T(8,128)(2,1)S(1)} %reduce_sum.53), channel_id=2, replica_groups=mesh['dp'=16,'shard'=8] {'dp'}, dimensions={0}, use_global_device_ids=true | all-gather | bytes 974848 | tf_op jit(solution)/shard_map/all_gather | solution.py:87
  68.5 18.9 %all-gather.1 = bf16[3584,128]{1,0:T(8,128)(2,1)S(1)} all-gather(bf16[224,128]{1,0:T(8,128)(2,1)S(1)} %reduce_sum.54), channel_id=3, replica_groups=mesh['dp'=16,'shard'=8] {'dp'}, dimensions={0}, use_global_device_ids=true | all-gather | bytes 974848 | tf_op jit(solution)/shard_map/all_gather | solution.py:87
  87.8 0.9 slice_convert_fusion.3
  88.7 1.0 slice_convert_fusion.2
  89.9 1.4 multiply_add_fusion
  91.3 1.0 copy-done.2
  92.4 0.8 fusion.2
  93.2 1.9 reshape.83
  95.4 1.0 copy-done.3
  96.5 0.4 reshape.82
  96.9 1.1 reshape.86
  98.0 1.0 multiply_add_fusion.3
  99.0 0.7 reshape.81
  100.0 0.9 copy-done.4
  101.2 1.7 dynamic_update_slice.42
  103.0 0.6 constant_dynamic-update-slice_fusion.10
  103.6 0.7 constant_dynamic-update-slice_fusion.9
  104.3 0.8 constant_dynamic-update-slice_fusion.8
  105.1 6.6 %all-to-all-start.2 = ((bf16[8,1152,128]{2,1,0:T(8,128)(2,1)}), bf16[8,1152,128]{2,1,0:T(8,128)(2,1)S(1)}, u32[]{:S(2)}, u32[]{:S(2)}) async-start(bf16[8,1152,128]{2,1,0:T(8,128)(2,1)} %constant_dynamic-update-slice_fusion.8), calls=%async_computation.2 | async-start | bytes 4718592 | tf_op jit(solution)/shard_map/all_to_all | solution.py:129
  111.8 31.7 %all-to-all-done.2 = bf16[8,1152,128]{2,1,0:T(8,128)(2,1)S(1)} async-done(((bf16[8,1152,128]{2,1,0:T(8,128)(2,1)}), bf16[8,1152,128]{2,1,0:T(8,128)(2,1)S(1)}, u32[]{:S(2)}, u32[]{:S(2)}) %all-to-all-start.2) | async-done | bytes 2359328 | tf_op jit(solution)/shard_map/all_to_all | solution.py:129
  143.5 8.8 %conditional.2 = (f32[768,1536]{1,0:T(8,128)}, f32[]{:T(128)}) conditional(s32[]{:T(128)} %clamp.4, bf16[8,1152,128]{2,1,0:T(8,128)(2,1)S(1)} %all-to-all-done.2, bf16[8,1152,128]{2,1,0:T(8,128)(2,1)S(1)} %all-to-all-done.2, bf16[8,1152,128]{2,1,0:T(8,128)(2,1)S(1)} %all-to-all-done.2, ...), branch_computations={%region_2.4_spmd, %region_4.6_spmd, %region_6.8_spmd, %region_8.10... | conditional | flops 3538943 | bytes 21233684 | solution.py:147
  143.5 1.4 slice.44
  144.9 3.6 %reshape.68 = bf16[768,1152]{1,0:T(8,128)(2,1)S(1)} reshape(bf16[8,864,128]{2,1,0:T(8,128)(2,1)} %slice.44) | data formatting | bytes 3538944 | tf_op jit(solution)/shard_map/cond/branch_0_fun/reshape | solution.py:136
  148.5 3.8 %multiply_reduce_fusion = (f32[]{:T(128)}, f32[768,1536]{1,0:T(8,128)}) fusion(bf16[768,1152]{1,0:T(8,128)(2,1)S(1)} %reshape.68), kind=kLoop, calls=%fused_computation | loop fusion | flops 3538943 | bytes 6488068 | tf_op jit(solution)/shard_map/reduce_sum | solution.py:23
  152.4 1.4 collective-permute-done
  155.0 2.9 %divide_convert_fusion = bf16[768,1536]{1,0:T(8,128)(2,1)S(1)} fusion(f32[768,1536]{1,0:T(8,128)} %get-tuple-element.34, f32[]{:T(128)S(6)} %add.149), kind=kLoop, calls=%fused_computation.9 | loop fusion | flops 2359296 | bytes 7077892 | tf_op jit(solution)/shard_map/convert_element_type | solution.py:25
  157.9 2.0 fusion.21
  160.2 3.1 %collective-permute-done.1 = bf16[768,768]{1,0:T(8,128)(2,1)} collective-permute-done((bf16[768,768]{1,0:T(8,128)(2,1)S(1)}, bf16[768,768]{1,0:T(8,128)(2,1)}, u32[]{:S(2)}, u32[]{:S(2)}) %collective-permute-start.1) | collective-permute-done | bytes 1179680 | tf_op jit(solution)/shard_map/ppermute | solution.py:107
  163.3 6.8 %add_convert_fusion.1 = bf16[768,1536]{1,0:T(8,128)(2,1)} fusion(bf16[768,1536]{1,0:T(8,128)(2,1)S(1)} %divide_convert_fusion, bf16[768,768]{1,0:T(8,128)(2,1)} %collective-permute-done.1, bf16[768,768]{1,0:T(8,128)(2,1)S(1)} %fusion.21), kind=kOutput, calls=%fused_computation.8 | convolution fusion | flops 2730295296 | bytes 7077888 | tf_op jit(solution)/shard_map/dot_general | solution.py:32
  170.1 4.5 %fusion.22 = bf16[768,768]{1,0:T(8,128)(2,1)S(1)} fusion(bf16[768,1536]{1,0:T(8,128)(2,1)} %add_convert_fusion.1), kind=kOutput, calls=%fused_computation.74 | convolution fusion | flops 1811939328 | bytes 3538944 | tf_op jit(solution)/shard_map/dot_general | solution.py:28
  174.8 2.8 %collective-permute-done.2 = bf16[768,768]{1,0:T(8,128)(2,1)S(1)} collective-permute-done((bf16[768,768]{1,0:T(8,128)(2,1)S(1)}, bf16[768,768]{1,0:T(8,128)(2,1)S(1)}, u32[]{:S(2)}, u32[]{:S(2)}) %collective-permute-start.2) | collective-permute-done | bytes 1179680 | tf_op jit(solution)/shard_map/ppermute | solution.py:107
  177.5 6.9 %add_convert_fusion = bf16[768,1536]{1,0:T(8,128)(2,1)} fusion(bf16[768,1536]{1,0:T(8,128)(2,1)} %add_convert_fusion.1, bf16[768,768]{1,0:T(8,128)(2,1)S(1)} %collective-permute-done.2, bf16[768,768]{1,0:T(8,128)(2,1)S(1)} %fusion.22), kind=kOutput, calls=%fused_computation.7 | convolution fusion | flops 2730295296 | bytes 7077888 | tf_op jit(solution)/shard_map/dot_general | solution.py:32
  184.4 4.5 %fusion.23 = bf16[768,768]{1,0:T(8,128)(2,1)S(1)} fusion(bf16[768,1536]{1,0:T(8,128)(2,1)} %add_convert_fusion), kind=kOutput, calls=%fused_computation.75 | convolution fusion | flops 1811939328 | bytes 3538944 | tf_op jit(solution)/shard_map/dot_general | solution.py:28
  188.9 0.4 collective-permute-start.3
  189.3 0.6 dynamic_slice.15
  189.9 2.0 collective-permute-done.3
  191.8 1.0 copy-done.20
  192.9 7.4 %multiply_convert_fusion = bf16[768,1536]{1,0:T(8,128)(2,1)S(1)} fusion(bf16[768,1536]{1,0:T(8,128)(2,1)} %add_convert_fusion, f32[]{:T(128)} %bitcast.6, bf16[768,768]{1,0:T(8,128)(2,1)} %copy-done.20, bf16[768,768]{1,0:T(8,128)(2,1)S(1)} %fusion.23), kind=kOutput, calls=%fused_computation.6 | convolution fusion | flops 2731474944 | bytes 7077892 | tf_op jit(solution)/shard_map/dot_general | solution.py:32
  200.2 6.5 %conditional.3 = (bf16[8,1152,128]{2,1,0:T(8,128)(2,1)}) conditional(s32[]{:T(128)} %clamp.4, bf16[768,1536]{1,0:T(8,128)(2,1)S(1)} %multiply_convert_fusion, bf16[768,1536]{1,0:T(8,128)(2,1)S(1)} %multiply_convert_fusion, bf16[768,1536]{1,0:T(8,128)(2,1)S(1)} %multiply_convert_fusion, ...), branch_computations={%region_11.12_spmd, %region_12.13_spmd, %region_13.14_spmd, %regio... | conditional | bytes 11206666 | solution.py:168
  200.3 1.4 slice.46
  201.6 3.5 %reshape.70 = bf16[8,864,128]{2,1,0:T(8,128)(2,1)S(1)} reshape(bf16[768,1152]{1,0:T(8,128)(2,1)} %slice.46) | data formatting | bytes 3538944 | tf_op jit(solution)/shard_map/cond/branch_0_fun/reshape | solution.py:159
  205.2 1.6 dynamic_update_slice.28
  206.8 43.9 %all_to_all.33 = bf16[8,1152,128]{2,1,0:T(8,128)(2,1)S(1)} all-to-all(bf16[8,1152,128]{2,1,0:T(8,128)(2,1)} %get-tuple-element.71), channel_id=1, replica_groups=mesh['dp'=16,'shard'=8] {'shard'}, dimensions={0} | all-to-all | bytes 4718592 | tf_op jit(solution)/shard_map/all_to_all | solution.py:169
  250.8 1.2 pad_maximum_fusion.1
  252.0 1.4 multiply_subtract_fusion.1
  253.6 0.3 reshape_squeeze_stack_squeeze.6
  254.4 0.7 broadcast_in_dim.13
  255.0 0.6 constant_dynamic-update-slice_fusion.5
  256.0 0.6 copy-done.12
  256.8 1.3 fusion.20
  258.7 0.9 slice.95
  259.7 1.0 slice.93
  260.9 0.6 constant_dynamic-update-slice_fusion.4
  261.6 0.7 constant_dynamic-update-slice_fusion
  262.3 0.7 constant_dynamic-update-slice_fusion.2
  263.0 0.7 constant_dynamic-update-slice_fusion.6
  263.8 2.8 %multiply_subtract_fusion = (f32[1,256,768]{2,1,0:T(8,128)}, f32[1,256,768]{2,1,0:T(8,128)}, f32[1,256,768]{2,1,0:T(8,128)}) fusion(f32[1,256,768]{2,1,0:T(8,128)S(1)} %copy-done.8, bf16[1,256,768]{2,1,0:T(8,128)(2,1)} %reduce-scatter.2.cloned.1.call-done, f32[1,256,768]{2,1,0:T(8,128)S(1)} %copy-done.9, f32[1,256,768]{2,1,0:T(8,128)S(1)} %copy-done.10), kind=kLoop, calls=%fused_computation.25 | loop fusion | flops 3145728 | bytes 5111808 | tf_op jit(solution)/shard_map/sub | solution.py:47
  (84 shorter events, 4.8 us)
Async XLA Ops:
  9.8 2.9 %copy-start.19 = (bf16[1,9984]{1,0:T(2,128)(2,1)S(1)}, bf16[1,9984]{1,0:T(2,128)(2,1)}, u32[]{:S(2)}) copy-start(bf16[1,9984]{1,0:T(2,128)(2,1)} %param.31) | copy-start | bytes 59908
  35.4 33.0 %all-to-all-start.1 = ((bf16[16,224,128]{2,1,0:T(8,128)(2,1)}), bf16[16,224,128]{2,1,0:T(8,128)(2,1)S(1)}, u32[]{:S(2)}, u32[]{:S(2)}) async-start(bf16[16,224,128]{2,1,0:T(8,128)(2,1)} %get-tuple-element.58), calls=%async_computation.1 | async-start | bytes 1835008 | tf_op jit(solution)/shard_map/all_to_all | solution.py:85
  87.6 2.1 copy-start
  91.3 1.0 copy-start.2
  92.4 2.9 %copy-start.5 = (f32[96,3072]{1,0:T(8,128)S(1)}, f32[96,3072]{1,0:T(8,128)}, u32[]{:S(2)}) copy-start(f32[96,3072]{1,0:T(8,128)} %param.35) | copy-start | bytes 3538948
  95.4 1.0 copy-start.3
  96.4 3.3 %copy-start.1 = (f32[221184]{0:T(1024)S(1)}, f32[221184]{0:T(1024)}, u32[]{:S(2)}) copy-start(f32[221184]{0:T(1024)} %slice_convert_fusion.2) | copy-start | bytes 2654212
  96.5 3.4 %copy-start.7 = (f32[96,2304]{1,0:T(8,128)S(1)}, f32[96,2304]{1,0:T(8,128)}, u32[]{:S(2)}) copy-start(f32[96,2304]{1,0:T(8,128)} %param.33) | copy-start | bytes 2654212
  99.0 1.0 copy-start.11
  100.0 0.9 copy-start.4
  100.9 2.0 copy-start.15
  100.9 3.4 %copy-start.6 = (bf16[1,1152,128]{2,1,0:T(8,128)(2,1)S(1)}, bf16[1,1152,128]{2,1,0:T(8,128)(2,1)}, u32[]{:S(2)}) copy-start(bf16[1,1152,128]{2,1,0:T(8,128)(2,1)} %reshape.83) | copy-start | bytes 884740
  105.1 38.4 %all-to-all-start.2 = ((bf16[8,1152,128]{2,1,0:T(8,128)(2,1)}), bf16[8,1152,128]{2,1,0:T(8,128)(2,1)S(1)}, u32[]{:S(2)}, u32[]{:S(2)}) async-start(bf16[8,1152,128]{2,1,0:T(8,128)(2,1)} %constant_dynamic-update-slice_fusion.8), calls=%async_computation.2 | async-start | bytes 4718592 | tf_op jit(solution)/shard_map/all_to_all | solution.py:129
  111.7 152.0 %reduce-scatter.2.cloned.1.call-start = ((), (), s32[]{:S(2)}) async-start(), calls=%async_computation.5 | async-start | bytes 6684672 | tf_op jit(solution)/shard_map/reduce_scatter | solution.py:186
  152.3 1.4 collective-permute-start
  159.9 3.3 %collective-permute-start.1 = (bf16[768,768]{1,0:T(8,128)(2,1)S(1)}, bf16[768,768]{1,0:T(8,128)(2,1)}, u32[]{:S(2)}, u32[]{:S(2)}) collective-permute-start(bf16[768,768]{1,0:T(8,128)(2,1)S(1)} %fusion.21), channel_id=1, source_target_pairs={{0,8},{8,0},{16,24},{24,16},{32,40},{40,32},{48,56},{56,48},{64,72... | collective-permute-start | bytes 3538952 | tf_op jit(solution)/shard_map/ppermute | solution.py:107
  174.6 3.0 %collective-permute-start.2 = (bf16[768,768]{1,0:T(8,128)(2,1)S(1)}, bf16[768,768]{1,0:T(8,128)(2,1)S(1)}, u32[]{:S(2)}, u32[]{:S(2)}) collective-permute-start(bf16[768,768]{1,0:T(8,128)(2,1)S(1)} %fusion.22), channel_id=1, source_target_pairs={{0,8},{8,0},{16,24},{24,16},{32,40},{40,32},{48,56},{56,48},{64,72... | collective-permute-start | bytes 3538952 | tf_op jit(solution)/shard_map/ppermute | solution.py:107
  184.4 4.9 %copy-start.21 = (f32[5]{0:T(128)S(1)}, f32[5]{0:T(128)}, u32[]{:S(2)}) copy-start(f32[5]{0:T(128)} %constant.125.clone) | copy-start | bytes 64
  188.9 2.9 %collective-permute-start.3 = (bf16[768,768]{1,0:T(8,128)(2,1)S(1)}, bf16[768,768]{1,0:T(8,128)(2,1)S(1)}, u32[]{:S(2)}, u32[]{:S(2)}) collective-permute-start(bf16[768,768]{1,0:T(8,128)(2,1)S(1)} %fusion.23), channel_id=1, source_target_pairs={{0,8},{8,0},{16,24},{24,16},{32,40},{40,32},{48,56},{56,48},{64,72... | collective-permute-start | bytes 3538952 | tf_op jit(solution)/shard_map/ppermute | solution.py:107
  191.8 1.0 copy-start.20
  250.7 1.3 copy-start.16
  250.7 1.3 copy-start.17
  250.7 1.3 copy-start.18
  252.0 4.8 %collective-permute-start.4 = (bf16[4,1152,128]{2,1,0:T(8,128)(2,1)}, bf16[4,1152,128]{2,1,0:T(8,128)(2,1)}, u32[]{:S(2)}, u32[]{:S(2)}) collective-permute-start(bf16[4,1152,128]{2,1,0:T(8,128)(2,1)} %pad_maximum_fusion.1), channel_id=1, source_target_pairs={{0,8},{8,0},{16,24},{24,16},{32,40},{40,32},{48,56},{56,48},{64,72... | collective-permute-start | bytes 3538952 | tf_op jit(solution)/shard_map/ppermute | solution.py:107
  255.8 0.8 copy-start.12
  255.9 0.9 copy-start.13
  256.8 1.3 copy-start.14
  258.0 5.7 %copy-start.8 = (f32[1,256,768]{2,1,0:T(8,128)S(1)}, f32[1,256,768]{2,1,0:T(8,128)}, u32[]{:S(2)}) copy-start(f32[1,256,768]{2,1,0:T(8,128)} %param.37) | copy-start | bytes 2359300
  258.1 5.7 %copy-start.9 = (f32[1,256,768]{2,1,0:T(8,128)S(1)}, f32[1,256,768]{2,1,0:T(8,128)}, u32[]{:S(2)}) copy-start(f32[1,256,768]{2,1,0:T(8,128)} %param.38) | copy-start | bytes 2359300
  258.1 5.7 %copy-start.10 = (f32[1,256,768]{2,1,0:T(8,128)S(1)}, f32[1,256,768]{2,1,0:T(8,128)}, u32[]{:S(2)}) copy-start(f32[1,256,768]{2,1,0:T(8,128)} %param.39) | copy-start | bytes 2359300
Sparse Core Ops, SparseCore 0:
  152.5 76.7 reduce-scatter.1

commit v8 on v6

--- a/solution.py
+++ b/solution.py
@@ -87,12 +87,10 @@
         sums.append(gathered[offset : offset + n].reshape(g.shape))
         offset += n
     moments_old = (moment_qkv, moment_out, moment_up, moment_down)
-    new_moments = []
     nesterov = []
     for which in range(4):
         total = sums[which].astype(jnp.float32)
         fresh = keep_rate * moments_old[which] + total
-        new_moments.append(fresh)
         nesterov.append((total + keep_rate * fresh).astype(jnp.bfloat16))
 
     core = lax.axis_index("dp") % 2
@@ -122,6 +120,10 @@
         part = halves[which].reshape(1, -1, lanes)
         outgoing = lax.dynamic_update_slice(outgoing, part, (owners[which], 0, 0))
     incoming = lax.all_to_all(outgoing, "shard", 0, 0, tiled=True)
+    _, late_moments = lax.optimization_barrier((outgoing, moments_old))
+    new_moments = [
+        keep_rate * late_moments[which] + sums[which].astype(jnp.float32) for which in range(4)
+    ]
 
     def assemble(which):
         hr, hc = halves[which].shape

time: 265 us -> 267 us (level)
  blocking collectives: 75.3 us -> 31.1 us
  waiting for transfers between devices: 73.5 us -> 100 us
  starting transfers between devices: 7.34 us -> 16.6 us
  other arithmetic: 19.1 us -> 23.9 us
  matrix products: 32 us -> 34.9 us
    all_to_all x1 -> x0, blocking collectives: 44.2 us -> none  [local(): returned = lax.all_to_all(answered, 'shard', 0, 0, tiled=True)]
    all_to_all x0 -> x1, waiting for transfers between devices: none -> 26.8 us  [local(): returned = lax.all_to_all(answered, 'shard', 0, 0, tiled=True)]
    all_to_all x0 -> x1, starting transfers between devices: none -> 9.06 us  [local(): returned = lax.all_to_all(answered, 'shard', 0, 0, tiled=True)]
    add x4, other arithmetic: 1.69 us -> 5.55 us  [local(): keep_rate * late_moments[which] + sums[which].astype(jnp.float32)]
    dot_general x3, matrix products: 21 us -> 24 us  [newton_schulz(): jnp.dot(poly, current, preferred_element_type=jnp.float32)]
    unnamed x45 -> x59, local copies, waits for them, and re-layouts: 6.77 us -> 6.07 us
  transfers between devices with their start and end apart: 8 -> 9, of which waited for: 6 -> 7; matrix products, arithmetic and copies ran while one was open for 21% -> 24% of each run, Pallas kernels for 0% -> 0%
where the time goes in v8:
time: 267 us; the launch traced here: 265 us
  waiting for transfers between devices  100 us (37%)
  local copies, waits for them, and re-layouts  41.6 us (16%)
  matrix products  34.9 us (13%)
  blocking collectives  31.1 us (12%)
  other arithmetic  23.9 us (9%)
  starting transfers between devices  16.6 us (6%)
  between operations  16 us (6%)
    all_gather x1, waiting for transfers between devices, local(): gathered = lax.all_gather(reduced, 'dp', axis=0, tiled=True).reshape(-1)  32.7 us
    all_to_all x1, waiting for transfers between devices, local(): incoming = lax.all_to_all(outgoing, 'shard', 0, 0, tiled=True)  31.6 us
    all_to_all x1, blocking collectives, local(): lax.all_to_all(flat.reshape(replicas, -1, lanes), 'dp', 0, 0, tiled=True)  31.1 us
    all_to_all x1, waiting for transfers between devices, local(): returned = lax.all_to_all(answered, 'shard', 0, 0, tiled=True)  26.8 us
    dot_general x3, matrix products, newton_schulz(): jnp.dot(poly, current, preferred_element_type=jnp.float32)  24 us
    dot_general x3, matrix products, newton_schulz(): part = jnp.dot(current, current.T, preferred_element_type=jnp.bfloat16)  10.9 us
    ppermute x5, waiting for transfers between devices, exchange(): return lax.ppermute(value, 'dp', partner)  9.28 us
    all_to_all x1, starting transfers between devices, local(): returned = lax.all_to_all(answered, 'shard', 0, 0, tiled=True)  9.06 us
  transfers between devices with their start and end apart: 9, of which 7 were waited for; matrix products, arithmetic and copies ran while one was open for 24% of the time, Pallas kernels for 0%

profile of v8, /device:TPU:0, one launch (start us, length us, event | category | flops | bytes accessed | tf_op | source)
XLA Modules:
  0.0 264.5 jit_solution(16001716134944749044)
XLA Ops:
  7.2 1.5 reshape_squeeze.30
  8.8 1.1 reshape_squeeze.31
  9.9 1.2 copy.36
  11.1 1.6 reshape_squeeze.33
  13.1 31.1 %all_to_all.27 = bf16[16,448,128]{2,1,0:T(8,128)(2,1)S(1)} all-to-all(bf16[16,448,128]{2,1,0:T(8,128)(2,1)S(1)} %bitcast.27), channel_id=1, replica_groups=mesh['dp'=16,'shard'=8] {'dp'}, dimensions={0} | all-to-all | bytes 3670016 | tf_op jit(solution)/shard_map/all_to_all | solution.py:81
  44.2 0.9 reduce_sum.41
  45.2 32.7 %all-gather.2.cloned.1.call-done = bf16[7168,128]{1,0:T(8,128)(2,1)} async-done(((bf16[448,128]{1,0:T(8,128)(2,1)}), bf16[7168,128]{1,0:T(8,128)(2,1)}) %all-gather.2.cloned.1.call-update) | async-done | bytes 1835024 | tf_op jit(solution)/shard_map/all_gather | solution.py:83
  77.9 1.1 slice_convert_fusion.2
  79.5 1.7 dynamic_update_slice.42
  81.2 0.9 slice_convert_fusion.3
  82.3 0.7 reshape.89
  83.0 1.4 slice_convert_fusion
  84.6 1.2 fusion.9
  85.7 1.1 reshape.90
  87.1 1.6 fusion.5
  89.0 1.5 constant_dynamic-update-slice_fusion.10
  90.5 0.7 constant_dynamic-update-slice_fusion.9
  91.2 0.7 constant_dynamic-update-slice_fusion.8
  91.9 6.4 %all-to-all-start.1 = ((bf16[8,1152,128]{2,1,0:T(8,128)(2,1)}), bf16[8,1152,128]{2,1,0:T(8,128)(2,1)S(1)}, u32[]{:S(2)}, u32[]{:S(2)}) async-start(bf16[8,1152,128]{2,1,0:T(8,128)(2,1)} %constant_dynamic-update-slice_fusion.8), calls=%async_computation.1 | async-start | bytes 4718592 | tf_op jit(solution)/shard_map/all_to_all | solution.py:122
  98.4 31.6 %all-to-all-done.1 = bf16[8,1152,128]{2,1,0:T(8,128)(2,1)S(1)} async-done(((bf16[8,1152,128]{2,1,0:T(8,128)(2,1)}), bf16[8,1152,128]{2,1,0:T(8,128)(2,1)S(1)}, u32[]{:S(2)}, u32[]{:S(2)}) %all-to-all-start.1) | async-done | bytes 2359328 | tf_op jit(solution)/shard_map/all_to_all | solution.py:122
  130.0 8.8 %conditional.2 = (f32[768,1536]{1,0:T(8,128)}, f32[]{:T(128)}) conditional(s32[]{:T(128)} %clamp.4, bf16[8,1152,128]{2,1,0:T(8,128)(2,1)S(1)} %all-to-all-done.1, bf16[8,1152,128]{2,1,0:T(8,128)(2,1)S(1)} %all-to-all-done.1, bf16[8,1152,128]{2,1,0:T(8,128)(2,1)S(1)} %all-to-all-done.1, ...), branch_computations={%region_1.3_spmd, %region_3.5_spmd, %region_5.7_spmd, %region_7.9_... | conditional | flops 3538943 | bytes 21233684 | solution.py:144
  130.0 1.4 slice.45
  131.3 3.6 %reshape.78 = bf16[768,1152]{1,0:T(8,128)(2,1)S(1)} reshape(bf16[8,864,128]{2,1,0:T(8,128)(2,1)} %slice.45) | data formatting | bytes 3538944 | tf_op jit(solution)/shard_map/cond/branch_0_fun/reshape | solution.py:133
  135.0 3.8 %multiply_reduce_fusion = (f32[]{:T(128)}, f32[768,1536]{1,0:T(8,128)}) fusion(bf16[768,1152]{1,0:T(8,128)(2,1)S(1)} %reshape.78), kind=kLoop, calls=%fused_computation | loop fusion | flops 3538943 | bytes 6488068 | tf_op jit(solution)/shard_map/reduce_sum | solution.py:23
  138.8 1.2 collective-permute-done
  141.3 2.9 %divide_convert_fusion = bf16[768,1536]{1,0:T(8,128)(2,1)S(1)} fusion(f32[768,1536]{1,0:T(8,128)} %get-tuple-element.39, f32[]{:T(128)S(6)} %add.162), kind=kLoop, calls=%fused_computation.9 | loop fusion | flops 2359296 | bytes 7077892 | tf_op jit(solution)/shard_map/convert_element_type | solution.py:25
  144.2 2.0 fusion.32
  146.3 1.0 copy-done.24
  147.5 3.1 %collective-permute-done.1 = bf16[768,768]{1,0:T(8,128)(2,1)} collective-permute-done((bf16[768,768]{1,0:T(8,128)(2,1)S(1)}, bf16[768,768]{1,0:T(8,128)(2,1)}, u32[]{:S(2)}, u32[]{:S(2)}) %collective-permute-start.1) | collective-permute-done | bytes 1179680 | tf_op jit(solution)/shard_map/ppermute | solution.py:100
  150.5 8.2 %add_convert_fusion.1 = bf16[768,1536]{1,0:T(8,128)(2,1)} fusion(bf16[768,1536]{1,0:T(8,128)(2,1)S(1)} %divide_convert_fusion, bf16[768,768]{1,0:T(8,128)(2,1)} %collective-permute-done.1, bf16[768,768]{1,0:T(8,128)(2,1)} %copy-done.24), kind=kOutput, calls=%fused_computation.8 | convolution fusion | flops 2730295296 | bytes 7077888 | tf_op jit(solution)/shard_map/dot_general | solution.py:32
  158.7 4.4 %fusion.33 = bf16[768,768]{1,0:T(8,128)(2,1)S(1)} fusion(bf16[768,1536]{1,0:T(8,128)(2,1)} %add_convert_fusion.1), kind=kOutput, calls=%fused_computation.82 | convolution fusion | flops 1811939328 | bytes 3538944 | tf_op jit(solution)/shard_map/dot_general | solution.py:28
  163.5 2.8 %collective-permute-done.2 = bf16[768,768]{1,0:T(8,128)(2,1)S(1)} collective-permute-done((bf16[768,768]{1,0:T(8,128)(2,1)S(1)}, bf16[768,768]{1,0:T(8,128)(2,1)S(1)}, u32[]{:S(2)}, u32[]{:S(2)}) %collective-permute-start.2) | collective-permute-done | bytes 1179680 | tf_op jit(solution)/shard_map/ppermute | solution.py:100
  166.2 6.9 %add_convert_fusion = bf16[768,1536]{1,0:T(8,128)(2,1)} fusion(bf16[768,1536]{1,0:T(8,128)(2,1)} %add_convert_fusion.1, bf16[768,768]{1,0:T(8,128)(2,1)S(1)} %collective-permute-done.2, bf16[768,768]{1,0:T(8,128)(2,1)S(1)} %fusion.33), kind=kOutput, calls=%fused_computation.7 | convolution fusion | flops 2730295296 | bytes 7077888 | tf_op jit(solution)/shard_map/dot_general | solution.py:32
  173.2 4.5 %fusion.34 = bf16[768,768]{1,0:T(8,128)(2,1)S(1)} fusion(bf16[768,1536]{1,0:T(8,128)(2,1)} %add_convert_fusion), kind=kOutput, calls=%fused_computation.83 | convolution fusion | flops 1811939328 | bytes 3538944 | tf_op jit(solution)/shard_map/dot_general | solution.py:28
  178.1 0.6 dynamic_slice.19
  178.7 2.2 collective-permute-done.3
  180.9 1.0 copy-done.25
  181.9 8.9 %multiply_convert_fusion = bf16[768,1536]{1,0:T(8,128)(2,1)S(1)} fusion(bf16[768,1536]{1,0:T(8,128)(2,1)} %add_convert_fusion, f32[]{:T(128)} %bitcast.3, bf16[768,768]{1,0:T(8,128)(2,1)} %copy-done.25, bf16[768,768]{1,0:T(8,128)(2,1)} %copy-done.23), kind=kOutput, calls=%fused_computation.6 | convolution fusion | flops 2731474944 | bytes 7077892 | tf_op jit(solution)/shard_map/dot_general | solution.py:32
  190.8 6.5 %conditional.3 = (bf16[8,1152,128]{2,1,0:T(8,128)(2,1)}) conditional(s32[]{:T(128)} %clamp.4, bf16[768,1536]{1,0:T(8,128)(2,1)S(1)} %multiply_convert_fusion, bf16[768,1536]{1,0:T(8,128)(2,1)S(1)} %multiply_convert_fusion, bf16[768,1536]{1,0:T(8,128)(2,1)S(1)} %multiply_convert_fusion, ...), branch_computations={%region_10.11_spmd, %region_11.12_spmd, %region_12.13_spmd, %regio... | conditional | bytes 11206666 | solution.py:165
  190.8 1.4 slice.47
  192.2 3.5 %reshape.80 = bf16[8,864,128]{2,1,0:T(8,128)(2,1)S(1)} reshape(bf16[768,1152]{1,0:T(8,128)(2,1)} %slice.47) | data formatting | bytes 3538944 | tf_op jit(solution)/shard_map/cond/branch_0_fun/reshape | solution.py:156
  195.7 1.6 dynamic_update_slice.28
  197.3 9.1 %all-to-all-start.2 = ((bf16[8,1152,128]{2,1,0:T(8,128)(2,1)}), bf16[8,1152,128]{2,1,0:T(8,128)(2,1)}, u32[]{:S(2)}, u32[]{:S(2)}) async-start(bf16[8,1152,128]{2,1,0:T(8,128)(2,1)} %get-tuple-element.77), calls=%async_computation.2 | async-start | bytes 4718592 | tf_op jit(solution)/shard_map/all_to_all | solution.py:166
  206.5 2.6 multiply_add_fusion
  209.0 1.0 multiply_add_fusion.2
  210.1 1.2 multiply_add_fusion.1
  211.3 26.8 %all-to-all-done.2 = bf16[8,1152,128]{2,1,0:T(8,128)(2,1)} async-done(((bf16[8,1152,128]{2,1,0:T(8,128)(2,1)}), bf16[8,1152,128]{2,1,0:T(8,128)(2,1)}, u32[]{:S(2)}, u32[]{:S(2)}) %all-to-all-start.2) | async-done | bytes 2359328 | tf_op jit(solution)/shard_map/all_to_all | solution.py:166
  238.1 1.3 fusion.30
  239.7 0.7 multiply_add_fusion.3
  240.4 1.4 multiply_subtract_fusion.1
  242.5 1.0 slice.83
  243.7 0.9 slice.89
  244.6 0.7 broadcast_in_dim.13
  245.3 0.6 constant_dynamic-update-slice_fusion.5
  246.1 0.8 copy-done.17
  247.0 0.6 copy-done.18
  247.8 1.0 copy-done.15
  249.2 1.0 slice.90
  250.3 1.1 fusion.31
  252.0 0.6 constant_dynamic-update-slice_fusion.4
  252.7 0.7 constant_dynamic-update-slice_fusion
  253.4 0.7 constant_dynamic-update-slice_fusion.6
  254.1 0.7 constant_dynamic-update-slice_fusion.2
  254.9 2.8 %multiply_subtract_fusion = (f32[1,256,768]{2,1,0:T(8,128)}, f32[1,256,768]{2,1,0:T(8,128)}, f32[1,256,768]{2,1,0:T(8,128)}) fusion(f32[1,256,768]{2,1,0:T(8,128)S(1)} %copy-done.10, bf16[1,256,768]{2,1,0:T(8,128)(2,1)} %reduce-scatter.2.cloned.1.call-done, f32[1,256,768]{2,1,0:T(8,128)S(1)} %copy-done.11, f32[1,256,768]{2,1,0:T(8,128)S(1)} %copy-done.12), kind=kLoop, calls=%fused_computation.24 | loop fusion | flops 3145728 | bytes 5111808 | tf_op jit(solution)/shard_map/sub | solution.py:47
  (91 shorter events, 5.3 us)
Async XLA Ops:
  7.2 70.7 %all-gather.2.cloned.1.call-start = ((), (), s32[]{:S(2)}) async-start(), calls=%async_computation.4 | async-start | bytes 1949696 | tf_op jit(solution)/shard_map/all_gather | solution.py:83
  9.9 2.9 %copy-start.22 = (bf16[1,9984]{1,0:T(2,128)(2,1)S(1)}, bf16[1,9984]{1,0:T(2,128)(2,1)}, u32[]{:S(2)}) copy-start(bf16[1,9984]{1,0:T(2,128)(2,1)} %param.31) | copy-start | bytes 59908
  44.2 34.9 %copy-start.5 = (f32[96,2304]{1,0:T(8,128)S(1)}, f32[96,2304]{1,0:T(8,128)}, u32[]{:S(2)}) copy-start(f32[96,2304]{1,0:T(8,128)} %param.33) | copy-start | bytes 2654212
  79.1 3.1 %copy-start.2 = (f32[96,2304]{1,0:T(8,128)}, f32[96,2304]{1,0:T(8,128)S(1)}, u32[]{:S(2)}) copy-start(f32[96,2304]{1,0:T(8,128)S(1)} %reshape.93) | copy-start | bytes 2654212
  79.1 3.1 %copy-start.13 = (f32[96,768]{1,0:T(8,128)S(1)}, f32[96,768]{1,0:T(8,128)}, u32[]{:S(2)}) copy-start(f32[96,768]{1,0:T(8,128)} %param.34) | copy-start | bytes 884740
  82.2 2.1 copy-start.7
  87.1 4.9 %copy-start = (f32[384,768]{1,0:T(8,128)}, f32[384,768]{1,0:T(8,128)S(1)}, u32[]{:S(2)}) copy-start(f32[384,768]{1,0:T(8,128)S(1)} %reshape.96) | copy-start | bytes 3538948
  87.1 3.4 %copy-start.9 = (bf16[1,1152,128]{2,1,0:T(8,128)(2,1)S(1)}, bf16[1,1152,128]{2,1,0:T(8,128)(2,1)}, u32[]{:S(2)}) copy-start(bf16[1,1152,128]{2,1,0:T(8,128)(2,1)} %reshape.90) | copy-start | bytes 884740
  91.9 38.1 %all-to-all-start.1 = ((bf16[8,1152,128]{2,1,0:T(8,128)(2,1)}), bf16[8,1152,128]{2,1,0:T(8,128)(2,1)S(1)}, u32[]{:S(2)}, u32[]{:S(2)}) async-start(bf16[8,1152,128]{2,1,0:T(8,128)(2,1)} %constant_dynamic-update-slice_fusion.8), calls=%async_computation.1 | async-start | bytes 4718592 | tf_op jit(solution)/shard_map/all_to_all | solution.py:122
  98.3 156.5 %reduce-scatter.2.cloned.1.call-start = ((), (), s32[]{:S(2)}) async-start(), calls=%async_computation.5 | async-start | bytes 6684672 | tf_op jit(solution)/shard_map/reduce_scatter | solution.py:183
  138.8 1.3 collective-permute-start
  146.2 1.0 copy-start.24
  147.3 3.3 %collective-permute-start.1 = (bf16[768,768]{1,0:T(8,128)(2,1)S(1)}, bf16[768,768]{1,0:T(8,128)(2,1)}, u32[]{:S(2)}, u32[]{:S(2)}) collective-permute-start(bf16[768,768]{1,0:T(8,128)(2,1)S(1)} %fusion.32), channel_id=1, source_target_pairs={{0,8},{8,0},{16,24},{24,16},{32,40},{40,32},{48,56},{56,48},{64,72... | collective-permute-start | bytes 3538952 | tf_op jit(solution)/shard_map/ppermute | solution.py:100
  163.1 3.1 %collective-permute-start.2 = (bf16[768,768]{1,0:T(8,128)(2,1)S(1)}, bf16[768,768]{1,0:T(8,128)(2,1)S(1)}, u32[]{:S(2)}, u32[]{:S(2)}) collective-permute-start(bf16[768,768]{1,0:T(8,128)(2,1)S(1)} %fusion.33), channel_id=1, source_target_pairs={{0,8},{8,0},{16,24},{24,16},{32,40},{40,32},{48,56},{56,48},{64,72... | collective-permute-start | bytes 3538952 | tf_op jit(solution)/shard_map/ppermute | solution.py:100
  173.2 4.9 %copy-start.26 = (f32[5]{0:T(128)S(1)}, f32[5]{0:T(128)}, u32[]{:S(2)}) copy-start(f32[5]{0:T(128)} %constant.124.clone) | copy-start | bytes 64
  177.7 3.2 %copy-start.23 = (bf16[768,768]{1,0:T(8,128)(2,1)}, bf16[768,768]{1,0:T(8,128)(2,1)S(1)}, u32[]{:S(2)}) copy-start(bf16[768,768]{1,0:T(8,128)(2,1)S(1)} %fusion.34) | copy-start | bytes 3538948
  177.7 3.2 %collective-permute-start.3 = (bf16[768,768]{1,0:T(8,128)(2,1)S(1)}, bf16[768,768]{1,0:T(8,128)(2,1)S(1)}, u32[]{:S(2)}, u32[]{:S(2)}) collective-permute-start(bf16[768,768]{1,0:T(8,128)(2,1)S(1)} %fusion.34), channel_id=1, source_target_pairs={{0,8},{8,0},{16,24},{24,16},{32,40},{40,32},{48,56},{56,48},{64,72... | collective-permute-start | bytes 3538952 | tf_op jit(solution)/shard_map/ppermute | solution.py:100
  180.9 1.0 copy-start.25
  197.3 9.1 %copy-start.1 = (f32[384,768]{1,0:T(8,128)S(1)}, f32[384,768]{1,0:T(8,128)}, u32[]{:S(2)}) copy-start(f32[384,768]{1,0:T(8,128)} %copy-done) | copy-start | bytes 3538948
  197.3 40.8 %all-to-all-start.2 = ((bf16[8,1152,128]{2,1,0:T(8,128)(2,1)}), bf16[8,1152,128]{2,1,0:T(8,128)(2,1)}, u32[]{:S(2)}, u32[]{:S(2)}) async-start(bf16[8,1152,128]{2,1,0:T(8,128)(2,1)} %get-tuple-element.77), calls=%async_computation.2 | async-start | bytes 4718592 | tf_op jit(solution)/shard_map/all_to_all | solution.py:166
  206.4 2.7 %copy-start.3 = (f32[96,2304]{1,0:T(8,128)S(1)}, f32[96,2304]{1,0:T(8,128)}, u32[]{:S(2)}) copy-start(f32[96,2304]{1,0:T(8,128)} %copy-done.2) | copy-start | bytes 2654212
  206.4 2.6 copy-start.6
  206.4 3.6 %copy-start.4 = (f32[96,3072]{1,0:T(8,128)S(1)}, f32[96,3072]{1,0:T(8,128)}, u32[]{:S(2)}) copy-start(f32[96,3072]{1,0:T(8,128)} %param.35) | copy-start | bytes 3538948
  211.3 28.4 %copy-start.8 = (f32[96,768]{1,0:T(8,128)S(1)}, f32[96,768]{1,0:T(8,128)}, u32[]{:S(2)}) copy-start(f32[96,768]{1,0:T(8,128)} %copy-done.7) | copy-start | bytes 884740
  211.3 28.4 %copy-start.14 = (f32[96,768]{1,0:T(8,128)S(1)}, f32[96,768]{1,0:T(8,128)}, u32[]{:S(2)}) copy-start(f32[96,768]{1,0:T(8,128)} %param.34) | copy-start | bytes 884740
  238.1 2.3 copy-start.19
  238.1 2.3 copy-start.20
  238.1 2.4 copy-start.21
  239.6 7.4 %collective-permute-start.4 = (bf16[4,1152,128]{2,1,0:T(8,128)(2,1)S(1)}, bf16[4,1152,128]{2,1,0:T(8,128)(2,1)S(1)}, u32[]{:S(2)}, u32[]{:S(2)}) collective-permute-start(bf16[4,1152,128]{2,1,0:T(8,128)(2,1)S(1)} %pad_maximum_fusion), channel_id=1, source_target_pairs={{0,8},{8,0},{16,24},{24,16},{32,40},{40,32},{48,56},{56,48},{64,72... | collective-permute-start | bytes 3538952 | tf_op jit(solution)/shard_map/ppermute | solution.py:100
  246.0 0.8 copy-start.17
  246.9 0.8 copy-start.18
  247.0 0.9 copy-start.16
  247.8 1.0 copy-start.15
  248.9 6.0 %copy-start.10 = (f32[1,256,768]{2,1,0:T(8,128)S(1)}, f32[1,256,768]{2,1,0:T(8,128)}, u32[]{:S(2)}) copy-start(f32[1,256,768]{2,1,0:T(8,128)} %param.37) | copy-start | bytes 2359300
  248.9 6.0 %copy-start.11 = (f32[1,256,768]{2,1,0:T(8,128)S(1)}, f32[1,256,768]{2,1,0:T(8,128)}, u32[]{:S(2)}) copy-start(f32[1,256,768]{2,1,0:T(8,128)} %param.38) | copy-start | bytes 2359300
  248.9 5.9 %copy-start.12 = (f32[1,256,768]{2,1,0:T(8,128)S(1)}, f32[1,256,768]{2,1,0:T(8,128)}, u32[]{:S(2)}) copy-start(f32[1,256,768]{2,1,0:T(8,128)} %param.39) | copy-start | bytes 2359300
Sparse Core Ops, SparseCore 0:
  45.3 32.5 all-gather.1
  138.9 75.9 reduce-scatter.1

commit v9 on v6

--- a/solution.py
+++ b/solution.py
@@ -80,7 +80,8 @@
     flat = jnp.pad(flat, (0, padded - flat.shape[0])).reshape(padded // lanes, lanes)
     parts = lax.all_to_all(flat.reshape(replicas, -1, lanes), "dp", 0, 0, tiled=True)
     reduced = jnp.sum(parts.astype(jnp.float32), axis=0).astype(jnp.bfloat16)
-    gathered = lax.all_gather(reduced, "dp", axis=0, tiled=True).reshape(-1)
+    copies = jnp.broadcast_to(reduced[None], (replicas,) + reduced.shape)
+    gathered = lax.all_to_all(copies, "dp", 0, 0, tiled=True).reshape(-1)
     sums = []
     offset = 0
     for g, n in zip(grads, sizes):

time: 265 us -> 264 us (level)
  waiting for transfers between devices: 73.5 us -> 65.6 us
  starting transfers between devices: 7.34 us -> 11 us
    all_gather x1 -> x0, waiting for transfers between devices: 32.7 us -> none  [local(): gathered = lax.all_gather(reduced, 'dp', axis=0, tiled=True).reshape(-1)]
    all_to_all x0 -> x1, waiting for transfers between devices: none -> 25.3 us  [local(): gathered = lax.all_to_all(copies, 'dp', 0, 0, tiled=True).reshape(-1)]
    all_to_all x0 -> x1, starting transfers between devices: none -> 3.71 us  [local(): gathered = lax.all_to_all(copies, 'dp', 0, 0, tiled=True).reshape(-1)]
where the time goes in v9:
time: 264 us; the launch traced here: 262 us
  blocking collectives  76.4 us (29%)
  waiting for transfers between devices  65.6 us (25%)
  local copies, waits for them, and re-layouts  41 us (16%)
  matrix products  32 us (12%)
  other arithmetic  19.9 us (8%)
  between operations  15.8 us (6%)
  starting transfers between devices  11 us (4%)
    all_to_all x1, blocking collectives, local(): returned = lax.all_to_all(answered, 'shard', 0, 0, tiled=True)  45.3 us
    all_to_all x1, blocking collectives, local(): lax.all_to_all(flat.reshape(replicas, -1, lanes), 'dp', 0, 0, tiled=True)  31.1 us
    all_to_all x1, waiting for transfers between devices, local(): incoming = lax.all_to_all(outgoing, 'shard', 0, 0, tiled=True)  30.9 us
    all_to_all x1, waiting for transfers between devices, local(): gathered = lax.all_to_all(copies, 'dp', 0, 0, tiled=True).reshape(-1)  25.3 us
    dot_general x3, matrix products, newton_schulz(): jnp.dot(poly, current, preferred_element_type=jnp.float32)  21 us
    dot_general x3, matrix products, newton_schulz(): part = jnp.dot(current, current.T, preferred_element_type=jnp.bfloat16)  11 us
    ppermute x5, waiting for transfers between devices, exchange(): return lax.ppermute(value, 'dp', partner)  9.37 us
    unnamed x45, local copies, waits for them, and re-layouts  6.83 us
  transfers between devices with their start and end apart: 8, of which 6 were waited for; matrix products, arithmetic and copies ran while one was open for 21% of the time, Pallas kernels for 0%

profile of v9, /device:TPU:0, one launch (start us, length us, event | category | flops | bytes accessed | tf_op | source)
XLA Modules:
  0.0 261.7 jit_solution(3156716622949319844)
XLA Ops:
  7.2 1.5 reshape_squeeze.30
  8.8 1.1 reshape_squeeze.31
  9.8 1.2 copy.36
  11.0 1.6 reshape_squeeze.33
  13.0 31.1 %all_to_all.32 = bf16[16,448,128]{2,1,0:T(8,128)(2,1)S(1)} all-to-all(bf16[16,448,128]{2,1,0:T(8,128)(2,1)S(1)} %bitcast.19), channel_id=1, replica_groups=mesh['dp'=16,'shard'=8] {'dp'}, dimensions={0} | all-to-all | bytes 3670016 | tf_op jit(solution)/shard_map/all_to_all | solution.py:81
  44.4 1.6 broadcast_in_dim.18
  46.0 3.7 %all-to-all-start.1 = ((bf16[16,448,128]{2,1,0:T(8,128)(2,1)}), bf16[16,448,128]{2,1,0:T(8,128)(2,1)S(1)}, u32[]{:S(2)}, u32[]{:S(2)}) async-start(bf16[16,448,128]{2,1,0:T(8,128)(2,1)} %broadcast_in_dim.18), calls=%async_computation.1 | async-start | bytes 3670016 | tf_op jit(solution)/shard_map/all_to_all | solution.py:84
  49.8 25.3 %all-to-all-done.1 = bf16[16,448,128]{2,1,0:T(8,128)(2,1)S(1)} async-done(((bf16[16,448,128]{2,1,0:T(8,128)(2,1)}), bf16[16,448,128]{2,1,0:T(8,128)(2,1)S(1)}, u32[]{:S(2)}, u32[]{:S(2)}) %all-to-all-start.1) | async-done | bytes 1835040 | tf_op jit(solution)/shard_map/all_to_all | solution.py:84
  75.1 1.3 slice_convert_fusion
  76.4 0.7 slice_convert_fusion.3
  77.1 1.0 slice_convert_fusion.2
  78.1 1.5 reshape.89
  79.6 1.4 multiply_add_fusion
  81.0 1.0 copy-done.2
  82.6 1.5 multiply_add_fusion.1
  84.1 1.0 copy-done.3
  85.2 0.4 reshape.83
  85.7 0.7 copy-done.9
  86.6 1.3 multiply_add_fusion.2
  87.9 0.9 copy-done.4
  89.1 1.7 dynamic_update_slice.42
  90.8 0.6 constant_dynamic-update-slice_fusion.10
  91.5 0.7 constant_dynamic-update-slice_fusion.9
  92.2 0.8 constant_dynamic-update-slice_fusion.8
  93.0 6.6 %all-to-all-start.2 = ((bf16[8,1152,128]{2,1,0:T(8,128)(2,1)}), bf16[8,1152,128]{2,1,0:T(8,128)(2,1)S(1)}, u32[]{:S(2)}, u32[]{:S(2)}) async-start(bf16[8,1152,128]{2,1,0:T(8,128)(2,1)} %constant_dynamic-update-slice_fusion.8), calls=%async_computation.2 | async-start | bytes 4718592 | tf_op jit(solution)/shard_map/all_to_all | solution.py:125
  99.7 30.9 %all-to-all-done.2 = bf16[8,1152,128]{2,1,0:T(8,128)(2,1)S(1)} async-done(((bf16[8,1152,128]{2,1,0:T(8,128)(2,1)}), bf16[8,1152,128]{2,1,0:T(8,128)(2,1)S(1)}, u32[]{:S(2)}, u32[]{:S(2)}) %all-to-all-start.2) | async-done | bytes 2359328 | tf_op jit(solution)/shard_map/all_to_all | solution.py:125
  130.6 8.8 %conditional.2 = (f32[768,1536]{1,0:T(8,128)}, f32[]{:T(128)}) conditional(s32[]{:T(128)} %clamp.4, bf16[8,1152,128]{2,1,0:T(8,128)(2,1)S(1)} %all-to-all-done.2, bf16[8,1152,128]{2,1,0:T(8,128)(2,1)S(1)} %all-to-all-done.2, bf16[8,1152,128]{2,1,0:T(8,128)(2,1)S(1)} %all-to-all-done.2, ...), branch_computations={%region_1.3_spmd, %region_3.5_spmd, %region_5.7_spmd, %region_7.9_... | conditional | flops 3538943 | bytes 21233684 | solution.py:143
  130.6 1.4 slice.40
  132.0 3.6 %reshape.69 = bf16[768,1152]{1,0:T(8,128)(2,1)S(1)} reshape(bf16[8,864,128]{2,1,0:T(8,128)(2,1)} %slice.40) | data formatting | bytes 3538944 | tf_op jit(solution)/shard_map/cond/branch_0_fun/reshape | solution.py:132
  135.6 3.8 %multiply_reduce_fusion = (f32[]{:T(128)}, f32[768,1536]{1,0:T(8,128)}) fusion(bf16[768,1152]{1,0:T(8,128)(2,1)S(1)} %reshape.69), kind=kLoop, calls=%fused_computation | loop fusion | flops 3538943 | bytes 6488068 | tf_op jit(solution)/shard_map/reduce_sum | solution.py:23
  139.4 1.4 collective-permute-done
  142.1 2.9 %divide_convert_fusion = bf16[768,1536]{1,0:T(8,128)(2,1)S(1)} fusion(f32[768,1536]{1,0:T(8,128)} %get-tuple-element.34, f32[]{:T(128)S(6)} %add.149), kind=kLoop, calls=%fused_computation.9 | loop fusion | flops 2359296 | bytes 7077892 | tf_op jit(solution)/shard_map/convert_element_type | solution.py:25
  145.0 2.0 fusion.20
  147.2 2.8 %collective-permute-done.1 = bf16[768,768]{1,0:T(8,128)(2,1)} collective-permute-done((bf16[768,768]{1,0:T(8,128)(2,1)S(1)}, bf16[768,768]{1,0:T(8,128)(2,1)}, u32[]{:S(2)}, u32[]{:S(2)}) %collective-permute-start.1) | collective-permute-done | bytes 1179680 | tf_op jit(solution)/shard_map/ppermute | solution.py:103
  150.1 6.8 %add_convert_fusion.1 = bf16[768,1536]{1,0:T(8,128)(2,1)} fusion(bf16[768,1536]{1,0:T(8,128)(2,1)S(1)} %divide_convert_fusion, bf16[768,768]{1,0:T(8,128)(2,1)} %collective-permute-done.1, bf16[768,768]{1,0:T(8,128)(2,1)S(1)} %fusion.20), kind=kOutput, calls=%fused_computation.8 | convolution fusion | flops 2730295296 | bytes 7077888 | tf_op jit(solution)/shard_map/dot_general | solution.py:32
  156.9 4.5 %fusion.21 = bf16[768,768]{1,0:T(8,128)(2,1)S(1)} fusion(bf16[768,1536]{1,0:T(8,128)(2,1)} %add_convert_fusion.1), kind=kOutput, calls=%fused_computation.72 | convolution fusion | flops 1811939328 | bytes 3538944 | tf_op jit(solution)/shard_map/dot_general | solution.py:28
  161.5 2.8 %collective-permute-done.2 = bf16[768,768]{1,0:T(8,128)(2,1)S(1)} collective-permute-done((bf16[768,768]{1,0:T(8,128)(2,1)S(1)}, bf16[768,768]{1,0:T(8,128)(2,1)S(1)}, u32[]{:S(2)}, u32[]{:S(2)}) %collective-permute-start.2) | collective-permute-done | bytes 1179680 | tf_op jit(solution)/shard_map/ppermute | solution.py:103
  164.4 6.9 %add_convert_fusion = bf16[768,1536]{1,0:T(8,128)(2,1)} fusion(bf16[768,1536]{1,0:T(8,128)(2,1)} %add_convert_fusion.1, bf16[768,768]{1,0:T(8,128)(2,1)S(1)} %collective-permute-done.2, bf16[768,768]{1,0:T(8,128)(2,1)S(1)} %fusion.21), kind=kOutput, calls=%fused_computation.7 | convolution fusion | flops 2730295296 | bytes 7077888 | tf_op jit(solution)/shard_map/dot_general | solution.py:32
  171.2 4.4 %fusion.22 = bf16[768,768]{1,0:T(8,128)(2,1)S(1)} fusion(bf16[768,1536]{1,0:T(8,128)(2,1)} %add_convert_fusion), kind=kOutput, calls=%fused_computation.73 | convolution fusion | flops 1811939328 | bytes 3538944 | tf_op jit(solution)/shard_map/dot_general | solution.py:28
  175.9 0.6 dynamic_slice.15
  176.4 2.3 collective-permute-done.3
  178.8 1.0 copy-done.18
  179.8 7.4 %multiply_convert_fusion = bf16[768,1536]{1,0:T(8,128)(2,1)S(1)} fusion(bf16[768,1536]{1,0:T(8,128)(2,1)} %add_convert_fusion, f32[]{:T(128)} %bitcast.4, bf16[768,768]{1,0:T(8,128)(2,1)} %copy-done.18, bf16[768,768]{1,0:T(8,128)(2,1)S(1)} %fusion.22), kind=kOutput, calls=%fused_computation.6 | convolution fusion | flops 2731474944 | bytes 7077892 | tf_op jit(solution)/shard_map/dot_general | solution.py:32
  187.2 6.5 %conditional.3 = (bf16[8,1152,128]{2,1,0:T(8,128)(2,1)}) conditional(s32[]{:T(128)} %clamp.4, bf16[768,1536]{1,0:T(8,128)(2,1)S(1)} %multiply_convert_fusion, bf16[768,1536]{1,0:T(8,128)(2,1)S(1)} %multiply_convert_fusion, bf16[768,1536]{1,0:T(8,128)(2,1)S(1)} %multiply_convert_fusion, ...), branch_computations={%region_10.11_spmd, %region_11.12_spmd, %region_12.13_spmd, %regio... | conditional | bytes 11206666 | solution.py:164
  187.2 1.4 slice.42
  188.6 3.5 %reshape.71 = bf16[8,864,128]{2,1,0:T(8,128)(2,1)S(1)} reshape(bf16[768,1152]{1,0:T(8,128)(2,1)} %slice.42) | data formatting | bytes 3538944 | tf_op jit(solution)/shard_map/cond/branch_0_fun/reshape | solution.py:155
  192.1 1.6 dynamic_update_slice.28
  193.7 45.3 %all_to_all.33 = bf16[8,1152,128]{2,1,0:T(8,128)(2,1)S(1)} all-to-all(bf16[8,1152,128]{2,1,0:T(8,128)(2,1)} %get-tuple-element.69), channel_id=1, replica_groups=mesh['dp'=16,'shard'=8] {'shard'}, dimensions={0} | all-to-all | bytes 4718592 | tf_op jit(solution)/shard_map/all_to_all | solution.py:165
  239.1 1.2 pad_maximum_fusion
  240.3 1.4 multiply_subtract_fusion.1
  242.0 0.3 reshape_squeeze_stack_squeeze.6
  242.4 0.3 reshape_squeeze.34
  242.7 0.7 broadcast_in_dim.20
  243.4 0.6 constant_dynamic-update-slice_fusion.5
  244.3 0.6 copy-done.10
  245.1 1.3 fusion.19
  246.7 0.3 reshape_squeeze.38
  247.0 0.9 slice.85
  248.0 1.0 slice.83
  249.3 0.6 constant_dynamic-update-slice_fusion.4
  249.9 0.7 constant_dynamic-update-slice_fusion
  250.6 0.7 constant_dynamic-update-slice_fusion.2
  251.4 0.7 constant_dynamic-update-slice_fusion.6
  252.1 2.8 %multiply_subtract_fusion = (f32[1,256,768]{2,1,0:T(8,128)}, f32[1,256,768]{2,1,0:T(8,128)}, f32[1,256,768]{2,1,0:T(8,128)}) fusion(f32[1,256,768]{2,1,0:T(8,128)S(1)} %copy-done.6, bf16[1,256,768]{2,1,0:T(8,128)(2,1)} %reduce-scatter.2.cloned.1.call-done, f32[1,256,768]{2,1,0:T(8,128)S(1)} %copy-done.7, f32[1,256,768]{2,1,0:T(8,128)S(1)} %copy-done.8), kind=kLoop, calls=%fused_computation.24 | loop fusion | flops 3145728 | bytes 5111808 | tf_op jit(solution)/shard_map/sub | solution.py:47
  (76 shorter events, 4.0 us)
Async XLA Ops:
  9.8 2.9 %copy-start.17 = (bf16[1,9984]{1,0:T(2,128)(2,1)S(1)}, bf16[1,9984]{1,0:T(2,128)(2,1)}, u32[]{:S(2)}) copy-start(bf16[1,9984]{1,0:T(2,128)(2,1)} %param.31) | copy-start | bytes 59908
  46.0 29.1 %all-to-all-start.1 = ((bf16[16,448,128]{2,1,0:T(8,128)(2,1)}), bf16[16,448,128]{2,1,0:T(8,128)(2,1)S(1)}, u32[]{:S(2)}, u32[]{:S(2)}) async-start(bf16[16,448,128]{2,1,0:T(8,128)(2,1)} %broadcast_in_dim.18), calls=%async_computation.1 | async-start | bytes 3670016 | tf_op jit(solution)/shard_map/all_to_all | solution.py:84
  75.1 3.0 %copy-start = (bf16[16,448,128]{2,1,0:T(8,128)(2,1)}, bf16[16,448,128]{2,1,0:T(8,128)(2,1)S(1)}, u32[]{:S(2)}) copy-start(bf16[16,448,128]{2,1,0:T(8,128)(2,1)S(1)} %all-to-all-done.1) | copy-start | bytes 5505028
  81.0 1.0 copy-start.2
  82.6 3.0 %copy-start.5 = (f32[73728]{0:T(1024)S(1)}, f32[73728]{0:T(1024)}, u32[]{:S(2)}) copy-start(f32[73728]{0:T(1024)} %slice_convert_fusion.3) | copy-start | bytes 884740
  82.6 3.0 %copy-start.13 = (f32[96,768]{1,0:T(8,128)S(1)}, f32[96,768]{1,0:T(8,128)}, u32[]{:S(2)}) copy-start(f32[96,768]{1,0:T(8,128)} %param.34) | copy-start | bytes 884740
  84.1 1.0 copy-start.3
  85.1 1.4 copy-start.1
  85.7 0.7 copy-start.9
  87.9 0.9 copy-start.4
  93.0 37.6 %all-to-all-start.2 = ((bf16[8,1152,128]{2,1,0:T(8,128)(2,1)}), bf16[8,1152,128]{2,1,0:T(8,128)(2,1)S(1)}, u32[]{:S(2)}, u32[]{:S(2)}) async-start(bf16[8,1152,128]{2,1,0:T(8,128)(2,1)} %constant_dynamic-update-slice_fusion.8), calls=%async_computation.2 | async-start | bytes 4718592 | tf_op jit(solution)/shard_map/all_to_all | solution.py:125
  99.6 152.5 %reduce-scatter.2.cloned.1.call-start = ((), (), s32[]{:S(2)}) async-start(), calls=%async_computation.5 | async-start | bytes 6684672 | tf_op jit(solution)/shard_map/reduce_scatter | solution.py:182
  139.4 1.4 collective-permute-start
  147.0 3.1 %collective-permute-start.1 = (bf16[768,768]{1,0:T(8,128)(2,1)S(1)}, bf16[768,768]{1,0:T(8,128)(2,1)}, u32[]{:S(2)}, u32[]{:S(2)}) collective-permute-start(bf16[768,768]{1,0:T(8,128)(2,1)S(1)} %fusion.20), channel_id=1, source_target_pairs={{0,8},{8,0},{16,24},{24,16},{32,40},{40,32},{48,56},{56,48},{64,72... | collective-permute-start | bytes 3538952 | tf_op jit(solution)/shard_map/ppermute | solution.py:103
  161.4 3.0 %collective-permute-start.2 = (bf16[768,768]{1,0:T(8,128)(2,1)S(1)}, bf16[768,768]{1,0:T(8,128)(2,1)S(1)}, u32[]{:S(2)}, u32[]{:S(2)}) collective-permute-start(bf16[768,768]{1,0:T(8,128)(2,1)S(1)} %fusion.21), channel_id=1, source_target_pairs={{0,8},{8,0},{16,24},{24,16},{32,40},{40,32},{48,56},{56,48},{64,72... | collective-permute-start | bytes 3538952 | tf_op jit(solution)/shard_map/ppermute | solution.py:103
  171.2 4.6 %copy-start.19 = (f32[5]{0:T(128)S(1)}, f32[5]{0:T(128)}, u32[]{:S(2)}) copy-start(f32[5]{0:T(128)} %constant.124.clone) | copy-start | bytes 64
  175.7 3.1 %collective-permute-start.3 = (bf16[768,768]{1,0:T(8,128)(2,1)S(1)}, bf16[768,768]{1,0:T(8,128)(2,1)S(1)}, u32[]{:S(2)}, u32[]{:S(2)}) collective-permute-start(bf16[768,768]{1,0:T(8,128)(2,1)S(1)} %fusion.22), channel_id=1, source_target_pairs={{0,8},{8,0},{16,24},{24,16},{32,40},{40,32},{48,56},{56,48},{64,72... | collective-permute-start | bytes 3538952 | tf_op jit(solution)/shard_map/ppermute | solution.py:103
  178.8 1.0 copy-start.18
  239.0 1.3 copy-start.14
  239.0 1.3 copy-start.15
  239.0 1.3 copy-start.16
  240.3 4.8 %collective-permute-start.4 = (bf16[4,1152,128]{2,1,0:T(8,128)(2,1)}, bf16[4,1152,128]{2,1,0:T(8,128)(2,1)}, u32[]{:S(2)}, u32[]{:S(2)}) collective-permute-start(bf16[4,1152,128]{2,1,0:T(8,128)(2,1)} %pad_maximum_fusion), channel_id=1, source_target_pairs={{0,8},{8,0},{16,24},{24,16},{32,40},{40,32},{48,56},{56,48},{64,72... | collective-permute-start | bytes 3538952 | tf_op jit(solution)/shard_map/ppermute | solution.py:103
  244.1 0.8 copy-start.10
  244.2 0.9 copy-start.11
  245.1 1.3 copy-start.12
  246.4 5.7 %copy-start.6 = (f32[1,256,768]{2,1,0:T(8,128)S(1)}, f32[1,256,768]{2,1,0:T(8,128)}, u32[]{:S(2)}) copy-start(f32[1,256,768]{2,1,0:T(8,128)} %param.37) | copy-start | bytes 2359300
  246.4 5.7 %copy-start.7 = (f32[1,256,768]{2,1,0:T(8,128)S(1)}, f32[1,256,768]{2,1,0:T(8,128)}, u32[]{:S(2)}) copy-start(f32[1,256,768]{2,1,0:T(8,128)} %param.38) | copy-start | bytes 2359300
  246.4 5.7 %copy-start.8 = (f32[1,256,768]{2,1,0:T(8,128)S(1)}, f32[1,256,768]{2,1,0:T(8,128)}, u32[]{:S(2)}) copy-start(f32[1,256,768]{2,1,0:T(8,128)} %param.39) | copy-start | bytes 2359300
Sparse Core Ops, SparseCore 0:
  139.6 79.7 reduce-scatter.1
